TPU v7x, 512 devices: a whole 4x8x8 slice. The times are simulated.
512 devices in a mesh: row: 16 (over z_lo, x, core), col: 32 (over z_hi, y).
Axes of the slice: x: 4, y: 8, z: 8 (z_hi: 4, z_lo: 2; z = z_hi * 2 + z_lo), core: 2. Of those that a mesh axis runs over, the one named last changes fastest.
Arguments:
- tiles: bfloat16 [16, 64, 256, 256], P('row', 'col'), may hold values from 0 to 48, as said below
- in_index: int32 [16, 64, 2], P('row', 'col'), may hold values from -1 to 63, as said below
- out_index: int32 [16, 128, 2], P('row', 'col'), may hold values from -1 to 63, as said below
Outputs:
- new_tiles: float32 [16, 128, 256, 256], P('row', 'col')
Inputs may be any that keep to these rules, and one draw needn't show every extreme that they name: `tiles`: entries are positive. `in_index`: the device at grid row r and grid column c holds in its 2 slots distinct tiles with block rows r * 4 to (r + 1) * 4 - 1 and block columns c * 2 to (c + 1) * 2 - 1; used slots come first and unused ones hold -1 in both entries. Every diagonal tile (b, b) is stored, and a device that holds diagonal tiles has every slot used. In one grid row and in one grid column every device has every slot used. `out_index`: same layout as in_index with 4 slots: tiles inside the device's region, used slots first, -1 in unused ones, every diagonal tile (b, b) present, every slot used on devices with diagonal tiles and on one whole grid row and one whole grid column.
All inputs are finite; a program needn't handle non-finite values.
Results may differ from a plain program's by a relative error of at most 0.0003.
Values may be sent and summed in bfloat16 or wider, within the bound.
No kernel may reach another device: no remote copies, remote signals or barrier semaphores. Data moves between devices by JAX's collectives and lax.ppermute only.
A program may use at most 64 MiB of HBM per device.

v0:
```python
import jax
import jax.numpy as jnp
from jax import lax
from jax.experimental import pallas as pl
from jax.experimental.pallas import tpu as pltpu
from jax.sharding import Mesh, PartitionSpec as P

COL_BLOCKS = 2
TILE = 256
PAD = 8
FINE = (("zl", 2), ("x", 4), ("core", 2), ("zh", 4), ("y", 8))
ROW = ("zl", "x", "core")
COL = ("zh", "y")
BUFS = 8


def shift(value, axis, size, by):
    return lax.ppermute(value, axis, [(i, (i + by) % size) for i in range(size)])


def product_kernel(pos_ref, out_ref_index, *refs):
    lefts = refs[:12]
    right, exp_ref, part_ref = refs[12:15]
    todo, lbuf, rbuf, sem = refs[15:]
    counts = [ref.shape[0] for ref in lefts]

    exp_ref[...] = jnp.zeros_like(exp_ref)

    def note(i, n):
        code = pos_ref[i]

        @pl.when(code >= 0)
        def _():
            todo[0, n] = code
            todo[1, n] = i

        return n + (code >= 0).astype(jnp.int32)

    total = lax.fori_loop(0, pos_ref.shape[0], note, jnp.int32(0))

    def start(n):
        slot = n % BUFS
        code = todo[0, n]
        first = 0
        for ref, count in zip(lefts, counts):

            @pl.when((code >= first) & (code < first + count))
            def _(ref=ref, first=first):
                pltpu.make_async_copy(
                    ref.at[code - first, pl.ds(0, TILE)], lbuf.at[slot], sem.at[0, slot]
                ).start()

            first += count
        pltpu.make_async_copy(
            right.at[todo[1, n] % 32, pl.ds(0, TILE)], rbuf.at[slot], sem.at[1, slot]
        ).start()

    def prime(n, carry):
        start(n)
        return carry

    lax.fori_loop(0, jnp.minimum(total, BUFS), prime, 0)

    def multiply(n, carry):
        slot = n % BUFS
        pltpu.make_async_copy(right.at[0, pl.ds(0, TILE)], lbuf.at[slot], sem.at[0, slot]).wait()
        pltpu.make_async_copy(right.at[0, pl.ds(0, TILE)], rbuf.at[slot], sem.at[1, slot]).wait()
        o = todo[1, n] // 32
        exp_ref[o] += jnp.dot(lbuf[slot], rbuf[slot], preferred_element_type=jnp.float32)

        @pl.when(n + BUFS < total)
        def _():
            start(n + BUFS)

        return carry

    lax.fori_loop(0, total, multiply, 0)

    part_ref[...] = jnp.zeros_like(part_ref)
    for o in range(exp_ref.shape[0]):
        value = exp_ref[o]
        squared = value * value
        exp_ref[o] = squared
        column = out_ref_index[o, 1]
        for j in range(COL_BLOCKS):

            @pl.when((column >= 0) & (column % COL_BLOCKS == j))
            def _():
                part_ref[j : j + 1, :] += jnp.sum(squared, axis=0, keepdims=True)


def shards(tiles, in_index, out_index):
    slots = tiles.shape[1]
    out_index = out_index[0]
    out_count = out_index.shape[0]
    marks = jnp.pad(
        in_index[0].astype(tiles.dtype)[:, None, :], ((0, 0), (0, PAD - 1), (0, TILE - 2))
    )
    mine = jnp.concatenate([tiles[0], marks], axis=1)

    pair = jnp.concatenate([mine, shift(mine, "zl", 2, 1)])

    own = lax.all_gather(mine, "y", axis=0, tiled=False)
    right = lax.all_gather(pair, ("x", "core"), axis=0, tiled=True)
    up = shift(mine[0], "zh", 4, 1)
    down = shift(mine[1], "zh", 4, -1)
    early = jnp.stack([up, down, shift(up, "zh", 4, 1), shift(down, "zh", 4, -1)])
    ring = [early]
    ahead = back = early
    for _ in range(3):
        ahead, back = shift(ahead, "y", 8, 1), shift(back, "y", 8, -1)
        ring += [ahead, back]
    ring += [shift(ahead[:2], "y", 8, 1), shift(back[2:], "y", 8, -1)]
    late_up = shift(own[:, 1], "zh", 4, 1)
    late_down = shift(own[:, 0], "zh", 4, -1)
    lefts = [own.reshape(-1, TILE + PAD, TILE)] + ring + [late_up, late_down]

    def index_of(stack):
        return stack[:, TILE, :2].astype(jnp.int32)

    left_index = jnp.concatenate([index_of(stack) for stack in lefts])
    right_index = index_of(right)
    matches = (
        (left_index[None, None, :, 0] == out_index[:, None, None, 0])
        & (left_index[None, None, :, 1] == right_index[None, :, None, 0])
        & (right_index[None, :, None, 1] == out_index[:, None, None, 1])
        & (out_index[:, None, None, 0] >= 0)
    )
    places = jnp.arange(left_index.shape[0], dtype=jnp.int32)
    pos = jnp.max(jnp.where(matches, places, -1), axis=2).reshape(-1)

    squared, part = pl.pallas_call(
        product_kernel,
        grid_spec=pltpu.PrefetchScalarGridSpec(
            num_scalar_prefetch=2,
            grid=(),
            in_specs=[pl.BlockSpec(memory_space=pl.ANY)] * 13,
            out_specs=[pl.BlockSpec(memory_space=pltpu.VMEM)] * 2,
            scratch_shapes=[
                pltpu.SMEM((2, out_count * 32), jnp.int32),
                pltpu.VMEM((BUFS, TILE, TILE), jnp.bfloat16),
                pltpu.VMEM((BUFS, TILE, TILE), jnp.bfloat16),
                pltpu.SemaphoreType.DMA((2, BUFS)),
            ],
        ),
        out_shape=[
            jax.ShapeDtypeStruct((out_count, TILE, TILE), jnp.float32),
            jax.ShapeDtypeStruct((COL_BLOCKS, TILE), jnp.float32),
        ],
    )(pos, out_index, *lefts, right)

    totals = jnp.sum(lax.all_gather(part, ROW, axis=0, tiled=False), axis=0)
    out_used = out_index[:, 0] >= 0
    second = (out_index[:, 1] % COL_BLOCKS == 1)[:, None]
    divisor = jnp.where(second, totals[1][None], totals[0][None])
    divisor = jnp.where(out_used[:, None], divisor, 1.0)
    return (TILE * squared / divisor[:, None, :])[None]


def solution(mesh):
    fine = Mesh(mesh.devices.reshape([size for _, size in FINE]), [name for name, _ in FINE])
    spec = P(ROW, COL)
    return jax.shard_map(
        shards, mesh=fine, in_specs=(spec, spec, spec), out_specs=spec, check_vma=False
    )
```

profile of v0, /device:TPU:1, one launch (start us, length us, event | category | flops | bytes accessed | tf_op | source)
XLA Modules:
  0.0 171.1 jit_solution(18011807797508614877)
XLA Ops:
  6.5 0.7 convert_bitcast_fusion
  7.2 1.7 pad_maximum_fusion.2
  8.9 0.0 all-gather.8.cloned.1.call-update
  8.9 0.0 all-gather.6.cloned.1.call-start
  9.0 4.8 %collective-permute-start.14 = (bf16[2,264,256]{2,1,0:T(8,128)(2,1)}, bf16[2,264,256]{2,1,0:T(8,128)(2,1)S(1)}, u32[]{:S(2)}, u32[]{:S(2)}) collective-permute-start(bf16[2,264,256]{2,1,0:T(8,128)(2,1)} %pad_maximum_fusion.2), channel_id=1, source_target_pairs={{0,256},{256,0},{1,257},{257,1},{2,258},{258,2},{3,259},{259,3},{4... | collective-permute-start | bytes 811016 | tf_op jit(solution)/shard_map/ppermute | solution.py:18
  13.8 4.0 %collective-permute-done.14 = bf16[2,264,256]{2,1,0:T(8,128)(2,1)S(1)} collective-permute-done((bf16[2,264,256]{2,1,0:T(8,128)(2,1)}, bf16[2,264,256]{2,1,0:T(8,128)(2,1)S(1)}, u32[]{:S(2)}, u32[]{:S(2)}) %collective-permute-start.14) | collective-permute-done | bytes 270368 | tf_op jit(solution)/shard_map/ppermute | solution.py:18
  17.9 1.8 %pad_maximum_fusion.1 = bf16[4,264,256]{2,1,0:T(8,128)(2,1)} fusion(bf16[2,264,256]{2,1,0:T(8,128)(2,1)S(1)} %collective-permute-done.14, bf16[2,8,256]{2,1,0:T(8,128)(2,1)S(1)} %pad.4, bf16[2,256,256]{2,1,0:T(8,128)(2,1)} %bitcast.61), kind=kLoop, calls=%fused_computation.4 | loop fusion | flops 1622016 | bytes 1081344 | tf_op jit(solution)/shard_map/concatenate | solution.py:101
  19.7 0.0 all-gather.6.cloned.1.call-update
  19.7 8.2 %collective-permute-start = (bf16[264,256]{1,0:T(8,128)(2,1)S(1)}, bf16[264,256]{1,0:T(8,128)(2,1)S(1)}, u32[]{:S(2)}, u32[]{:S(2)}) collective-permute-start(bf16[264,256]{1,0:T(8,128)(2,1)S(1)} %get-tuple-element.11), channel_id=1, source_target_pairs={{0,8},{8,16},{16,24},{24,0},{1,9},{9,17},{17,25},{25,1},{2,10},{10... | collective-permute-start | bytes 405512 | tf_op jit(solution)/shard_map/ppermute | solution.py:18
  27.9 5.8 %collective-permute-start.1 = (bf16[264,256]{1,0:T(8,128)(2,1)S(1)}, bf16[264,256]{1,0:T(8,128)(2,1)S(1)}, u32[]{:S(2)}, u32[]{:S(2)}) collective-permute-start(bf16[264,256]{1,0:T(8,128)(2,1)S(1)} %get-tuple-element.12), channel_id=1, source_target_pairs={{0,24},{8,0},{16,8},{24,16},{1,25},{9,1},{17,9},{25,17},{2,26},{10... | collective-permute-start | bytes 405512 | tf_op jit(solution)/shard_map/ppermute | solution.py:18
  33.7 0.6 collective-permute-done
  34.3 4.3 %collective-permute-start.2 = (bf16[264,256]{1,0:T(8,128)(2,1)S(1)}, bf16[264,256]{1,0:T(8,128)(2,1)S(1)}, u32[]{:S(2)}, u32[]{:S(2)}) collective-permute-start(bf16[264,256]{1,0:T(8,128)(2,1)S(1)} %collective-permute-done), channel_id=1, source_target_pairs={{0,8},{8,16},{16,24},{24,0},{1,9},{9,17},{17,25},{25,1},{2,10},{10... | collective-permute-start | bytes 405512 | tf_op jit(solution)/shard_map/ppermute | solution.py:18
  38.6 0.5 collective-permute-done.1
  39.0 5.0 %collective-permute-start.3 = (bf16[264,256]{1,0:T(8,128)(2,1)S(1)}, bf16[264,256]{1,0:T(8,128)(2,1)S(1)}, u32[]{:S(2)}, u32[]{:S(2)}) collective-permute-start(bf16[264,256]{1,0:T(8,128)(2,1)S(1)} %collective-permute-done.1), channel_id=1, source_target_pairs={{0,24},{8,0},{16,8},{24,16},{1,25},{9,1},{17,9},{25,17},{2,26},{10... | collective-permute-start | bytes 405512 | tf_op jit(solution)/shard_map/ppermute | solution.py:18
  44.0 7.2 %collective-permute-done.3 = bf16[264,256]{1,0:T(8,128)(2,1)S(1)} collective-permute-done((bf16[264,256]{1,0:T(8,128)(2,1)S(1)}, bf16[264,256]{1,0:T(8,128)(2,1)S(1)}, u32[]{:S(2)}, u32[]{:S(2)}) %collective-permute-start.3) | collective-permute-done | bytes 135200 | tf_op jit(solution)/shard_map/ppermute | solution.py:18
  51.2 0.1 pad_maximum_fusion.refs_1_
  51.3 3.1 %collective-permute-start.4 = (bf16[4,264,256]{2,1,0:T(8,128)(2,1)S(1)}, bf16[4,264,256]{2,1,0:T(8,128)(2,1)S(1)}, u32[]{:S(2)}, u32[]{:S(2)}) collective-permute-start(bf16[4,264,256]{2,1,0:T(8,128)(2,1)S(1)} %pad_maximum_fusion.refs_1_), channel_id=1, source_target_pairs={{0,1},{1,2},{2,3},{3,4},{4,5},{5,6},{6,7},{7,0},{8,9},{9,10},{10,1... | collective-permute-start | bytes 1622024 | tf_op jit(solution)/shard_map/ppermute | solution.py:18
  54.4 3.8 %collective-permute-start.5 = (bf16[4,264,256]{2,1,0:T(8,128)(2,1)S(1)}, bf16[4,264,256]{2,1,0:T(8,128)(2,1)S(1)}, u32[]{:S(2)}, u32[]{:S(2)}) collective-permute-start(bf16[4,264,256]{2,1,0:T(8,128)(2,1)S(1)} %pad_maximum_fusion.refs_1_), channel_id=1, source_target_pairs={{0,7},{1,0},{2,1},{3,2},{4,3},{5,4},{6,5},{7,6},{8,15},{9,8},{10,9... | collective-permute-start | bytes 1622024 | tf_op jit(solution)/shard_map/ppermute | solution.py:18
  58.3 10.4 %collective-permute-done.4.refs_2_ = bf16[4,264,256]{2,1,0:T(8,128)(2,1)S(1)} collective-permute-done((bf16[4,264,256]{2,1,0:T(8,128)(2,1)S(1)}, bf16[4,264,256]{2,1,0:T(8,128)(2,1)S(1)}, u32[]{:S(2)}, u32[]{:S(2)}) %collective-permute-start.4) | collective-permute-done | bytes 540704 | tf_op jit(solution)/shard_map/ppermute | solution.py:18
  68.7 2.0 %collective-permute-start.6 = (bf16[4,264,256]{2,1,0:T(8,128)(2,1)S(1)}, bf16[4,264,256]{2,1,0:T(8,128)(2,1)}, u32[]{:S(2)}, u32[]{:S(2)}) collective-permute-start(bf16[4,264,256]{2,1,0:T(8,128)(2,1)S(1)} %collective-permute-done.4.refs_2_), channel_id=1, source_target_pairs={{0,1},{1,2},{2,3},{3,4},{4,5},{5,6},{6,7},{7,0},{8,9},{9,10},{10,1... | collective-permute-start | bytes 1622024 | tf_op jit(solution)/shard_map/ppermute | solution.py:18
  70.8 4.4 %collective-permute-start.7 = (bf16[4,264,256]{2,1,0:T(8,128)(2,1)S(1)}, bf16[4,264,256]{2,1,0:T(8,128)(2,1)}, u32[]{:S(2)}, u32[]{:S(2)}) collective-permute-start(bf16[4,264,256]{2,1,0:T(8,128)(2,1)S(1)} %collective-permute-done.5.refs_3_), channel_id=1, source_target_pairs={{0,7},{1,0},{2,1},{3,2},{4,3},{5,4},{6,5},{7,6},{8,15},{9,8},{10,9... | collective-permute-start | bytes 1622024 | tf_op jit(solution)/shard_map/ppermute | solution.py:18
  75.2 0.0 all-gather.8.cloned.1.call-done.refs_0_
  75.2 3.3 %slice_bitcast_fusion = (bf16[8,264,256]{2,1,0:T(8,128)(2,1)}, bf16[8,264,256]{2,1,0:T(8,128)(2,1)}) fusion(bf16[8,2,264,256]{3,2,1,0:T(8,128)(2,1)} %bitcast.59), kind=kLoop, calls=%fused_computation | loop fusion | bytes 4325376 | tf_op jit(solution)/shard_map/squeeze | solution.py:115
  78.5 3.7 %collective-permute-start.12 = (bf16[8,264,256]{2,1,0:T(8,128)(2,1)}, bf16[8,264,256]{2,1,0:T(8,128)(2,1)S(1)}, u32[]{:S(2)}, u32[]{:S(2)}) collective-permute-start(bf16[8,264,256]{2,1,0:T(8,128)(2,1)} %get-tuple-element.10), channel_id=1, source_target_pairs={{0,8},{8,16},{16,24},{24,0},{1,9},{9,17},{17,25},{25,1},{2,10},{10... | collective-permute-start | bytes 3244040 | tf_op jit(solution)/shard_map/ppermute | solution.py:18
  82.2 3.7 %collective-permute-start.13 = (bf16[8,264,256]{2,1,0:T(8,128)(2,1)}, bf16[8,264,256]{2,1,0:T(8,128)(2,1)}, u32[]{:S(2)}, u32[]{:S(2)}) collective-permute-start(bf16[8,264,256]{2,1,0:T(8,128)(2,1)} %get-tuple-element.9), channel_id=1, source_target_pairs={{0,24},{8,0},{16,8},{24,16},{1,25},{9,1},{17,9},{25,17},{2,26},{10... | collective-permute-start | bytes 3244040 | tf_op jit(solution)/shard_map/ppermute | solution.py:18
  85.9 1.9 %collective-permute-start.8 = (bf16[4,264,256]{2,1,0:T(8,128)(2,1)}, bf16[4,264,256]{2,1,0:T(8,128)(2,1)S(1)}, u32[]{:S(2)}, u32[]{:S(2)}) collective-permute-start(bf16[4,264,256]{2,1,0:T(8,128)(2,1)} %collective-permute-done.6.refs_4_), channel_id=1, source_target_pairs={{0,1},{1,2},{2,3},{3,4},{4,5},{5,6},{6,7},{7,0},{8,9},{9,10},{10,1... | collective-permute-start | bytes 1622024 | tf_op jit(solution)/shard_map/ppermute | solution.py:18
  87.9 4.6 %collective-permute-start.9 = (bf16[4,264,256]{2,1,0:T(8,128)(2,1)}, bf16[4,264,256]{2,1,0:T(8,128)(2,1)S(1)}, u32[]{:S(2)}, u32[]{:S(2)}) collective-permute-start(bf16[4,264,256]{2,1,0:T(8,128)(2,1)} %collective-permute-done.7.refs_5_), channel_id=1, source_target_pairs={{0,7},{1,0},{2,1},{3,2},{4,3},{5,4},{6,5},{7,6},{8,15},{9,8},{10,9... | collective-permute-start | bytes 1622024 | tf_op jit(solution)/shard_map/ppermute | solution.py:18
  92.5 8.1 %collective-permute-done.8.refs_6_ = bf16[4,264,256]{2,1,0:T(8,128)(2,1)S(1)} collective-permute-done((bf16[4,264,256]{2,1,0:T(8,128)(2,1)}, bf16[4,264,256]{2,1,0:T(8,128)(2,1)S(1)}, u32[]{:S(2)}, u32[]{:S(2)}) %collective-permute-start.8) | collective-permute-done | bytes 540704 | tf_op jit(solution)/shard_map/ppermute | solution.py:18
  100.5 0.8 slice.126
  101.3 1.9 %collective-permute-start.10 = (bf16[2,264,256]{2,1,0:T(8,128)(2,1)}, bf16[2,264,256]{2,1,0:T(8,128)(2,1)S(1)}, u32[]{:S(2)}, u32[]{:S(2)}) collective-permute-start(bf16[2,264,256]{2,1,0:T(8,128)(2,1)} %slice.126), channel_id=1, source_target_pairs={{0,1},{1,2},{2,3},{3,4},{4,5},{5,6},{6,7},{7,0},{8,9},{9,10},{10,1... | collective-permute-start | bytes 811016 | tf_op jit(solution)/shard_map/ppermute | solution.py:18
  103.2 0.8 slice.128
  104.0 4.6 %collective-permute-start.11 = (bf16[2,264,256]{2,1,0:T(8,128)(2,1)}, bf16[2,264,256]{2,1,0:T(8,128)(2,1)}, u32[]{:S(2)}, u32[]{:S(2)}) collective-permute-start(bf16[2,264,256]{2,1,0:T(8,128)(2,1)} %slice.128), channel_id=1, source_target_pairs={{0,7},{1,0},{2,1},{3,2},{4,3},{5,4},{6,5},{7,6},{8,15},{9,8},{10,9... | collective-permute-start | bytes 811016 | tf_op jit(solution)/shard_map/ppermute | solution.py:18
  108.6 0.7 copy.103.out_ref_index
  109.3 0.1 copy.89
  109.4 0.1 copy.90
  109.5 0.7 slice.121
  110.2 0.1 copy.91
  110.3 0.7 slice.122
  111.0 0.1 copy.92
  111.2 0.7 slice.123
  111.9 0.1 copy.93
  112.0 0.1 copy.94
  112.1 0.1 copy.95
  112.2 0.1 copy.104
  112.3 0.7 slice.129
  113.0 0.1 copy.105
  113.1 0.8 slice.114
  113.9 0.1 copy.88
  114.0 0.1 copy.97
  114.1 9.7 %collective-permute-done.13.refs_11_ = bf16[8,264,256]{2,1,0:T(8,128)(2,1)} collective-permute-done((bf16[8,264,256]{2,1,0:T(8,128)(2,1)}, bf16[8,264,256]{2,1,0:T(8,128)(2,1)}, u32[]{:S(2)}, u32[]{:S(2)}) %collective-permute-start.13) | collective-permute-done | bytes 1081376 | tf_op jit(solution)/shard_map/ppermute | solution.py:18
  123.8 0.7 slice.133
  124.6 0.1 copy.99
  124.7 0.1 concatenate.13
  124.8 0.1 broadcast_compare_fusion.2
  124.9 0.9 slice.134
  125.7 0.1 copy.108
  125.8 0.1 broadcast_compare_fusion
  125.9 0.1 broadcast_compare_fusion.1
  126.0 0.2 select_reduce_fusion
  126.2 0.7 reshape.208.pos_ref
  126.9 6.7 %shard_map.37 = (f32[4,256,256]{2,1,0:T(8,128)}, f32[2,256]{1,0:T(2,128)}) custom-call(s32[128]{0:T(128)} %reshape.208.pos_ref, s32[4,2]{1,0:T(4,128)} %copy.103.out_ref_index, bf16[16,264,256]{2,1,0:T(8,128)(2,1)} %all-gather.8.cloned.1.call-done.refs_0_, bf16[4,264,256]{2,1,0:T(8,128)(2,1)} %copy-done.1, bf16[4,264,256]{2,1,0:T(8,128)(2,1)} %copy-done.5, ...), custom_call_target="tpu_custom_call" | custom-call | tf_op jit(solution)/shard_map/pallas_call | solution.py:132
  133.6 28.3 %all-gather.2 = f32[16,2,256]{2,1,0:T(2,128)S(1)} all-gather(f32[1,2,256]{2,1,0:T(2,128)} %bitcast.73), channel_id=3, replica_groups=mesh['zl'=2,'x'=4,'core'=2,'zh'=4,'y'=8] {'zl','x','core'}, dimensions={0}, use_global_device_ids=true | all-gather | bytes 34816 | tf_op jit(solution)/shard_map/all_gather | solution.py:152
  161.9 0.1 select_select_fusion
  162.0 2.3 %divide_bitcast_fusion = f32[1,4,256,256]{3,2,1,0:T(8,128)} fusion(f32[4,256,256]{2,1,0:T(8,128)} %get-tuple-element.7, f32[4,256]{1,0:T(4,128)S(1)} %select_select_fusion), kind=kLoop, calls=%fused_computation.2 | loop fusion | flops 524288 | bytes 2101248 | tf_op jit(solution)/shard_map/broadcast_in_dim | solution.py:157
  (46 shorter events, 0.2 us)
Async XLA Ops:
  6.5 68.7 %all-gather.8.cloned.1.call-start = ((), (), s32[]{:S(2)}) async-start(), calls=%async_computation.1 | async-start | bytes 2433024 | tf_op jit(solution)/shard_map/all_gather | solution.py:103
  8.9 10.8 %copy-start = (bf16[1,2,256,256]{3,2,1,0:T(8,128)(2,1)S(1)}, bf16[1,2,256,256]{3,2,1,0:T(8,128)(2,1)}, u32[]{:S(2)}) copy-start(bf16[1,2,256,256]{3,2,1,0:T(8,128)(2,1)} %param.3) | copy-start | bytes 786436
  8.9 115.9 %all-gather.6.cloned.1.call-start = ((), (), s32[]{:S(2)}) async-start(), calls=%async_computation | async-start | bytes 4866048 | tf_op jit(solution)/shard_map/all_gather | solution.py:104
  9.0 8.9 %collective-permute-start.14 = (bf16[2,264,256]{2,1,0:T(8,128)(2,1)}, bf16[2,264,256]{2,1,0:T(8,128)(2,1)S(1)}, u32[]{:S(2)}, u32[]{:S(2)}) collective-permute-start(bf16[2,264,256]{2,1,0:T(8,128)(2,1)} %pad_maximum_fusion.2), channel_id=1, source_target_pairs={{0,256},{256,0},{1,257},{257,1},{2,258},{258,2},{3,259},{259,3},{4... | collective-permute-start | bytes 811016 | tf_op jit(solution)/shard_map/ppermute | solution.py:18
  19.7 14.6 %collective-permute-start = (bf16[264,256]{1,0:T(8,128)(2,1)S(1)}, bf16[264,256]{1,0:T(8,128)(2,1)S(1)}, u32[]{:S(2)}, u32[]{:S(2)}) collective-permute-start(bf16[264,256]{1,0:T(8,128)(2,1)S(1)} %get-tuple-element.11), channel_id=1, source_target_pairs={{0,8},{8,16},{16,24},{24,0},{1,9},{9,17},{17,25},{25,1},{2,10},{10... | collective-permute-start | bytes 405512 | tf_op jit(solution)/shard_map/ppermute | solution.py:18
  27.9 11.1 %collective-permute-start.1 = (bf16[264,256]{1,0:T(8,128)(2,1)S(1)}, bf16[264,256]{1,0:T(8,128)(2,1)S(1)}, u32[]{:S(2)}, u32[]{:S(2)}) collective-permute-start(bf16[264,256]{1,0:T(8,128)(2,1)S(1)} %get-tuple-element.12), channel_id=1, source_target_pairs={{0,24},{8,0},{16,8},{24,16},{1,25},{9,1},{17,9},{25,17},{2,26},{10... | collective-permute-start | bytes 405512 | tf_op jit(solution)/shard_map/ppermute | solution.py:18
  34.3 9.7 %collective-permute-start.2 = (bf16[264,256]{1,0:T(8,128)(2,1)S(1)}, bf16[264,256]{1,0:T(8,128)(2,1)S(1)}, u32[]{:S(2)}, u32[]{:S(2)}) collective-permute-start(bf16[264,256]{1,0:T(8,128)(2,1)S(1)} %collective-permute-done), channel_id=1, source_target_pairs={{0,8},{8,16},{16,24},{24,0},{1,9},{9,17},{17,25},{25,1},{2,10},{10... | collective-permute-start | bytes 405512 | tf_op jit(solution)/shard_map/ppermute | solution.py:18
  39.0 12.2 %collective-permute-start.3 = (bf16[264,256]{1,0:T(8,128)(2,1)S(1)}, bf16[264,256]{1,0:T(8,128)(2,1)S(1)}, u32[]{:S(2)}, u32[]{:S(2)}) collective-permute-start(bf16[264,256]{1,0:T(8,128)(2,1)S(1)} %collective-permute-done.1), channel_id=1, source_target_pairs={{0,24},{8,0},{16,8},{24,16},{1,25},{9,1},{17,9},{25,17},{2,26},{10... | collective-permute-start | bytes 405512 | tf_op jit(solution)/shard_map/ppermute | solution.py:18
  51.3 58.0 %copy-start.1 = (bf16[4,264,256]{2,1,0:T(8,128)(2,1)}, bf16[4,264,256]{2,1,0:T(8,128)(2,1)S(1)}, u32[]{:S(2)}) copy-start(bf16[4,264,256]{2,1,0:T(8,128)(2,1)S(1)} %pad_maximum_fusion.refs_1_) | copy-start | bytes 1622020
  51.3 17.3 %collective-permute-start.4 = (bf16[4,264,256]{2,1,0:T(8,128)(2,1)S(1)}, bf16[4,264,256]{2,1,0:T(8,128)(2,1)S(1)}, u32[]{:S(2)}, u32[]{:S(2)}) collective-permute-start(bf16[4,264,256]{2,1,0:T(8,128)(2,1)S(1)} %pad_maximum_fusion.refs_1_), channel_id=1, source_target_pairs={{0,1},{1,2},{2,3},{3,4},{4,5},{5,6},{6,7},{7,0},{8,9},{9,10},{10,1... | collective-permute-start | bytes 1622024 | tf_op jit(solution)/shard_map/ppermute | solution.py:18
  54.4 16.3 %collective-permute-start.5 = (bf16[4,264,256]{2,1,0:T(8,128)(2,1)S(1)}, bf16[4,264,256]{2,1,0:T(8,128)(2,1)S(1)}, u32[]{:S(2)}, u32[]{:S(2)}) collective-permute-start(bf16[4,264,256]{2,1,0:T(8,128)(2,1)S(1)} %pad_maximum_fusion.refs_1_), channel_id=1, source_target_pairs={{0,7},{1,0},{2,1},{3,2},{4,3},{5,4},{6,5},{7,6},{8,15},{9,8},{10,9... | collective-permute-start | bytes 1622024 | tf_op jit(solution)/shard_map/ppermute | solution.py:18
  68.7 40.7 %copy-start.5 = (bf16[4,264,256]{2,1,0:T(8,128)(2,1)}, bf16[4,264,256]{2,1,0:T(8,128)(2,1)S(1)}, u32[]{:S(2)}) copy-start(bf16[4,264,256]{2,1,0:T(8,128)(2,1)S(1)} %collective-permute-done.4.refs_2_) | copy-start | bytes 1622020
  68.7 17.2 %collective-permute-start.6 = (bf16[4,264,256]{2,1,0:T(8,128)(2,1)S(1)}, bf16[4,264,256]{2,1,0:T(8,128)(2,1)}, u32[]{:S(2)}, u32[]{:S(2)}) collective-permute-start(bf16[4,264,256]{2,1,0:T(8,128)(2,1)S(1)} %collective-permute-done.4.refs_2_), channel_id=1, source_target_pairs={{0,1},{1,2},{2,3},{3,4},{4,5},{5,6},{6,7},{7,0},{8,9},{9,10},{10,1... | collective-permute-start | bytes 1622024 | tf_op jit(solution)/shard_map/ppermute | solution.py:18
  70.7 7.8 %copy-start.6 = (bf16[4,264,256]{2,1,0:T(8,128)(2,1)}, bf16[4,264,256]{2,1,0:T(8,128)(2,1)S(1)}, u32[]{:S(2)}) copy-start(bf16[4,264,256]{2,1,0:T(8,128)(2,1)S(1)} %collective-permute-done.5.refs_3_) | copy-start | bytes 1622020
  70.8 17.1 %collective-permute-start.7 = (bf16[4,264,256]{2,1,0:T(8,128)(2,1)S(1)}, bf16[4,264,256]{2,1,0:T(8,128)(2,1)}, u32[]{:S(2)}, u32[]{:S(2)}) collective-permute-start(bf16[4,264,256]{2,1,0:T(8,128)(2,1)S(1)} %collective-permute-done.5.refs_3_), channel_id=1, source_target_pairs={{0,7},{1,0},{2,1},{3,2},{4,3},{5,4},{6,5},{7,6},{8,15},{9,8},{10,9... | collective-permute-start | bytes 1622024 | tf_op jit(solution)/shard_map/ppermute | solution.py:18
  75.2 17.2 %copy-start.8 = (s32[1,4,2]{1,2,0:T(2,128)S(1)}, s32[1,4,2]{1,2,0:T(2,128)}, u32[]{:S(2)}) copy-start(s32[1,4,2]{1,2,0:T(2,128)} %param.5) | copy-start | bytes 100
  78.5 35.5 %collective-permute-start.12 = (bf16[8,264,256]{2,1,0:T(8,128)(2,1)}, bf16[8,264,256]{2,1,0:T(8,128)(2,1)S(1)}, u32[]{:S(2)}, u32[]{:S(2)}) collective-permute-start(bf16[8,264,256]{2,1,0:T(8,128)(2,1)} %get-tuple-element.10), channel_id=1, source_target_pairs={{0,8},{8,16},{16,24},{24,0},{1,9},{9,17},{17,25},{25,1},{2,10},{10... | collective-permute-start | bytes 3244040 | tf_op jit(solution)/shard_map/ppermute | solution.py:18
  82.2 41.6 %collective-permute-start.13 = (bf16[8,264,256]{2,1,0:T(8,128)(2,1)}, bf16[8,264,256]{2,1,0:T(8,128)(2,1)}, u32[]{:S(2)}, u32[]{:S(2)}) collective-permute-start(bf16[8,264,256]{2,1,0:T(8,128)(2,1)} %get-tuple-element.9), channel_id=1, source_target_pairs={{0,24},{8,0},{16,8},{24,16},{1,25},{9,1},{17,9},{25,17},{2,26},{10... | collective-permute-start | bytes 3244040 | tf_op jit(solution)/shard_map/ppermute | solution.py:18
  85.9 14.6 %collective-permute-start.8 = (bf16[4,264,256]{2,1,0:T(8,128)(2,1)}, bf16[4,264,256]{2,1,0:T(8,128)(2,1)S(1)}, u32[]{:S(2)}, u32[]{:S(2)}) collective-permute-start(bf16[4,264,256]{2,1,0:T(8,128)(2,1)} %collective-permute-done.6.refs_4_), channel_id=1, source_target_pairs={{0,1},{1,2},{2,3},{3,4},{4,5},{5,6},{6,7},{7,0},{8,9},{9,10},{10,1... | collective-permute-start | bytes 1622024 | tf_op jit(solution)/shard_map/ppermute | solution.py:18
  87.9 15.3 %collective-permute-start.9 = (bf16[4,264,256]{2,1,0:T(8,128)(2,1)}, bf16[4,264,256]{2,1,0:T(8,128)(2,1)S(1)}, u32[]{:S(2)}, u32[]{:S(2)}) collective-permute-start(bf16[4,264,256]{2,1,0:T(8,128)(2,1)} %collective-permute-done.7.refs_5_), channel_id=1, source_target_pairs={{0,7},{1,0},{2,1},{3,2},{4,3},{5,4},{6,5},{7,6},{8,15},{9,8},{10,9... | collective-permute-start | bytes 1622024 | tf_op jit(solution)/shard_map/ppermute | solution.py:18
  100.5 26.4 %copy-start.2 = (bf16[4,264,256]{2,1,0:T(8,128)(2,1)}, bf16[4,264,256]{2,1,0:T(8,128)(2,1)S(1)}, u32[]{:S(2)}) copy-start(bf16[4,264,256]{2,1,0:T(8,128)(2,1)S(1)} %collective-permute-done.8.refs_6_) | copy-start | bytes 1622020
  101.3 10.9 %collective-permute-start.10 = (bf16[2,264,256]{2,1,0:T(8,128)(2,1)}, bf16[2,264,256]{2,1,0:T(8,128)(2,1)S(1)}, u32[]{:S(2)}, u32[]{:S(2)}) collective-permute-start(bf16[2,264,256]{2,1,0:T(8,128)(2,1)} %slice.126), channel_id=1, source_target_pairs={{0,1},{1,2},{2,3},{3,4},{4,5},{5,6},{6,7},{7,0},{8,9},{9,10},{10,1... | collective-permute-start | bytes 811016 | tf_op jit(solution)/shard_map/ppermute | solution.py:18
  103.2 23.7 %copy-start.3 = (bf16[4,264,256]{2,1,0:T(8,128)(2,1)}, bf16[4,264,256]{2,1,0:T(8,128)(2,1)S(1)}, u32[]{:S(2)}) copy-start(bf16[4,264,256]{2,1,0:T(8,128)(2,1)S(1)} %collective-permute-done.9.refs_7_) | copy-start | bytes 1622020
  104.0 8.3 %collective-permute-start.11 = (bf16[2,264,256]{2,1,0:T(8,128)(2,1)}, bf16[2,264,256]{2,1,0:T(8,128)(2,1)}, u32[]{:S(2)}, u32[]{:S(2)}) collective-permute-start(bf16[2,264,256]{2,1,0:T(8,128)(2,1)} %slice.128), channel_id=1, source_target_pairs={{0,7},{1,0},{2,1},{3,2},{4,3},{5,4},{6,5},{7,6},{8,15},{9,8},{10,9... | collective-permute-start | bytes 811016 | tf_op jit(solution)/shard_map/ppermute | solution.py:18
  112.2 14.7 %copy-start.7 = (bf16[2,264,256]{2,1,0:T(8,128)(2,1)}, bf16[2,264,256]{2,1,0:T(8,128)(2,1)S(1)}, u32[]{:S(2)}) copy-start(bf16[2,264,256]{2,1,0:T(8,128)(2,1)S(1)} %collective-permute-done.10.refs_8_) | copy-start | bytes 811012
  114.0 12.9 %copy-start.4 = (bf16[8,264,256]{2,1,0:T(8,128)(2,1)}, bf16[8,264,256]{2,1,0:T(8,128)(2,1)S(1)}, u32[]{:S(2)}) copy-start(bf16[8,264,256]{2,1,0:T(8,128)(2,1)S(1)} %collective-permute-done.12.refs_10_) | copy-start | bytes 3244036
Sparse Core Ops, SparseCore 0:
  9.4 45.5 all-gather.7
  57.1 42.0 all-gather.5
where the time goes:
time: 172 us; the launch traced here: 171 us
  starting transfers between devices  61.8 us (36%)
  waiting for transfers between devices  40.6 us (24%)
  blocking collectives  28.3 us (16%)
  between operations  13.7 us (8%)
  local copies, waits for them, and re-layouts  12.9 us (8%)
  other arithmetic  7.13 us (4%)
  Pallas kernels  6.67 us (4%)
    ppermute x15, starting transfers between devices, shift(): lax.ppermute(value, axis, [(i, (i + by) % size) for i in range(size)])  61.8 us
    ppermute x15, waiting for transfers between devices, shift(): lax.ppermute(value, axis, [(i, (i + by) % size) for i in range(size)])  40.5 us
    all_gather x1, blocking collectives, shards(): totals = jnp.sum(lax.all_gather(part, ROW, axis=0, tiled=False), axis=0)  28.3 us
    pallas_call x1, Pallas kernels, shards(): pl.pallas_call(product_kernel, grid_spec=pltpu.PrefetchScalarGridSpec(num...  6.67 us
    slice x23, local copies, waits for them, and re-layouts, index_of(): return stack[:, TILE, :2].astype(jnp.int32)  6.23 us
  transfers between devices with their start and end apart: 17, of which 7 were waited for; matrix products, arithmetic and copies ran while one was open for 8% of the time, Pallas kernels for 0%

commit v1 on v0

--- a/solution.py
+++ b/solution.py
@@ -93,40 +93,54 @@
     slots = tiles.shape[1]
     out_index = out_index[0]
     out_count = out_index.shape[0]
-    marks = jnp.pad(
-        in_index[0].astype(tiles.dtype)[:, None, :], ((0, 0), (0, PAD - 1), (0, TILE - 2))
-    )
-    mine = jnp.concatenate([tiles[0], marks], axis=1)
-
-    pair = jnp.concatenate([mine, shift(mine, "zl", 2, 1)])
+    marks = in_index[0].reshape(1, 1, -1).astype(tiles.dtype)
+    marks = jnp.pad(marks, ((0, 0), (0, PAD - 1), (0, TILE - 2 * slots)))
+    mine = jnp.concatenate([tiles[0], jnp.broadcast_to(marks, (slots, PAD, TILE))], axis=1)
 
     own = lax.all_gather(mine, "y", axis=0, tiled=False)
-    right = lax.all_gather(pair, ("x", "core"), axis=0, tiled=True)
     up = shift(mine[0], "zh", 4, 1)
     down = shift(mine[1], "zh", 4, -1)
     early = jnp.stack([up, down, shift(up, "zh", 4, 1), shift(down, "zh", 4, -1)])
     ring = [early]
-    ahead = back = early
-    for _ in range(3):
+    ahead, back = shift(early, "y", 8, 1), shift(early, "y", 8, -1)
+    ring += [ahead, back]
+
+    other, _ = lax.optimization_barrier((mine, early))
+    other = shift(other, "zl", 2, 1)
+    right = lax.all_gather(jnp.concatenate([mine, other]), ("x", "core"), axis=0, tiled=True)
+
+    first, second, ahead, back = lax.optimization_barrier((own[:, 0], own[:, 1], ahead, back))
+    late_up = shift(second, "zh", 4, 1)
+    late_down = shift(first, "zh", 4, -1)
+    for _ in range(2):
         ahead, back = shift(ahead, "y", 8, 1), shift(back, "y", 8, -1)
         ring += [ahead, back]
     ring += [shift(ahead[:2], "y", 8, 1), shift(back[2:], "y", 8, -1)]
-    late_up = shift(own[:, 1], "zh", 4, 1)
-    late_down = shift(own[:, 0], "zh", 4, -1)
     lefts = [own.reshape(-1, TILE + PAD, TILE)] + ring + [late_up, late_down]
 
-    def index_of(stack):
-        return stack[:, TILE, :2].astype(jnp.int32)
+    def marks_of(stack):
+        return stack[:, TILE, : 2 * slots]
 
-    left_index = jnp.concatenate([index_of(stack) for stack in lefts])
-    right_index = index_of(right)
+    rows = jnp.concatenate([marks_of(stack) for stack in ring]).reshape(8, 4, 2, 2)
+    rows = rows.astype(jnp.int32)
+    turn = (lax.axis_index("y") + jnp.array([0, -1, 1, -2, 2, -3, 3, 4], jnp.int32)) % 8
+    left_index = jnp.concatenate(
+        [
+            marks_of(own[:, 0]).astype(jnp.int32).reshape(-1, 2),
+            jnp.stack([rows[:, t, t % 2] for t in range(4)], axis=1).reshape(-1, 2),
+            rows[:, 0, 1],
+            rows[:, 1, 0],
+        ]
+    )
+    places = jnp.concatenate([jnp.arange(48, dtype=jnp.int32), 48 + turn, 56 + turn])
+    right_rows = marks_of(right).astype(jnp.int32).reshape(16, 2, 2, 2)
+    right_index = jnp.stack([right_rows[:, t, t] for t in range(2)], axis=1).reshape(-1, 2)
     matches = (
         (left_index[None, None, :, 0] == out_index[:, None, None, 0])
         & (left_index[None, None, :, 1] == right_index[None, :, None, 0])
         & (right_index[None, :, None, 1] == out_index[:, None, None, 1])
         & (out_index[:, None, None, 0] >= 0)
     )
-    places = jnp.arange(left_index.shape[0], dtype=jnp.int32)
     pos = jnp.max(jnp.where(matches, places, -1), axis=2).reshape(-1)
 
     squared, part = pl.pallas_call(
@@ -149,7 +163,8 @@
         ],
     )(pos, out_index, *lefts, right)
 
-    totals = jnp.sum(lax.all_gather(part, ROW, axis=0, tiled=False), axis=0)
+    parts = jnp.broadcast_to(part[None], (16,) + part.shape)
+    totals = jnp.sum(lax.all_to_all(parts, ROW, split_axis=0, concat_axis=0), axis=0)
     out_used = out_index[:, 0] >= 0
     second = (out_index[:, 1] % COL_BLOCKS == 1)[:, None]
     divisor = jnp.where(second, totals[1][None], totals[0][None])

time: 172 us -> 192 us (1.12)
  waiting for transfers between devices: 40.6 us -> 76.1 us
  blocking collectives: 28.3 us -> 0 us
  starting transfers between devices: 61.8 us -> 70.3 us
  other arithmetic: 7.13 us -> 11.5 us
  Pallas kernels: 6.67 us -> 3.37 us
  local copies, waits for them, and re-layouts: 12.9 us -> 16 us
    ppermute x15, waiting for transfers between devices: 40.5 us -> 70.3 us  [shift(): lax.ppermute(value, axis, [(i, (i + by) % size) for i in range(size)])]
    all_gather x1 -> x0, blocking collectives: 28.3 us -> none  [shards(): totals = jnp.sum(lax.all_gather(part, ROW, axis=0, tiled=False), axis=0)]
    all_to_all x0 -> x1, starting transfers between devices: none -> 5.94 us  [shards(): lax.all_to_all(parts, ROW, split_axis=0, concat_axis=0)]
    all_to_all x0 -> x1, waiting for transfers between devices: none -> 5.79 us  [shards(): lax.all_to_all(parts, ROW, split_axis=0, concat_axis=0)]
    pallas_call x1, Pallas kernels: 6.67 us -> 3.37 us  [shards(): pl.pallas_call(product_kernel, grid_spec=pltpu.PrefetchScalarGridSpec(num...]
    ppermute x15, starting transfers between devices: 61.8 us -> 64.3 us  [shift(): lax.ppermute(value, axis, [(i, (i + by) % size) for i in range(size)])]
    slice x23 -> x12, local copies, waits for them, and re-layouts: 6.23 us -> 4.16 us  [the longest x10 3.64 us: marks_of(): return stack[:, TILE, :2 * slots]]
    squeeze x1 -> x10, local copies, waits for them, and re-layouts: 3.28 us -> 4.82 us  [the longest x1 2.68 us: shards(): own[:, 1]]
  transfers between devices with their start and end apart: 17 -> 18, of which waited for: 7 -> 12; matrix products, arithmetic and copies ran while one was open for 8% -> 11% of each run, Pallas kernels for 0% -> 0%
where the time goes in v1:
time: 192 us; the launch traced here: 191 us
  waiting for transfers between devices  76.1 us (40%)
  starting transfers between devices  70.3 us (37%)
  local copies, waits for them, and re-layouts  16 us (8%)
  between operations  13.7 us (7%)
  other arithmetic  11.5 us (6%)
  Pallas kernels  3.37 us (2%)
    ppermute x15, waiting for transfers between devices, shift(): lax.ppermute(value, axis, [(i, (i + by) % size) for i in range(size)])  70.3 us
    ppermute x15, starting transfers between devices, shift(): lax.ppermute(value, axis, [(i, (i + by) % size) for i in range(size)])  64.3 us
    all_to_all x1, starting transfers between devices, shards(): lax.all_to_all(parts, ROW, split_axis=0, concat_axis=0)  5.94 us
    all_to_all x1, waiting for transfers between devices, shards(): lax.all_to_all(parts, ROW, split_axis=0, concat_axis=0)  5.79 us
  transfers between devices with their start and end apart: 18, of which 12 were waited for; matrix products, arithmetic and copies ran while one was open for 11% of the time, Pallas kernels for 0%

profile of v1, /device:TPU:1, one launch (start us, length us, event | category | flops | bytes accessed | tf_op | source)
XLA Modules:
  0.0 191.1 jit_solution(12559705112553635731)
XLA Ops:
  6.5 0.7 convert_element_type.36
  7.3 1.7 pad_maximum_fusion.2
  9.1 1.0 fusion.1
  10.1 6.6 %collective-permute-start = (bf16[264,256]{1,0:T(8,128)(2,1)S(1)}, bf16[264,256]{1,0:T(8,128)(2,1)S(1)}, u32[]{:S(2)}, u32[]{:S(2)}) collective-permute-start(bf16[264,256]{1,0:T(8,128)(2,1)S(1)} %get-tuple-element.31), channel_id=1, source_target_pairs={{0,8},{8,16},{16,24},{24,0},{1,9},{9,17},{17,25},{25,1},{2,10},{10... | collective-permute-start | bytes 405512 | tf_op jit(solution)/shard_map/ppermute | solution.py:18
  16.7 6.8 %collective-permute-start.1 = (bf16[264,256]{1,0:T(8,128)(2,1)S(1)}, bf16[264,256]{1,0:T(8,128)(2,1)S(1)}, u32[]{:S(2)}, u32[]{:S(2)}) collective-permute-start(bf16[264,256]{1,0:T(8,128)(2,1)S(1)} %get-tuple-element.32), channel_id=1, source_target_pairs={{0,24},{8,0},{16,8},{24,16},{1,25},{9,1},{17,9},{25,17},{2,26},{10... | collective-permute-start | bytes 405512 | tf_op jit(solution)/shard_map/ppermute | solution.py:18
  23.5 0.8 collective-permute-done
  24.4 3.7 %collective-permute-start.2 = (bf16[264,256]{1,0:T(8,128)(2,1)S(1)}, bf16[264,256]{1,0:T(8,128)(2,1)S(1)}, u32[]{:S(2)}, u32[]{:S(2)}) collective-permute-start(bf16[264,256]{1,0:T(8,128)(2,1)S(1)} %collective-permute-done), channel_id=1, source_target_pairs={{0,8},{8,16},{16,24},{24,0},{1,9},{9,17},{17,25},{25,1},{2,10},{10... | collective-permute-start | bytes 405512 | tf_op jit(solution)/shard_map/ppermute | solution.py:18
  28.1 1.2 collective-permute-done.1
  29.3 5.1 %collective-permute-start.3 = (bf16[264,256]{1,0:T(8,128)(2,1)S(1)}, bf16[264,256]{1,0:T(8,128)(2,1)S(1)}, u32[]{:S(2)}, u32[]{:S(2)}) collective-permute-start(bf16[264,256]{1,0:T(8,128)(2,1)S(1)} %collective-permute-done.1), channel_id=1, source_target_pairs={{0,24},{8,0},{16,8},{24,16},{1,25},{9,1},{17,9},{25,17},{2,26},{10... | collective-permute-start | bytes 405512 | tf_op jit(solution)/shard_map/ppermute | solution.py:18
  34.4 2.7 %collective-permute-done.3 = bf16[264,256]{1,0:T(8,128)(2,1)S(1)} collective-permute-done((bf16[264,256]{1,0:T(8,128)(2,1)S(1)}, bf16[264,256]{1,0:T(8,128)(2,1)S(1)}, u32[]{:S(2)}, u32[]{:S(2)}) %collective-permute-start.3) | collective-permute-done | bytes 135200 | tf_op jit(solution)/shard_map/ppermute | solution.py:18
  37.2 8.1 %collective-permute-start.12 = (bf16[2,264,256]{2,1,0:T(8,128)(2,1)S(1)}, bf16[2,264,256]{2,1,0:T(8,128)(2,1)S(1)}, u32[]{:S(2)}, u32[]{:S(2)}) collective-permute-start(bf16[2,264,256]{2,1,0:T(8,128)(2,1)S(1)} %copy-done.4), channel_id=1, source_target_pairs={{0,256},{256,0},{1,257},{257,1},{2,258},{258,2},{3,259},{259,3},{4... | collective-permute-start | bytes 811016 | tf_op jit(solution)/shard_map/ppermute | solution.py:18
  45.3 5.9 %collective-permute-done.12 = bf16[2,264,256]{2,1,0:T(8,128)(2,1)S(1)} collective-permute-done((bf16[2,264,256]{2,1,0:T(8,128)(2,1)S(1)}, bf16[2,264,256]{2,1,0:T(8,128)(2,1)S(1)}, u32[]{:S(2)}, u32[]{:S(2)}) %collective-permute-start.12) | collective-permute-done | bytes 270368 | tf_op jit(solution)/shard_map/ppermute | solution.py:18
  51.2 0.9 pad_maximum_fusion.1
  52.1 2.9 %collective-permute-start.4 = (bf16[4,264,256]{2,1,0:T(8,128)(2,1)S(1)}, bf16[4,264,256]{2,1,0:T(8,128)(2,1)S(1)}, u32[]{:S(2)}, u32[]{:S(2)}) collective-permute-start(bf16[4,264,256]{2,1,0:T(8,128)(2,1)S(1)} %pad_maximum_fusion.refs_1_), channel_id=1, source_target_pairs={{0,1},{1,2},{2,3},{3,4},{4,5},{5,6},{6,7},{7,0},{8,9},{9,10},{10,1... | collective-permute-start | bytes 1622024 | tf_op jit(solution)/shard_map/ppermute | solution.py:18
  55.0 3.8 %collective-permute-start.5 = (bf16[4,264,256]{2,1,0:T(8,128)(2,1)S(1)}, bf16[4,264,256]{2,1,0:T(8,128)(2,1)S(1)}, u32[]{:S(2)}, u32[]{:S(2)}) collective-permute-start(bf16[4,264,256]{2,1,0:T(8,128)(2,1)S(1)} %pad_maximum_fusion.refs_1_), channel_id=1, source_target_pairs={{0,7},{1,0},{2,1},{3,2},{4,3},{5,4},{6,5},{7,6},{8,15},{9,8},{10,9... | collective-permute-start | bytes 1622024 | tf_op jit(solution)/shard_map/ppermute | solution.py:18
  58.9 2.7 %slice_bitcast_fusion = (bf16[8,264,256]{2,1,0:T(8,128)(2,1)}, bf16[8,264,256]{2,1,0:T(8,128)(2,1)S(1)}) fusion(bf16[8,2,264,256]{3,2,1,0:T(8,128)(2,1)} %bitcast.66), kind=kLoop, calls=%fused_computation | loop fusion | bytes 4325376 | tf_op jit(solution)/shard_map/squeeze | solution.py:112
  61.6 6.1 %collective-permute-done.4.refs_2_ = bf16[4,264,256]{2,1,0:T(8,128)(2,1)S(1)} collective-permute-done((bf16[4,264,256]{2,1,0:T(8,128)(2,1)S(1)}, bf16[4,264,256]{2,1,0:T(8,128)(2,1)S(1)}, u32[]{:S(2)}, u32[]{:S(2)}) %collective-permute-start.4) | collective-permute-done | bytes 540704 | tf_op jit(solution)/shard_map/ppermute | solution.py:18
  67.7 0.6 collective-permute-done.5.refs_3_
  68.2 3.3 %collective-permute-start.6 = (bf16[4,264,256]{2,1,0:T(8,128)(2,1)S(1)}, bf16[4,264,256]{2,1,0:T(8,128)(2,1)}, u32[]{:S(2)}, u32[]{:S(2)}) collective-permute-start(bf16[4,264,256]{2,1,0:T(8,128)(2,1)S(1)} %collective-permute-done.4.refs_2_), channel_id=1, source_target_pairs={{0,1},{1,2},{2,3},{3,4},{4,5},{5,6},{6,7},{7,0},{8,9},{9,10},{10,1... | collective-permute-start | bytes 1622024 | tf_op jit(solution)/shard_map/ppermute | solution.py:18
  71.5 3.9 %collective-permute-start.7 = (bf16[4,264,256]{2,1,0:T(8,128)(2,1)S(1)}, bf16[4,264,256]{2,1,0:T(8,128)(2,1)}, u32[]{:S(2)}, u32[]{:S(2)}) collective-permute-start(bf16[4,264,256]{2,1,0:T(8,128)(2,1)S(1)} %collective-permute-done.5.refs_3_), channel_id=1, source_target_pairs={{0,7},{1,0},{2,1},{3,2},{4,3},{5,4},{6,5},{7,6},{8,15},{9,8},{10,9... | collective-permute-start | bytes 1622024 | tf_op jit(solution)/shard_map/ppermute | solution.py:18
  75.5 7.7 %collective-permute-done.6.refs_4_ = bf16[4,264,256]{2,1,0:T(8,128)(2,1)} collective-permute-done((bf16[4,264,256]{2,1,0:T(8,128)(2,1)S(1)}, bf16[4,264,256]{2,1,0:T(8,128)(2,1)}, u32[]{:S(2)}, u32[]{:S(2)}) %collective-permute-start.6) | collective-permute-done | bytes 540704 | tf_op jit(solution)/shard_map/ppermute | solution.py:18
  83.1 1.9 collective-permute-start.8
  85.0 0.2 collective-permute-done.7.refs_5_
  85.3 4.3 %collective-permute-start.9 = (bf16[4,264,256]{2,1,0:T(8,128)(2,1)}, bf16[4,264,256]{2,1,0:T(8,128)(2,1)S(1)}, u32[]{:S(2)}, u32[]{:S(2)}) collective-permute-start(bf16[4,264,256]{2,1,0:T(8,128)(2,1)} %collective-permute-done.7.refs_5_), channel_id=1, source_target_pairs={{0,7},{1,0},{2,1},{3,2},{4,3},{5,4},{6,5},{7,6},{8,15},{9,8},{10,9... | collective-permute-start | bytes 1622024 | tf_op jit(solution)/shard_map/ppermute | solution.py:18
  89.6 0.5 broadcast_compare_fusion.3
  90.2 0.5 slice_bitcast_fusion.7
  90.7 5.9 %collective-permute-done.8.refs_6_ = bf16[4,264,256]{2,1,0:T(8,128)(2,1)S(1)} collective-permute-done((bf16[4,264,256]{2,1,0:T(8,128)(2,1)}, bf16[4,264,256]{2,1,0:T(8,128)(2,1)S(1)}, u32[]{:S(2)}, u32[]{:S(2)}) %collective-permute-start.8) | collective-permute-done | bytes 540704 | tf_op jit(solution)/shard_map/ppermute | solution.py:18
  96.6 0.8 slice.153
  97.4 1.9 collective-permute-start.10
  99.3 0.8 slice.155
  100.1 4.6 %collective-permute-start.11 = (bf16[2,264,256]{2,1,0:T(8,128)(2,1)}, bf16[2,264,256]{2,1,0:T(8,128)(2,1)}, u32[]{:S(2)}, u32[]{:S(2)}) collective-permute-start(bf16[2,264,256]{2,1,0:T(8,128)(2,1)} %slice.155), channel_id=1, source_target_pairs={{0,7},{1,0},{2,1},{3,2},{4,3},{5,4},{6,5},{7,6},{8,15},{9,8},{10,9... | collective-permute-start | bytes 811016 | tf_op jit(solution)/shard_map/ppermute | solution.py:18
  104.7 0.7 copy.99.out_ref_index
  105.4 0.6 pad_add_fusion.3
  106.0 0.1 copy.101
  106.1 0.1 copy.102
  106.2 0.7 slice.147
  106.9 0.1 copy.103
  107.2 1.9 collective-permute-start.13
  109.1 5.5 %collective-permute-start.14 = (bf16[8,264,256]{2,1,0:T(8,128)(2,1)S(1)}, bf16[8,264,256]{2,1,0:T(8,128)(2,1)}, u32[]{:S(2)}, u32[]{:S(2)}) collective-permute-start(bf16[8,264,256]{2,1,0:T(8,128)(2,1)S(1)} %get-tuple-element.16), channel_id=1, source_target_pairs={{0,24},{8,0},{16,8},{24,16},{1,25},{9,1},{17,9},{25,17},{2,26},{10... | collective-permute-start | bytes 3244040 | tf_op jit(solution)/shard_map/ppermute | solution.py:18
  114.6 0.7 slice.149
  115.3 0.1 copy.104
  115.4 0.7 slice.150
  116.2 0.1 copy.106
  116.3 0.1 copy.107
  116.4 0.7 copy.108
  117.1 0.7 slice.156
  117.8 0.7 copy.109
  118.5 0.8 concatenate.16
  119.3 0.3 slice_reduce_fusion.7
  120.0 0.6 slice_bitcast_fusion.5
  120.5 1.3 broadcast_compare_fusion.2
  121.8 0.9 slice.163
  122.9 0.2 slice_reduce_fusion.1
  123.2 0.6 broadcast_compare_fusion.1
  123.9 0.7 broadcast_compare_fusion
  124.6 0.9 select_reduce_fusion
  125.5 0.7 reshape.203.pos_ref
  126.2 18.5 %collective-permute-done.13.refs_10_ = bf16[8,264,256]{2,1,0:T(8,128)(2,1)S(1)} collective-permute-done((bf16[8,264,256]{2,1,0:T(8,128)(2,1)}, bf16[8,264,256]{2,1,0:T(8,128)(2,1)S(1)}, u32[]{:S(2)}, u32[]{:S(2)}) %collective-permute-start.13) | collective-permute-done | bytes 1081376 | tf_op jit(solution)/shard_map/ppermute | solution.py:18
  144.7 20.7 %collective-permute-done.14.refs_11_ = bf16[8,264,256]{2,1,0:T(8,128)(2,1)} collective-permute-done((bf16[8,264,256]{2,1,0:T(8,128)(2,1)S(1)}, bf16[8,264,256]{2,1,0:T(8,128)(2,1)}, u32[]{:S(2)}, u32[]{:S(2)}) %collective-permute-start.14) | collective-permute-done | bytes 1081376 | tf_op jit(solution)/shard_map/ppermute | solution.py:18
  165.4 3.4 %shard_map.46 = (f32[4,256,256]{2,1,0:T(8,128)}, f32[2,256]{1,0:T(2,128)}) custom-call(s32[128]{0:T(128)} %reshape.203.pos_ref, s32[4,2]{1,0:T(4,128)} %copy.99.out_ref_index, bf16[16,264,256]{2,1,0:T(8,128)(2,1)} %all-gather.6.cloned.1.call-done.refs_0_, bf16[4,264,256]{2,1,0:T(8,128)(2,1)} %copy-done.1, bf16[4,264,256]{2,1,0:T(8,128)(2,1)} %copy-done.6, ...), custom_call_target="tpu_custom_call" | custom-call | tf_op jit(solution)/shard_map/pallas_call | solution.py:146
  168.8 1.3 broadcast_in_dim.79
  170.1 5.9 %all-to-all-start = ((f32[16,2,256]{2,1,0:T(2,128)}), f32[16,2,256]{2,1,0:T(2,128)S(1)}, u32[]{:S(2)}, u32[]{:S(2)}) async-start(f32[16,2,256]{2,1,0:T(2,128)} %broadcast_in_dim.79), calls=%async_computation | async-start | bytes 65536 | tf_op jit(solution)/shard_map/all_to_all | solution.py:167
  176.1 5.8 %all-to-all-done = f32[16,2,256]{2,1,0:T(2,128)S(1)} async-done(((f32[16,2,256]{2,1,0:T(2,128)}), f32[16,2,256]{2,1,0:T(2,128)S(1)}, u32[]{:S(2)}, u32[]{:S(2)}) %all-to-all-start) | async-done | bytes 32800 | tf_op jit(solution)/shard_map/all_to_all | solution.py:167
  182.0 2.3 %divide_bitcast_fusion = f32[1,4,256,256]{3,2,1,0:T(8,128)} fusion(f32[4,256,256]{2,1,0:T(8,128)} %get-tuple-element.17, f32[4,256]{1,0:T(4,128)S(1)} %select_select_fusion), kind=kLoop, calls=%fused_computation.2 | loop fusion | flops 524288 | bytes 2101248 | tf_op jit(solution)/shard_map/broadcast_in_dim | solution.py:172
  (65 shorter events, 1.5 us)
Async XLA Ops:
  6.5 52.3 %all-gather.6.cloned.1.call-start = ((), (), s32[]{:S(2)}) async-start(), calls=%async_computation.2 | async-start | bytes 2433024 | tf_op jit(solution)/shard_map/all_gather | solution.py:100
  9.0 28.2 %copy-start.4 = (bf16[2,264,256]{2,1,0:T(8,128)(2,1)S(1)}, bf16[2,264,256]{2,1,0:T(8,128)(2,1)}, u32[]{:S(2)}) copy-start(bf16[2,264,256]{2,1,0:T(8,128)(2,1)} %pad_maximum_fusion.2) | copy-start | bytes 811012
  9.0 42.2 %copy-start = (bf16[1,2,256,256]{3,2,1,0:T(8,128)(2,1)S(1)}, bf16[1,2,256,256]{3,2,1,0:T(8,128)(2,1)}, u32[]{:S(2)}) copy-start(bf16[1,2,256,256]{3,2,1,0:T(8,128)(2,1)} %param.4) | copy-start | bytes 786436
  9.0 112.8 %all-gather.4.cloned.1.call-start = ((), (), s32[]{:S(2)}) async-start(), calls=%async_computation.1 | async-start | bytes 4866048 | tf_op jit(solution)/shard_map/all_gather | solution.py:110
  10.1 14.3 %collective-permute-start = (bf16[264,256]{1,0:T(8,128)(2,1)S(1)}, bf16[264,256]{1,0:T(8,128)(2,1)S(1)}, u32[]{:S(2)}, u32[]{:S(2)}) collective-permute-start(bf16[264,256]{1,0:T(8,128)(2,1)S(1)} %get-tuple-element.31), channel_id=1, source_target_pairs={{0,8},{8,16},{16,24},{24,0},{1,9},{9,17},{17,25},{25,1},{2,10},{10... | collective-permute-start | bytes 405512 | tf_op jit(solution)/shard_map/ppermute | solution.py:18
  16.7 12.6 %collective-permute-start.1 = (bf16[264,256]{1,0:T(8,128)(2,1)S(1)}, bf16[264,256]{1,0:T(8,128)(2,1)S(1)}, u32[]{:S(2)}, u32[]{:S(2)}) collective-permute-start(bf16[264,256]{1,0:T(8,128)(2,1)S(1)} %get-tuple-element.32), channel_id=1, source_target_pairs={{0,24},{8,0},{16,8},{24,16},{1,25},{9,1},{17,9},{25,17},{2,26},{10... | collective-permute-start | bytes 405512 | tf_op jit(solution)/shard_map/ppermute | solution.py:18
  24.4 10.1 %collective-permute-start.2 = (bf16[264,256]{1,0:T(8,128)(2,1)S(1)}, bf16[264,256]{1,0:T(8,128)(2,1)S(1)}, u32[]{:S(2)}, u32[]{:S(2)}) collective-permute-start(bf16[264,256]{1,0:T(8,128)(2,1)S(1)} %collective-permute-done), channel_id=1, source_target_pairs={{0,8},{8,16},{16,24},{24,0},{1,9},{9,17},{17,25},{25,1},{2,10},{10... | collective-permute-start | bytes 405512 | tf_op jit(solution)/shard_map/ppermute | solution.py:18
  29.3 7.8 %collective-permute-start.3 = (bf16[264,256]{1,0:T(8,128)(2,1)S(1)}, bf16[264,256]{1,0:T(8,128)(2,1)S(1)}, u32[]{:S(2)}, u32[]{:S(2)}) collective-permute-start(bf16[264,256]{1,0:T(8,128)(2,1)S(1)} %collective-permute-done.1), channel_id=1, source_target_pairs={{0,24},{8,0},{16,8},{24,16},{1,25},{9,1},{17,9},{25,17},{2,26},{10... | collective-permute-start | bytes 405512 | tf_op jit(solution)/shard_map/ppermute | solution.py:18
  37.2 68.8 %copy-start.1 = (bf16[4,264,256]{2,1,0:T(8,128)(2,1)}, bf16[4,264,256]{2,1,0:T(8,128)(2,1)S(1)}, u32[]{:S(2)}) copy-start(bf16[4,264,256]{2,1,0:T(8,128)(2,1)S(1)} %pad_maximum_fusion.refs_1_) | copy-start | bytes 1622020
  37.2 14.0 %collective-permute-start.12 = (bf16[2,264,256]{2,1,0:T(8,128)(2,1)S(1)}, bf16[2,264,256]{2,1,0:T(8,128)(2,1)S(1)}, u32[]{:S(2)}, u32[]{:S(2)}) collective-permute-start(bf16[2,264,256]{2,1,0:T(8,128)(2,1)S(1)} %copy-done.4), channel_id=1, source_target_pairs={{0,256},{256,0},{1,257},{257,1},{2,258},{258,2},{3,259},{259,3},{4... | collective-permute-start | bytes 811016 | tf_op jit(solution)/shard_map/ppermute | solution.py:18
  52.1 15.6 %collective-permute-start.4 = (bf16[4,264,256]{2,1,0:T(8,128)(2,1)S(1)}, bf16[4,264,256]{2,1,0:T(8,128)(2,1)S(1)}, u32[]{:S(2)}, u32[]{:S(2)}) collective-permute-start(bf16[4,264,256]{2,1,0:T(8,128)(2,1)S(1)} %pad_maximum_fusion.refs_1_), channel_id=1, source_target_pairs={{0,1},{1,2},{2,3},{3,4},{4,5},{5,6},{6,7},{7,0},{8,9},{9,10},{10,1... | collective-permute-start | bytes 1622024 | tf_op jit(solution)/shard_map/ppermute | solution.py:18
  55.0 13.2 %collective-permute-start.5 = (bf16[4,264,256]{2,1,0:T(8,128)(2,1)S(1)}, bf16[4,264,256]{2,1,0:T(8,128)(2,1)S(1)}, u32[]{:S(2)}, u32[]{:S(2)}) collective-permute-start(bf16[4,264,256]{2,1,0:T(8,128)(2,1)S(1)} %pad_maximum_fusion.refs_1_), channel_id=1, source_target_pairs={{0,7},{1,0},{2,1},{3,2},{4,3},{5,4},{6,5},{7,6},{8,15},{9,8},{10,9... | collective-permute-start | bytes 1622024 | tf_op jit(solution)/shard_map/ppermute | solution.py:18
  58.9 30.8 %copy-start.9 = (s32[1,4,2]{1,2,0:T(2,128)S(1)}, s32[1,4,2]{1,2,0:T(2,128)}, u32[]{:S(2)}) copy-start(s32[1,4,2]{1,2,0:T(2,128)} %param.6) | copy-start | bytes 100
  58.9 31.3 %copy-start.10 = (s32[8]{0:T(128)S(1)}, s32[8]{0:T(128)}, u32[]{:S(2)}) copy-start(s32[8]{0:T(128)} %constant.55.clone) | copy-start | bytes 100
  67.7 39.4 %copy-start.6 = (bf16[4,264,256]{2,1,0:T(8,128)(2,1)}, bf16[4,264,256]{2,1,0:T(8,128)(2,1)S(1)}, u32[]{:S(2)}) copy-start(bf16[4,264,256]{2,1,0:T(8,128)(2,1)S(1)} %collective-permute-done.4.refs_2_) | copy-start | bytes 1622020
  68.2 16.8 %copy-start.7 = (bf16[4,264,256]{2,1,0:T(8,128)(2,1)}, bf16[4,264,256]{2,1,0:T(8,128)(2,1)S(1)}, u32[]{:S(2)}) copy-start(bf16[4,264,256]{2,1,0:T(8,128)(2,1)S(1)} %collective-permute-done.5.refs_3_) | copy-start | bytes 1622020
  68.2 14.9 %collective-permute-start.6 = (bf16[4,264,256]{2,1,0:T(8,128)(2,1)S(1)}, bf16[4,264,256]{2,1,0:T(8,128)(2,1)}, u32[]{:S(2)}, u32[]{:S(2)}) collective-permute-start(bf16[4,264,256]{2,1,0:T(8,128)(2,1)S(1)} %collective-permute-done.4.refs_2_), channel_id=1, source_target_pairs={{0,1},{1,2},{2,3},{3,4},{4,5},{5,6},{6,7},{7,0},{8,9},{9,10},{10,1... | collective-permute-start | bytes 1622024 | tf_op jit(solution)/shard_map/ppermute | solution.py:18
  71.5 13.8 %collective-permute-start.7 = (bf16[4,264,256]{2,1,0:T(8,128)(2,1)S(1)}, bf16[4,264,256]{2,1,0:T(8,128)(2,1)}, u32[]{:S(2)}, u32[]{:S(2)}) collective-permute-start(bf16[4,264,256]{2,1,0:T(8,128)(2,1)S(1)} %collective-permute-done.5.refs_3_), channel_id=1, source_target_pairs={{0,7},{1,0},{2,1},{3,2},{4,3},{5,4},{6,5},{7,6},{8,15},{9,8},{10,9... | collective-permute-start | bytes 1622024 | tf_op jit(solution)/shard_map/ppermute | solution.py:18
  83.1 13.5 %collective-permute-start.8 = (bf16[4,264,256]{2,1,0:T(8,128)(2,1)}, bf16[4,264,256]{2,1,0:T(8,128)(2,1)S(1)}, u32[]{:S(2)}, u32[]{:S(2)}) collective-permute-start(bf16[4,264,256]{2,1,0:T(8,128)(2,1)} %collective-permute-done.6.refs_4_), channel_id=1, source_target_pairs={{0,1},{1,2},{2,3},{3,4},{4,5},{5,6},{6,7},{7,0},{8,9},{9,10},{10,1... | collective-permute-start | bytes 1622024 | tf_op jit(solution)/shard_map/ppermute | solution.py:18
  85.3 14.0 %collective-permute-start.9 = (bf16[4,264,256]{2,1,0:T(8,128)(2,1)}, bf16[4,264,256]{2,1,0:T(8,128)(2,1)S(1)}, u32[]{:S(2)}, u32[]{:S(2)}) collective-permute-start(bf16[4,264,256]{2,1,0:T(8,128)(2,1)} %collective-permute-done.7.refs_5_), channel_id=1, source_target_pairs={{0,7},{1,0},{2,1},{3,2},{4,3},{5,4},{6,5},{7,6},{8,15},{9,8},{10,9... | collective-permute-start | bytes 1622024 | tf_op jit(solution)/shard_map/ppermute | solution.py:18
  96.6 68.8 %copy-start.2 = (bf16[4,264,256]{2,1,0:T(8,128)(2,1)}, bf16[4,264,256]{2,1,0:T(8,128)(2,1)S(1)}, u32[]{:S(2)}) copy-start(bf16[4,264,256]{2,1,0:T(8,128)(2,1)S(1)} %collective-permute-done.8.refs_6_) | copy-start | bytes 1622020
  97.4 19.1 %collective-permute-start.10 = (bf16[2,264,256]{2,1,0:T(8,128)(2,1)}, bf16[2,264,256]{2,1,0:T(8,128)(2,1)S(1)}, u32[]{:S(2)}, u32[]{:S(2)}) collective-permute-start(bf16[2,264,256]{2,1,0:T(8,128)(2,1)} %slice.153), channel_id=1, source_target_pairs={{0,1},{1,2},{2,3},{3,4},{4,5},{5,6},{6,7},{7,0},{8,9},{9,10},{10,1... | collective-permute-start | bytes 811016 | tf_op jit(solution)/shard_map/ppermute | solution.py:18
  99.3 66.1 %copy-start.3 = (bf16[4,264,256]{2,1,0:T(8,128)(2,1)}, bf16[4,264,256]{2,1,0:T(8,128)(2,1)S(1)}, u32[]{:S(2)}) copy-start(bf16[4,264,256]{2,1,0:T(8,128)(2,1)S(1)} %collective-permute-done.9.refs_7_) | copy-start | bytes 1622020
  100.1 17.0 %collective-permute-start.11 = (bf16[2,264,256]{2,1,0:T(8,128)(2,1)}, bf16[2,264,256]{2,1,0:T(8,128)(2,1)}, u32[]{:S(2)}, u32[]{:S(2)}) collective-permute-start(bf16[2,264,256]{2,1,0:T(8,128)(2,1)} %slice.155), channel_id=1, source_target_pairs={{0,7},{1,0},{2,1},{3,2},{4,3},{5,4},{6,5},{7,6},{8,15},{9,8},{10,9... | collective-permute-start | bytes 811016 | tf_op jit(solution)/shard_map/ppermute | solution.py:18
  107.2 37.6 %collective-permute-start.13 = (bf16[8,264,256]{2,1,0:T(8,128)(2,1)}, bf16[8,264,256]{2,1,0:T(8,128)(2,1)S(1)}, u32[]{:S(2)}, u32[]{:S(2)}) collective-permute-start(bf16[8,264,256]{2,1,0:T(8,128)(2,1)} %get-tuple-element.15), channel_id=1, source_target_pairs={{0,8},{8,16},{16,24},{24,0},{1,9},{9,17},{17,25},{25,1},{2,10},{10... | collective-permute-start | bytes 3244040 | tf_op jit(solution)/shard_map/ppermute | solution.py:18
  109.1 56.3 %collective-permute-start.14 = (bf16[8,264,256]{2,1,0:T(8,128)(2,1)S(1)}, bf16[8,264,256]{2,1,0:T(8,128)(2,1)}, u32[]{:S(2)}, u32[]{:S(2)}) collective-permute-start(bf16[8,264,256]{2,1,0:T(8,128)(2,1)S(1)} %get-tuple-element.16), channel_id=1, source_target_pairs={{0,24},{8,0},{16,8},{24,16},{1,25},{9,1},{17,9},{25,17},{2,26},{10... | collective-permute-start | bytes 3244040 | tf_op jit(solution)/shard_map/ppermute | solution.py:18
  116.4 49.0 %copy-start.8 = (bf16[2,264,256]{2,1,0:T(8,128)(2,1)}, bf16[2,264,256]{2,1,0:T(8,128)(2,1)S(1)}, u32[]{:S(2)}) copy-start(bf16[2,264,256]{2,1,0:T(8,128)(2,1)S(1)} %collective-permute-done.10.refs_8_) | copy-start | bytes 811012
  144.7 20.7 %copy-start.5 = (bf16[8,264,256]{2,1,0:T(8,128)(2,1)}, bf16[8,264,256]{2,1,0:T(8,128)(2,1)S(1)}, u32[]{:S(2)}) copy-start(bf16[8,264,256]{2,1,0:T(8,128)(2,1)S(1)} %collective-permute-done.13.refs_10_) | copy-start | bytes 3244036
  170.1 11.7 %all-to-all-start = ((f32[16,2,256]{2,1,0:T(2,128)}), f32[16,2,256]{2,1,0:T(2,128)S(1)}, u32[]{:S(2)}, u32[]{:S(2)}) async-start(f32[16,2,256]{2,1,0:T(2,128)} %broadcast_in_dim.79), calls=%async_computation | async-start | bytes 65536 | tf_op jit(solution)/shard_map/all_to_all | solution.py:167
Sparse Core Ops, SparseCore 0:
  9.4 45.5 all-gather.5
  57.1 41.3 all-gather.3

commit v2 on v0

v2 whole, which is shorter than its diff:
```python
import jax
import jax.numpy as jnp
from jax import lax
from jax.experimental import pallas as pl
from jax.experimental.pallas import tpu as pltpu
from jax.sharding import Mesh, PartitionSpec as P

COL_BLOCKS = 2
TILE = 256
FINE = (("zl", 2), ("x", 4), ("core", 2), ("zh", 4), ("y", 8))
ROW = ("zl", "x", "core")
COL = ("zh", "y")
N_ROW, N_COL, N_ZH, N_Y = 16, 32, 4, 8
RIGHTS = 32
BUFS = 8


def shift(value, axis, size, by):
    return lax.ppermute(value, axis, [(i, (i + by) % size) for i in range(size)])


def to_all(value, axes, size):
    every = jnp.broadcast_to(value[None], (size,) + value.shape)
    return lax.all_to_all(every, axes, split_axis=0, concat_axis=0)


def product_kernel(pos_ref, out_index_ref, *refs):
    lefts = refs[:-7]
    right, exp_ref, part_ref = refs[-7:-4]
    todo, lbuf, rbuf, sem = refs[-4:]

    exp_ref[...] = jnp.zeros_like(exp_ref)

    def note(i, n):
        code = pos_ref[i]

        @pl.when(code >= 0)
        def _():
            todo[0, n] = code
            todo[1, n] = i

        return n + (code >= 0).astype(jnp.int32)

    total = lax.fori_loop(0, pos_ref.shape[0], note, jnp.int32(0))

    def start(n):
        slot = n % BUFS
        code = todo[0, n]
        first = 0
        for ref in lefts:
            count = ref.shape[0]

            @pl.when((code >= first) & (code < first + count))
            def _(ref=ref, first=first):
                pltpu.make_async_copy(ref.at[code - first], lbuf.at[slot], sem.at[0, slot]).start()

            first += count
        pltpu.make_async_copy(
            right.at[todo[1, n] % RIGHTS], rbuf.at[slot], sem.at[1, slot]
        ).start()

    def prime(n, carry):
        start(n)
        return carry

    lax.fori_loop(0, jnp.minimum(total, BUFS), prime, 0)

    def multiply(n, carry):
        slot = n % BUFS
        pltpu.make_async_copy(right.at[0], lbuf.at[slot], sem.at[0, slot]).wait()
        pltpu.make_async_copy(right.at[0], rbuf.at[slot], sem.at[1, slot]).wait()
        o = todo[1, n] // RIGHTS
        exp_ref[o] += jnp.dot(lbuf[slot], rbuf[slot], preferred_element_type=jnp.float32)

        @pl.when(n + BUFS < total)
        def _():
            start(n + BUFS)

        return carry

    lax.fori_loop(0, total, multiply, 0)

    part_ref[...] = jnp.zeros_like(part_ref)
    for o in range(exp_ref.shape[0]):
        value = exp_ref[o]
        squared = value * value
        exp_ref[o] = squared
        column = out_index_ref[o, 1]
        for j in range(COL_BLOCKS):

            @pl.when((column >= 0) & (column % COL_BLOCKS == j))
            def _():
                part_ref[:, j : j + 1, :] += jnp.sum(squared, axis=0, keepdims=True)[None]


def match_table(in_index, out_index):
    row = to_all(in_index.reshape(1, -1), COL, N_COL).reshape(N_ZH, N_Y, -1, 2)
    column = to_all(in_index.reshape(1, -1), ROW, N_ROW).reshape(-1, 2)
    zh, y = lax.axis_index("zh"), lax.axis_index("y")
    hop = (jnp.arange(N_ZH, dtype=jnp.int32)[:, None, None] - zh) % N_ZH
    source = jnp.arange(N_Y, dtype=jnp.int32)[None, :, None]
    slot = jnp.arange(in_index.shape[0], dtype=jnp.int32)[None, None, :]
    away = (source - y) % N_Y
    block = jnp.where(away == 4, 7, jnp.where(away < 4, 2 * away, 2 * (8 - away) - 1))
    place = jnp.where(
        hop == 0,
        2 * source + slot,
        jnp.where(
            hop == 2,
            48 + 2 * block + slot,
            16 + 4 * block + slot + jnp.where(hop == 1, 2, 0),
        ),
    )
    matches = (
        (row[None, None, ..., 0] == out_index[:, 0][:, None, None, None, None])
        & (row[None, None, ..., 1] == column[:, 0][None, :, None, None, None])
        & (column[:, 1][None, :] == out_index[:, 1][:, None])[..., None, None, None]
        & (out_index[:, 0] >= 0)[:, None, None, None, None]
    )
    return jnp.max(jnp.where(matches, place, -1), axis=(2, 3, 4)).reshape(-1)


def shards(tiles, in_index, out_index):
    tiles, in_index, out_index = tiles[0], in_index[0], out_index[0]
    out_count = out_index.shape[0]

    own = lax.all_gather(tiles, "y", axis=0, tiled=True)
    right = lax.all_gather(tiles, ROW, axis=0, tiled=True)
    pos = match_table(in_index, out_index)

    up = shift(tiles, "zh", N_ZH, 1)
    down = shift(tiles, "zh", N_ZH, -1)
    near = [jnp.concatenate([up, down])]
    far = [shift(up, "zh", N_ZH, 1)]

    def step(ring, ahead, back):
        ahead, back = shift(ahead, "y", N_Y, 1), shift(back, "y", N_Y, -1)
        ring += [ahead, back]
        return ahead, back

    near_ends = step(near, near[0], near[0])
    far_ends = step(far, far[0], far[0])
    near_ends, pos = lax.optimization_barrier((near_ends, pos))
    near_ends = step(near, *near_ends)
    far_ends, _ = lax.optimization_barrier((far_ends, near[1:3]))
    far_ends = step(far, *far_ends)
    near_ends, _ = lax.optimization_barrier((near_ends, far[1:3]))
    near_ends = step(near, *near_ends)
    far_ends, _ = lax.optimization_barrier((far_ends, near[3:5]))
    far_ends = step(far, *far_ends)
    near_ends, _ = lax.optimization_barrier((near_ends, far[3:5]))
    near.append(shift(near_ends[1], "y", N_Y, -1))
    far.append(shift(far_ends[0], "y", N_Y, 1))

    lefts = [own] + near + far
    squared, parts = pl.pallas_call(
        product_kernel,
        grid_spec=pltpu.PrefetchScalarGridSpec(
            num_scalar_prefetch=2,
            grid=(),
            in_specs=[pl.BlockSpec(memory_space=pl.ANY)] * (len(lefts) + 1),
            out_specs=[pl.BlockSpec(memory_space=pltpu.VMEM)] * 2,
            scratch_shapes=[
                pltpu.SMEM((2, out_count * RIGHTS), jnp.int32),
                pltpu.VMEM((BUFS, TILE, TILE), jnp.bfloat16),
                pltpu.VMEM((BUFS, TILE, TILE), jnp.bfloat16),
                pltpu.SemaphoreType.DMA((2, BUFS)),
            ],
        ),
        out_shape=[
            jax.ShapeDtypeStruct((out_count, TILE, TILE), jnp.float32),
            jax.ShapeDtypeStruct((N_ROW, COL_BLOCKS, TILE), jnp.float32),
        ],
    )(pos, out_index, *lefts, right)

    totals = jnp.sum(lax.all_to_all(parts, ROW, split_axis=0, concat_axis=0), axis=0)
    out_used = out_index[:, 0] >= 0
    odd = (out_index[:, 1] % COL_BLOCKS == 1)[:, None]
    divisor = jnp.where(odd, totals[1][None], totals[0][None])
    divisor = jnp.where(out_used[:, None], divisor, 1.0)
    return (TILE * squared / divisor[:, None, :])[None]


def solution(mesh):
    fine = Mesh(mesh.devices.reshape([size for _, size in FINE]), [name for name, _ in FINE])
    spec = P(ROW, COL)
    return jax.shard_map(
        shards, mesh=fine, in_specs=(spec, spec, spec), out_specs=spec, check_vma=False
    )
```

time: 172 us -> 172 us (level)
  blocking collectives: 28.3 us -> 0 us
  starting transfers between devices: 61.8 us -> 88.7 us
  waiting for transfers between devices: 40.6 us -> 54.4 us
  local copies, waits for them, and re-layouts: 12.9 us -> 6.62 us
  Pallas kernels: 6.67 us -> 3.38 us
  other arithmetic: 7.13 us -> 4.26 us
    all_gather x1 -> x0, blocking collectives: 28.3 us -> none  [shards(): totals = jnp.sum(lax.all_gather(part, ROW, axis=0, tiled=False), axis=0)]
    all_to_all x0 -> x3, starting transfers between devices: none -> 27.3 us  [the longest x2 17.2 us: to_all(): return lax.all_to_all(every, axes, split_axis=0, concat_axis=0)]
    all_to_all x0 -> x3, waiting for transfers between devices: none -> 21.3 us  [the longest x2 15.6 us: to_all(): return lax.all_to_all(every, axes, split_axis=0, concat_axis=0)]
    ppermute x15 -> x17, waiting for transfers between devices: 40.5 us -> 31.6 us  [shift(): lax.ppermute(value, axis, [(i, (i + by) % size) for i in range(size)])]
    slice x26 -> x2, local copies, waits for them, and re-layouts: 7.78 us -> 0.18 us  [the longest x1 0.18 us: match_table(): column[:, 0][None, :, None, None, None]]
    concatenate x3 -> x0, other arithmetic: 3.47 us -> none  [the longest x1 1.78 us: shards(): pair = jnp.concatenate([mine, shift(mine, 'zl', 2, 1)])]
    pallas_call x1, Pallas kernels: 6.67 us -> 3.38 us  [shards(): pl.pallas_call(product_kernel, grid_spec=pltpu.PrefetchScalarGridSpec(num...]
    squeeze x2 -> x1, local copies, waits for them, and re-layouts: 3.95 us -> 1.36 us  [shards(): tiles, in_index, out_index = (tiles[0], in_index[0], out_index[0])]
  transfers between devices with their start and end apart: 17 -> 22, of which waited for: 7 -> 10; matrix products, arithmetic and copies ran while one was open for 8% -> 4% of each run, Pallas kernels for 0% -> 0%
where the time goes in v2:
time: 172 us; the launch traced here: 171 us
  starting transfers between devices  88.7 us (52%)
  waiting for transfers between devices  54.4 us (32%)
  between operations  13.8 us (8%)
  local copies, waits for them, and re-layouts  6.62 us (4%)
  other arithmetic  4.26 us (2%)
  Pallas kernels  3.38 us (2%)
    ppermute x17, starting transfers between devices, shift(): lax.ppermute(value, axis, [(i, (i + by) % size) for i in range(size)])  61.3 us
    ppermute x17, waiting for transfers between devices, shift(): lax.ppermute(value, axis, [(i, (i + by) % size) for i in range(size)])  31.6 us
    all_to_all x2, starting transfers between devices, to_all(): return lax.all_to_all(every, axes, split_axis=0, concat_axis=0)  17.2 us
    all_to_all x2, waiting for transfers between devices, to_all(): return lax.all_to_all(every, axes, split_axis=0, concat_axis=0)  15.6 us
    all_to_all x1, starting transfers between devices, shards(): lax.all_to_all(parts, ROW, split_axis=0, concat_axis=0)  10.1 us
    all_to_all x1, waiting for transfers between devices, shards(): lax.all_to_all(parts, ROW, split_axis=0, concat_axis=0)  5.69 us
  transfers between devices with their start and end apart: 22, of which 10 were waited for; matrix products, arithmetic and copies ran while one was open for 4% of the time, Pallas kernels for 0%

profile of v2, /device:TPU:1, one launch (start us, length us, event | category | flops | bytes accessed | tf_op | source)
XLA Modules:
  0.0 171.1 jit_solution(5911957513299307039)
XLA Ops:
  6.5 0.7 all-gather.5.cloned.1.call-update
  7.3 0.0 all-gather.7.cloned.1.call-start
  7.3 0.7 all-gather.7.cloned.1.call-update
  8.0 6.6 %collective-permute-start = (bf16[2,256,256]{2,1,0:T(8,128)(2,1)}, bf16[2,256,256]{2,1,0:T(8,128)(2,1)S(1)}, u32[]{:S(2)}, u32[]{:S(2)}) collective-permute-start(bf16[2,256,256]{2,1,0:T(8,128)(2,1)} %bitcast.29), channel_id=1, source_target_pairs={{0,8},{8,16},{16,24},{24,0},{1,9},{9,17},{17,25},{25,1},{2,10},{10... | collective-permute-start | bytes 786440 | tf_op jit(solution)/shard_map/ppermute | solution.py:19
  14.7 6.8 %collective-permute-start.1 = (bf16[2,256,256]{2,1,0:T(8,128)(2,1)}, bf16[2,256,256]{2,1,0:T(8,128)(2,1)S(1)}, u32[]{:S(2)}, u32[]{:S(2)}) collective-permute-start(bf16[2,256,256]{2,1,0:T(8,128)(2,1)} %bitcast.30), channel_id=1, source_target_pairs={{0,24},{8,0},{16,8},{24,16},{1,25},{9,1},{17,9},{25,17},{2,26},{10... | collective-permute-start | bytes 786440 | tf_op jit(solution)/shard_map/ppermute | solution.py:19
  21.4 0.8 broadcast_in_dim.107
  22.2 0.6 broadcast_in_dim.109
  22.8 6.2 %all-to-all-start.1 = ((s32[16,1,4]{2,1,0:T(1,128)}), s32[16,1,4]{2,1,0:T(1,128)S(1)}, u32[]{:S(2)}, u32[]{:S(2)}) async-start(s32[16,1,4]{2,1,0:T(1,128)} %broadcast_in_dim.109), calls=%async_computation.1 | async-start | bytes 16384 | tf_op jit(solution)/shard_map/all_to_all | solution.py:24
  29.1 0.8 slice_bitcast_fusion.3
  29.8 0.1 select_select_fusion.1
  29.9 0.7 broadcast_compare_fusion.5
  30.6 6.1 %all-to-all-done.1 = s32[16,1,4]{2,1,0:T(1,128)S(1)} async-done(((s32[16,1,4]{2,1,0:T(1,128)}), s32[16,1,4]{2,1,0:T(1,128)S(1)}, u32[]{:S(2)}, u32[]{:S(2)}) %all-to-all-start.1) | async-done | bytes 288 | tf_op jit(solution)/shard_map/all_to_all | solution.py:24
  36.7 0.6 broadcast_in_dim.108
  37.3 11.0 %all-to-all-start = ((s32[32,1,4]{2,1,0:T(1,128)}), s32[32,1,4]{2,1,0:T(1,128)S(1)}, u32[]{:S(2)}, u32[]{:S(2)}) async-start(s32[32,1,4]{2,1,0:T(1,128)} %broadcast_in_dim.108), calls=%async_computation | async-start | bytes 32768 | tf_op jit(solution)/shard_map/all_to_all | solution.py:24
  48.3 0.5 broadcast.439
  48.9 0.6 reduce.7
  49.5 0.1 reshape.268
  49.6 0.2 slice_reduce_fusion.1
  49.8 0.1 broadcast_compare_fusion.2
  49.8 9.6 %all-to-all-done = s32[32,1,4]{2,1,0:T(1,128)S(1)} async-done(((s32[32,1,4]{2,1,0:T(1,128)}), s32[32,1,4]{2,1,0:T(1,128)S(1)}, u32[]{:S(2)}, u32[]{:S(2)}) %all-to-all-start) | async-done | bytes 544 | tf_op jit(solution)/shard_map/all_to_all | solution.py:24
  59.4 0.1 copy.16
  59.5 0.1 reshape.267
  59.6 0.0 collective-permute-done
  59.6 0.0 collective-permute-done.1
  59.7 2.3 %collective-permute-start.2 = (bf16[4,256,256]{2,1,0:T(8,128)(2,1)S(1)}, bf16[4,256,256]{2,1,0:T(8,128)(2,1)S(1)}, u32[]{:S(2)}, u32[]{:S(2)}) collective-permute-start(bf16[4,256,256]{2,1,0:T(8,128)(2,1)S(1)} %constant_dynamic-update-slice_fusion.refs_1_), channel_id=1, source_target_pairs={{0,1},{1,2},{2,3},{3,4},{4,5},{5,6},{6,7},{7,0},{8,9},{9,10},{10,1... | collective-permute-start | bytes 1572872 | tf_op jit(solution)/shard_map/ppermute | solution.py:19
  62.0 4.2 %collective-permute-start.3 = (bf16[4,256,256]{2,1,0:T(8,128)(2,1)S(1)}, bf16[4,256,256]{2,1,0:T(8,128)(2,1)S(1)}, u32[]{:S(2)}, u32[]{:S(2)}) collective-permute-start(bf16[4,256,256]{2,1,0:T(8,128)(2,1)S(1)} %constant_dynamic-update-slice_fusion.refs_1_), channel_id=1, source_target_pairs={{0,7},{1,0},{2,1},{3,2},{4,3},{5,4},{6,5},{7,6},{8,15},{9,8},{10,9... | collective-permute-start | bytes 1572872 | tf_op jit(solution)/shard_map/ppermute | solution.py:19
  66.2 0.1 broadcast_compare_fusion.1
  66.3 0.1 broadcast_compare_fusion
  66.3 0.1 select_reduce_fusion
  66.5 0.7 reshape.269.pos_ref
  67.1 2.2 %collective-permute-start.6 = (bf16[2,256,256]{2,1,0:T(8,128)(2,1)S(1)}, bf16[2,256,256]{2,1,0:T(8,128)(2,1)S(1)}, u32[]{:S(2)}, u32[]{:S(2)}) collective-permute-start(bf16[2,256,256]{2,1,0:T(8,128)(2,1)S(1)} %collective-permute-done), channel_id=1, source_target_pairs={{0,8},{8,16},{16,24},{24,0},{1,9},{9,17},{17,25},{25,1},{2,10},{10... | collective-permute-start | bytes 786440 | tf_op jit(solution)/shard_map/ppermute | solution.py:19
  69.3 4.8 %collective-permute-done.2.refs_2_ = bf16[4,256,256]{2,1,0:T(8,128)(2,1)S(1)} collective-permute-done((bf16[4,256,256]{2,1,0:T(8,128)(2,1)S(1)}, bf16[4,256,256]{2,1,0:T(8,128)(2,1)S(1)}, u32[]{:S(2)}, u32[]{:S(2)}) %collective-permute-start.2) | collective-permute-done | bytes 524320 | tf_op jit(solution)/shard_map/ppermute | solution.py:19
  74.1 0.9 collective-permute-done.3.refs_3_
  75.0 2.0 %collective-permute-start.4 = (bf16[4,256,256]{2,1,0:T(8,128)(2,1)S(1)}, bf16[4,256,256]{2,1,0:T(8,128)(2,1)S(1)}, u32[]{:S(2)}, u32[]{:S(2)}) collective-permute-start(bf16[4,256,256]{2,1,0:T(8,128)(2,1)S(1)} %collective-permute-done.2.refs_2_), channel_id=1, source_target_pairs={{0,1},{1,2},{2,3},{3,4},{4,5},{5,6},{6,7},{7,0},{8,9},{9,10},{10,1... | collective-permute-start | bytes 1572872 | tf_op jit(solution)/shard_map/ppermute | solution.py:19
  77.0 5.3 %collective-permute-start.5 = (bf16[4,256,256]{2,1,0:T(8,128)(2,1)S(1)}, bf16[4,256,256]{2,1,0:T(8,128)(2,1)S(1)}, u32[]{:S(2)}, u32[]{:S(2)}) collective-permute-start(bf16[4,256,256]{2,1,0:T(8,128)(2,1)S(1)} %collective-permute-done.3.refs_3_), channel_id=1, source_target_pairs={{0,7},{1,0},{2,1},{3,2},{4,3},{5,4},{6,5},{7,6},{8,15},{9,8},{10,9... | collective-permute-start | bytes 1572872 | tf_op jit(solution)/shard_map/ppermute | solution.py:19
  82.3 2.6 %collective-permute-done.6.refs_9_ = bf16[2,256,256]{2,1,0:T(8,128)(2,1)S(1)} collective-permute-done((bf16[2,256,256]{2,1,0:T(8,128)(2,1)S(1)}, bf16[2,256,256]{2,1,0:T(8,128)(2,1)S(1)}, u32[]{:S(2)}, u32[]{:S(2)}) %collective-permute-start.6) | collective-permute-done | bytes 262176 | tf_op jit(solution)/shard_map/ppermute | solution.py:19
  84.9 1.9 %collective-permute-start.7 = (bf16[2,256,256]{2,1,0:T(8,128)(2,1)S(1)}, bf16[2,256,256]{2,1,0:T(8,128)(2,1)S(1)}, u32[]{:S(2)}, u32[]{:S(2)}) collective-permute-start(bf16[2,256,256]{2,1,0:T(8,128)(2,1)S(1)} %collective-permute-done.6.refs_9_), channel_id=1, source_target_pairs={{0,1},{1,2},{2,3},{3,4},{4,5},{5,6},{6,7},{7,0},{8,9},{9,10},{10,1... | collective-permute-start | bytes 786440 | tf_op jit(solution)/shard_map/ppermute | solution.py:19
  86.8 4.6 %collective-permute-start.8 = (bf16[2,256,256]{2,1,0:T(8,128)(2,1)S(1)}, bf16[2,256,256]{2,1,0:T(8,128)(2,1)S(1)}, u32[]{:S(2)}, u32[]{:S(2)}) collective-permute-start(bf16[2,256,256]{2,1,0:T(8,128)(2,1)S(1)} %collective-permute-done.6.refs_9_), channel_id=1, source_target_pairs={{0,7},{1,0},{2,1},{3,2},{4,3},{5,4},{6,5},{7,6},{8,15},{9,8},{10,9... | collective-permute-start | bytes 786440 | tf_op jit(solution)/shard_map/ppermute | solution.py:19
  91.4 5.0 %collective-permute-done.7.refs_10_ = bf16[2,256,256]{2,1,0:T(8,128)(2,1)S(1)} collective-permute-done((bf16[2,256,256]{2,1,0:T(8,128)(2,1)S(1)}, bf16[2,256,256]{2,1,0:T(8,128)(2,1)S(1)}, u32[]{:S(2)}, u32[]{:S(2)}) %collective-permute-start.7) | collective-permute-done | bytes 262176 | tf_op jit(solution)/shard_map/ppermute | solution.py:19
  96.3 1.2 collective-permute-done.8.refs_11_
  97.5 0.0 collective-permute-done.4.refs_4_
  97.5 0.0 collective-permute-done.5.refs_5_
  97.5 5.3 %collective-permute-start.10 = (bf16[4,256,256]{2,1,0:T(8,128)(2,1)S(1)}, bf16[4,256,256]{2,1,0:T(8,128)(2,1)S(1)}, u32[]{:S(2)}, u32[]{:S(2)}) collective-permute-start(bf16[4,256,256]{2,1,0:T(8,128)(2,1)S(1)} %collective-permute-done.5.refs_5_), channel_id=1, source_target_pairs={{0,7},{1,0},{2,1},{3,2},{4,3},{5,4},{6,5},{7,6},{8,15},{9,8},{10,9... | collective-permute-start | bytes 1572872 | tf_op jit(solution)/shard_map/ppermute | solution.py:19
  102.9 1.9 %collective-permute-start.9 = (bf16[4,256,256]{2,1,0:T(8,128)(2,1)S(1)}, bf16[4,256,256]{2,1,0:T(8,128)(2,1)S(1)}, u32[]{:S(2)}, u32[]{:S(2)}) collective-permute-start(bf16[4,256,256]{2,1,0:T(8,128)(2,1)S(1)} %collective-permute-done.4.refs_4_), channel_id=1, source_target_pairs={{0,1},{1,2},{2,3},{3,4},{4,5},{5,6},{6,7},{7,0},{8,9},{9,10},{10,1... | collective-permute-start | bytes 1572872 | tf_op jit(solution)/shard_map/ppermute | solution.py:19
  104.8 1.9 %collective-permute-start.11 = (bf16[2,256,256]{2,1,0:T(8,128)(2,1)S(1)}, bf16[2,256,256]{2,1,0:T(8,128)(2,1)S(1)}, u32[]{:S(2)}, u32[]{:S(2)}) collective-permute-start(bf16[2,256,256]{2,1,0:T(8,128)(2,1)S(1)} %collective-permute-done.7.refs_10_), channel_id=1, source_target_pairs={{0,1},{1,2},{2,3},{3,4},{4,5},{5,6},{6,7},{7,0},{8,9},{9,10},{10,1... | collective-permute-start | bytes 786440 | tf_op jit(solution)/shard_map/ppermute | solution.py:19
  106.7 4.6 %collective-permute-start.12 = (bf16[2,256,256]{2,1,0:T(8,128)(2,1)S(1)}, bf16[2,256,256]{2,1,0:T(8,128)(2,1)}, u32[]{:S(2)}, u32[]{:S(2)}) collective-permute-start(bf16[2,256,256]{2,1,0:T(8,128)(2,1)S(1)} %collective-permute-done.8.refs_11_), channel_id=1, source_target_pairs={{0,7},{1,0},{2,1},{3,2},{4,3},{5,4},{6,5},{7,6},{8,15},{9,8},{10,9... | collective-permute-start | bytes 786440 | tf_op jit(solution)/shard_map/ppermute | solution.py:19
  111.3 10.9 %collective-permute-done.11.refs_12_ = bf16[2,256,256]{2,1,0:T(8,128)(2,1)S(1)} collective-permute-done((bf16[2,256,256]{2,1,0:T(8,128)(2,1)S(1)}, bf16[2,256,256]{2,1,0:T(8,128)(2,1)S(1)}, u32[]{:S(2)}, u32[]{:S(2)}) %collective-permute-start.11) | collective-permute-done | bytes 262176 | tf_op jit(solution)/shard_map/ppermute | solution.py:19
  122.3 0.0 collective-permute-done.12.refs_13_
  122.3 1.9 %collective-permute-start.14 = (bf16[2,256,256]{2,1,0:T(8,128)(2,1)S(1)}, bf16[2,256,256]{2,1,0:T(8,128)(2,1)}, u32[]{:S(2)}, u32[]{:S(2)}) collective-permute-start(bf16[2,256,256]{2,1,0:T(8,128)(2,1)S(1)} %collective-permute-done.11.refs_12_), channel_id=1, source_target_pairs={{0,1},{1,2},{2,3},{3,4},{4,5},{5,6},{6,7},{7,0},{8,9},{9,10},{10,1... | collective-permute-start | bytes 786440 | tf_op jit(solution)/shard_map/ppermute | solution.py:19
  124.2 0.0 collective-permute-done.9.refs_6_
  124.2 0.8 copy-done.6
  125.0 4.6 %collective-permute-start.13 = (bf16[4,256,256]{2,1,0:T(8,128)(2,1)S(1)}, bf16[4,256,256]{2,1,0:T(8,128)(2,1)}, u32[]{:S(2)}, u32[]{:S(2)}) collective-permute-start(bf16[4,256,256]{2,1,0:T(8,128)(2,1)S(1)} %collective-permute-done.10.refs_7_), channel_id=1, source_target_pairs={{0,7},{1,0},{2,1},{3,2},{4,3},{5,4},{6,5},{7,6},{8,15},{9,8},{10,9... | collective-permute-start | bytes 1572872 | tf_op jit(solution)/shard_map/ppermute | solution.py:19
  129.6 1.9 %collective-permute-start.15 = (bf16[2,256,256]{2,1,0:T(8,128)(2,1)}, bf16[2,256,256]{2,1,0:T(8,128)(2,1)}, u32[]{:S(2)}, u32[]{:S(2)}) collective-permute-start(bf16[2,256,256]{2,1,0:T(8,128)(2,1)} %collective-permute-done.12.refs_13_), channel_id=1, source_target_pairs={{0,7},{1,0},{2,1},{3,2},{4,3},{5,4},{6,5},{7,6},{8,15},{9,8},{10,9... | collective-permute-start | bytes 786440 | tf_op jit(solution)/shard_map/ppermute | solution.py:19
  131.6 0.0 collective-permute-done.14.refs_14_
  131.6 3.4 %collective-permute-start.16 = (bf16[2,256,256]{2,1,0:T(8,128)(2,1)}, bf16[2,256,256]{2,1,0:T(8,128)(2,1)}, u32[]{:S(2)}, u32[]{:S(2)}) collective-permute-start(bf16[2,256,256]{2,1,0:T(8,128)(2,1)} %collective-permute-done.14.refs_14_), channel_id=1, source_target_pairs={{0,1},{1,2},{2,3},{3,4},{4,5},{5,6},{6,7},{7,0},{8,9},{9,10},{10,1... | collective-permute-start | bytes 786440 | tf_op jit(solution)/shard_map/ppermute | solution.py:19
  134.9 1.4 copy.21.out_index_ref
  136.3 6.3 %collective-permute-done.15.refs_15_ = bf16[2,256,256]{2,1,0:T(8,128)(2,1)} collective-permute-done((bf16[2,256,256]{2,1,0:T(8,128)(2,1)}, bf16[2,256,256]{2,1,0:T(8,128)(2,1)}, u32[]{:S(2)}, u32[]{:S(2)}) %collective-permute-start.15) | collective-permute-done | bytes 262176 | tf_op jit(solution)/shard_map/ppermute | solution.py:19
  142.6 0.0 all-gather.7.cloned.1.call-done
  142.7 0.0 copy-start.11
  142.7 3.4 %shard_map.37 = (f32[4,256,256]{2,1,0:T(8,128)}, f32[16,2,256]{2,1,0:T(2,128)}) custom-call(s32[128]{0:T(128)} %reshape.269.pos_ref, s32[4,2]{1,0:T(4,128)} %copy.21.out_index_ref, bf16[16,256,256]{2,1,0:T(8,128)(2,1)} %bitcast.26, bf16[4,256,256]{2,1,0:T(8,128)(2,1)} %copy-done, bf16[4,256,256]{2,1,0:T(8,128)(2,1)} %copy-done.1, ...), custom_call_target="tpu_custom_call" | custom-call | tf_op jit(solution)/shard_map/pallas_call | solution.py:156
  146.1 10.1 %all-to-all-start.2 = ((f32[16,2,256]{2,1,0:T(2,128)}), f32[16,2,256]{2,1,0:T(2,128)S(1)}, u32[]{:S(2)}, u32[]{:S(2)}) async-start(f32[16,2,256]{2,1,0:T(2,128)} %get-tuple-element.28), calls=%async_computation.2 | async-start | bytes 65536 | tf_op jit(solution)/shard_map/all_to_all | solution.py:176
  156.2 5.7 %all-to-all-done.2 = f32[16,2,256]{2,1,0:T(2,128)S(1)} async-done(((f32[16,2,256]{2,1,0:T(2,128)}), f32[16,2,256]{2,1,0:T(2,128)S(1)}, u32[]{:S(2)}, u32[]{:S(2)}) %all-to-all-start.2) | async-done | bytes 32800 | tf_op jit(solution)/shard_map/all_to_all | solution.py:176
  161.9 0.1 select_select_fusion
  162.0 2.3 %divide_bitcast_fusion = f32[1,4,256,256]{3,2,1,0:T(8,128)} fusion(f32[4,256,256]{2,1,0:T(8,128)} %get-tuple-element.27, f32[4,256]{1,0:T(4,128)S(1)} %select_select_fusion), kind=kLoop, calls=%fused_computation | loop fusion | flops 524288 | bytes 2101248 | tf_op jit(solution)/shard_map/broadcast_in_dim | solution.py:181
  (42 shorter events, 0.2 us)
Async XLA Ops:
  6.5 136.0 %all-gather.5.cloned.1.call-start = ((), (), s32[]{:S(2)}) async-start(), calls=%async_computation.3 | async-start | bytes 2359296 | tf_op jit(solution)/shard_map/all_gather | solution.py:127
  7.3 135.3 %all-gather.7.cloned.1.call-start = ((), (), s32[]{:S(2)}) async-start(), calls=%async_computation.4 | async-start | bytes 4456448 | tf_op jit(solution)/shard_map/all_gather | solution.py:128
  8.0 51.6 %collective-permute-start = (bf16[2,256,256]{2,1,0:T(8,128)(2,1)}, bf16[2,256,256]{2,1,0:T(8,128)(2,1)S(1)}, u32[]{:S(2)}, u32[]{:S(2)}) collective-permute-start(bf16[2,256,256]{2,1,0:T(8,128)(2,1)} %bitcast.29), channel_id=1, source_target_pairs={{0,8},{8,16},{16,24},{24,0},{1,9},{9,17},{17,25},{25,1},{2,10},{10... | collective-permute-start | bytes 786440 | tf_op jit(solution)/shard_map/ppermute | solution.py:19
  14.7 45.0 %collective-permute-start.1 = (bf16[2,256,256]{2,1,0:T(8,128)(2,1)}, bf16[2,256,256]{2,1,0:T(8,128)(2,1)S(1)}, u32[]{:S(2)}, u32[]{:S(2)}) collective-permute-start(bf16[2,256,256]{2,1,0:T(8,128)(2,1)} %bitcast.30), channel_id=1, source_target_pairs={{0,24},{8,0},{16,8},{24,16},{1,25},{9,1},{17,9},{25,17},{2,26},{10... | collective-permute-start | bytes 786440 | tf_op jit(solution)/shard_map/ppermute | solution.py:19
  22.8 13.9 %all-to-all-start.1 = ((s32[16,1,4]{2,1,0:T(1,128)}), s32[16,1,4]{2,1,0:T(1,128)S(1)}, u32[]{:S(2)}, u32[]{:S(2)}) async-start(s32[16,1,4]{2,1,0:T(1,128)} %broadcast_in_dim.109), calls=%async_computation.1 | async-start | bytes 16384 | tf_op jit(solution)/shard_map/all_to_all | solution.py:24
  37.3 22.1 %all-to-all-start = ((s32[32,1,4]{2,1,0:T(1,128)}), s32[32,1,4]{2,1,0:T(1,128)S(1)}, u32[]{:S(2)}, u32[]{:S(2)}) async-start(s32[32,1,4]{2,1,0:T(1,128)} %broadcast_in_dim.108), calls=%async_computation | async-start | bytes 32768 | tf_op jit(solution)/shard_map/all_to_all | solution.py:24
  59.7 82.9 %copy-start = (bf16[4,256,256]{2,1,0:T(8,128)(2,1)}, bf16[4,256,256]{2,1,0:T(8,128)(2,1)S(1)}, u32[]{:S(2)}) copy-start(bf16[4,256,256]{2,1,0:T(8,128)(2,1)S(1)} %constant_dynamic-update-slice_fusion.refs_1_) | copy-start | bytes 1572868
  59.7 14.5 %collective-permute-start.2 = (bf16[4,256,256]{2,1,0:T(8,128)(2,1)S(1)}, bf16[4,256,256]{2,1,0:T(8,128)(2,1)S(1)}, u32[]{:S(2)}, u32[]{:S(2)}) collective-permute-start(bf16[4,256,256]{2,1,0:T(8,128)(2,1)S(1)} %constant_dynamic-update-slice_fusion.refs_1_), channel_id=1, source_target_pairs={{0,1},{1,2},{2,3},{3,4},{4,5},{5,6},{6,7},{7,0},{8,9},{9,10},{10,1... | collective-permute-start | bytes 1572872 | tf_op jit(solution)/shard_map/ppermute | solution.py:19
  62.0 13.1 %collective-permute-start.3 = (bf16[4,256,256]{2,1,0:T(8,128)(2,1)S(1)}, bf16[4,256,256]{2,1,0:T(8,128)(2,1)S(1)}, u32[]{:S(2)}, u32[]{:S(2)}) collective-permute-start(bf16[4,256,256]{2,1,0:T(8,128)(2,1)S(1)} %constant_dynamic-update-slice_fusion.refs_1_), channel_id=1, source_target_pairs={{0,7},{1,0},{2,1},{3,2},{4,3},{5,4},{6,5},{7,6},{8,15},{9,8},{10,9... | collective-permute-start | bytes 1572872 | tf_op jit(solution)/shard_map/ppermute | solution.py:19
  67.1 17.7 %collective-permute-start.6 = (bf16[2,256,256]{2,1,0:T(8,128)(2,1)S(1)}, bf16[2,256,256]{2,1,0:T(8,128)(2,1)S(1)}, u32[]{:S(2)}, u32[]{:S(2)}) collective-permute-start(bf16[2,256,256]{2,1,0:T(8,128)(2,1)S(1)} %collective-permute-done), channel_id=1, source_target_pairs={{0,8},{8,16},{16,24},{24,0},{1,9},{9,17},{17,25},{25,1},{2,10},{10... | collective-permute-start | bytes 786440 | tf_op jit(solution)/shard_map/ppermute | solution.py:19
  74.1 68.5 %copy-start.1 = (bf16[4,256,256]{2,1,0:T(8,128)(2,1)}, bf16[4,256,256]{2,1,0:T(8,128)(2,1)S(1)}, u32[]{:S(2)}) copy-start(bf16[4,256,256]{2,1,0:T(8,128)(2,1)S(1)} %collective-permute-done.2.refs_2_) | copy-start | bytes 1572868
  75.0 67.6 %copy-start.2 = (bf16[4,256,256]{2,1,0:T(8,128)(2,1)}, bf16[4,256,256]{2,1,0:T(8,128)(2,1)S(1)}, u32[]{:S(2)}) copy-start(bf16[4,256,256]{2,1,0:T(8,128)(2,1)S(1)} %collective-permute-done.3.refs_3_) | copy-start | bytes 1572868
  75.0 22.5 %collective-permute-start.4 = (bf16[4,256,256]{2,1,0:T(8,128)(2,1)S(1)}, bf16[4,256,256]{2,1,0:T(8,128)(2,1)S(1)}, u32[]{:S(2)}, u32[]{:S(2)}) collective-permute-start(bf16[4,256,256]{2,1,0:T(8,128)(2,1)S(1)} %collective-permute-done.2.refs_2_), channel_id=1, source_target_pairs={{0,1},{1,2},{2,3},{3,4},{4,5},{5,6},{6,7},{7,0},{8,9},{9,10},{10,1... | collective-permute-start | bytes 1572872 | tf_op jit(solution)/shard_map/ppermute | solution.py:19
  77.0 20.5 %collective-permute-start.5 = (bf16[4,256,256]{2,1,0:T(8,128)(2,1)S(1)}, bf16[4,256,256]{2,1,0:T(8,128)(2,1)S(1)}, u32[]{:S(2)}, u32[]{:S(2)}) collective-permute-start(bf16[4,256,256]{2,1,0:T(8,128)(2,1)S(1)} %collective-permute-done.3.refs_3_), channel_id=1, source_target_pairs={{0,7},{1,0},{2,1},{3,2},{4,3},{5,4},{6,5},{7,6},{8,15},{9,8},{10,9... | collective-permute-start | bytes 1572872 | tf_op jit(solution)/shard_map/ppermute | solution.py:19
  84.9 57.8 %copy-start.7 = (bf16[2,256,256]{2,1,0:T(8,128)(2,1)}, bf16[2,256,256]{2,1,0:T(8,128)(2,1)S(1)}, u32[]{:S(2)}) copy-start(bf16[2,256,256]{2,1,0:T(8,128)(2,1)S(1)} %collective-permute-done.6.refs_9_) | copy-start | bytes 786436
  84.9 11.5 %collective-permute-start.7 = (bf16[2,256,256]{2,1,0:T(8,128)(2,1)S(1)}, bf16[2,256,256]{2,1,0:T(8,128)(2,1)S(1)}, u32[]{:S(2)}, u32[]{:S(2)}) collective-permute-start(bf16[2,256,256]{2,1,0:T(8,128)(2,1)S(1)} %collective-permute-done.6.refs_9_), channel_id=1, source_target_pairs={{0,1},{1,2},{2,3},{3,4},{4,5},{5,6},{6,7},{7,0},{8,9},{9,10},{10,1... | collective-permute-start | bytes 786440 | tf_op jit(solution)/shard_map/ppermute | solution.py:19
  86.8 10.8 %collective-permute-start.8 = (bf16[2,256,256]{2,1,0:T(8,128)(2,1)S(1)}, bf16[2,256,256]{2,1,0:T(8,128)(2,1)S(1)}, u32[]{:S(2)}, u32[]{:S(2)}) collective-permute-start(bf16[2,256,256]{2,1,0:T(8,128)(2,1)S(1)} %collective-permute-done.6.refs_9_), channel_id=1, source_target_pairs={{0,7},{1,0},{2,1},{3,2},{4,3},{5,4},{6,5},{7,6},{8,15},{9,8},{10,9... | collective-permute-start | bytes 786440 | tf_op jit(solution)/shard_map/ppermute | solution.py:19
  96.3 33.3 %copy-start.8 = (bf16[2,256,256]{2,1,0:T(8,128)(2,1)}, bf16[2,256,256]{2,1,0:T(8,128)(2,1)S(1)}, u32[]{:S(2)}) copy-start(bf16[2,256,256]{2,1,0:T(8,128)(2,1)S(1)} %collective-permute-done.7.refs_10_) | copy-start | bytes 786436
  97.5 34.0 %copy-start.9 = (bf16[2,256,256]{2,1,0:T(8,128)(2,1)}, bf16[2,256,256]{2,1,0:T(8,128)(2,1)S(1)}, u32[]{:S(2)}) copy-start(bf16[2,256,256]{2,1,0:T(8,128)(2,1)S(1)} %collective-permute-done.8.refs_11_) | copy-start | bytes 786436
  97.5 45.1 %copy-start.3 = (bf16[4,256,256]{2,1,0:T(8,128)(2,1)}, bf16[4,256,256]{2,1,0:T(8,128)(2,1)S(1)}, u32[]{:S(2)}) copy-start(bf16[4,256,256]{2,1,0:T(8,128)(2,1)S(1)} %collective-permute-done.4.refs_4_) | copy-start | bytes 1572868
  97.5 45.1 %copy-start.4 = (bf16[4,256,256]{2,1,0:T(8,128)(2,1)}, bf16[4,256,256]{2,1,0:T(8,128)(2,1)S(1)}, u32[]{:S(2)}) copy-start(bf16[4,256,256]{2,1,0:T(8,128)(2,1)S(1)} %collective-permute-done.5.refs_5_) | copy-start | bytes 1572868
  97.5 26.6 %collective-permute-start.10 = (bf16[4,256,256]{2,1,0:T(8,128)(2,1)S(1)}, bf16[4,256,256]{2,1,0:T(8,128)(2,1)S(1)}, u32[]{:S(2)}, u32[]{:S(2)}) collective-permute-start(bf16[4,256,256]{2,1,0:T(8,128)(2,1)S(1)} %collective-permute-done.5.refs_5_), channel_id=1, source_target_pairs={{0,7},{1,0},{2,1},{3,2},{4,3},{5,4},{6,5},{7,6},{8,15},{9,8},{10,9... | collective-permute-start | bytes 1572872 | tf_op jit(solution)/shard_map/ppermute | solution.py:19
  102.9 21.3 %collective-permute-start.9 = (bf16[4,256,256]{2,1,0:T(8,128)(2,1)S(1)}, bf16[4,256,256]{2,1,0:T(8,128)(2,1)S(1)}, u32[]{:S(2)}, u32[]{:S(2)}) collective-permute-start(bf16[4,256,256]{2,1,0:T(8,128)(2,1)S(1)} %collective-permute-done.4.refs_4_), channel_id=1, source_target_pairs={{0,1},{1,2},{2,3},{3,4},{4,5},{5,6},{6,7},{7,0},{8,9},{9,10},{10,1... | collective-permute-start | bytes 1572872 | tf_op jit(solution)/shard_map/ppermute | solution.py:19
  104.8 17.4 %collective-permute-start.11 = (bf16[2,256,256]{2,1,0:T(8,128)(2,1)S(1)}, bf16[2,256,256]{2,1,0:T(8,128)(2,1)S(1)}, u32[]{:S(2)}, u32[]{:S(2)}) collective-permute-start(bf16[2,256,256]{2,1,0:T(8,128)(2,1)S(1)} %collective-permute-done.7.refs_10_), channel_id=1, source_target_pairs={{0,1},{1,2},{2,3},{3,4},{4,5},{5,6},{6,7},{7,0},{8,9},{9,10},{10,1... | collective-permute-start | bytes 786440 | tf_op jit(solution)/shard_map/ppermute | solution.py:19
  106.7 15.5 %collective-permute-start.12 = (bf16[2,256,256]{2,1,0:T(8,128)(2,1)S(1)}, bf16[2,256,256]{2,1,0:T(8,128)(2,1)}, u32[]{:S(2)}, u32[]{:S(2)}) collective-permute-start(bf16[2,256,256]{2,1,0:T(8,128)(2,1)S(1)} %collective-permute-done.8.refs_11_), channel_id=1, source_target_pairs={{0,7},{1,0},{2,1},{3,2},{4,3},{5,4},{6,5},{7,6},{8,15},{9,8},{10,9... | collective-permute-start | bytes 786440 | tf_op jit(solution)/shard_map/ppermute | solution.py:19
  122.2 9.3 %copy-start.10 = (bf16[2,256,256]{2,1,0:T(8,128)(2,1)}, bf16[2,256,256]{2,1,0:T(8,128)(2,1)S(1)}, u32[]{:S(2)}) copy-start(bf16[2,256,256]{2,1,0:T(8,128)(2,1)S(1)} %collective-permute-done.11.refs_12_) | copy-start | bytes 786436
  122.3 9.3 %collective-permute-start.14 = (bf16[2,256,256]{2,1,0:T(8,128)(2,1)S(1)}, bf16[2,256,256]{2,1,0:T(8,128)(2,1)}, u32[]{:S(2)}, u32[]{:S(2)}) collective-permute-start(bf16[2,256,256]{2,1,0:T(8,128)(2,1)S(1)} %collective-permute-done.11.refs_12_), channel_id=1, source_target_pairs={{0,1},{1,2},{2,3},{3,4},{4,5},{5,6},{6,7},{7,0},{8,9},{9,10},{10,1... | collective-permute-start | bytes 786440 | tf_op jit(solution)/shard_map/ppermute | solution.py:19
  124.2 18.5 %copy-start.5 = (bf16[4,256,256]{2,1,0:T(8,128)(2,1)}, bf16[4,256,256]{2,1,0:T(8,128)(2,1)S(1)}, u32[]{:S(2)}) copy-start(bf16[4,256,256]{2,1,0:T(8,128)(2,1)S(1)} %collective-permute-done.10.refs_7_) | copy-start | bytes 1572868
  124.2 0.8 copy-start.6
  125.0 17.5 %collective-permute-start.13 = (bf16[4,256,256]{2,1,0:T(8,128)(2,1)S(1)}, bf16[4,256,256]{2,1,0:T(8,128)(2,1)}, u32[]{:S(2)}, u32[]{:S(2)}) collective-permute-start(bf16[4,256,256]{2,1,0:T(8,128)(2,1)S(1)} %collective-permute-done.10.refs_7_), channel_id=1, source_target_pairs={{0,7},{1,0},{2,1},{3,2},{4,3},{5,4},{6,5},{7,6},{8,15},{9,8},{10,9... | collective-permute-start | bytes 1572872 | tf_op jit(solution)/shard_map/ppermute | solution.py:19
  129.6 12.9 %collective-permute-start.15 = (bf16[2,256,256]{2,1,0:T(8,128)(2,1)}, bf16[2,256,256]{2,1,0:T(8,128)(2,1)}, u32[]{:S(2)}, u32[]{:S(2)}) collective-permute-start(bf16[2,256,256]{2,1,0:T(8,128)(2,1)} %collective-permute-done.12.refs_13_), channel_id=1, source_target_pairs={{0,7},{1,0},{2,1},{3,2},{4,3},{5,4},{6,5},{7,6},{8,15},{9,8},{10,9... | collective-permute-start | bytes 786440 | tf_op jit(solution)/shard_map/ppermute | solution.py:19
  131.6 11.0 %collective-permute-start.16 = (bf16[2,256,256]{2,1,0:T(8,128)(2,1)}, bf16[2,256,256]{2,1,0:T(8,128)(2,1)}, u32[]{:S(2)}, u32[]{:S(2)}) collective-permute-start(bf16[2,256,256]{2,1,0:T(8,128)(2,1)} %collective-permute-done.14.refs_14_), channel_id=1, source_target_pairs={{0,1},{1,2},{2,3},{3,4},{4,5},{5,6},{6,7},{7,0},{8,9},{9,10},{10,1... | collective-permute-start | bytes 786440 | tf_op jit(solution)/shard_map/ppermute | solution.py:19
  142.7 13.5 %copy-start.11 = (s32[1,4,2]{1,2,0:T(2,128)S(1)}, s32[1,4,2]{1,2,0:T(2,128)}, u32[]{:S(2)}) copy-start(s32[1,4,2]{1,2,0:T(2,128)} %param.5) | copy-start | bytes 100
  146.1 15.8 %all-to-all-start.2 = ((f32[16,2,256]{2,1,0:T(2,128)}), f32[16,2,256]{2,1,0:T(2,128)S(1)}, u32[]{:S(2)}, u32[]{:S(2)}) async-start(f32[16,2,256]{2,1,0:T(2,128)} %get-tuple-element.28), calls=%async_computation.2 | async-start | bytes 65536 | tf_op jit(solution)/shard_map/all_to_all | solution.py:176
Sparse Core Ops, SparseCore 0:
  9.4 45.7 all-gather.4
  57.4 49.4 all-gather.6

commit v3 on v2

--- a/solution.py
+++ b/solution.py
@@ -10,7 +10,7 @@
 FINE = (("zl", 2), ("x", 4), ("core", 2), ("zh", 4), ("y", 8))
 ROW = ("zl", "x", "core")
 COL = ("zh", "y")
-N_ROW, N_COL, N_ZH, N_Y = 16, 32, 4, 8
+N_ROW, N_ZH, N_Y = 16, 4, 8
 RIGHTS = 32
 BUFS = 8
 
@@ -94,23 +94,16 @@
 
 
 def match_table(in_index, out_index):
-    row = to_all(in_index.reshape(1, -1), COL, N_COL).reshape(N_ZH, N_Y, -1, 2)
+    row = to_all(to_all(in_index.reshape(1, -1), "zh", N_ZH), "y", N_Y)
+    row = row.reshape(N_Y, N_ZH, -1, 2)
     column = to_all(in_index.reshape(1, -1), ROW, N_ROW).reshape(-1, 2)
-    zh, y = lax.axis_index("zh"), lax.axis_index("y")
-    hop = (jnp.arange(N_ZH, dtype=jnp.int32)[:, None, None] - zh) % N_ZH
-    source = jnp.arange(N_Y, dtype=jnp.int32)[None, :, None]
+    source = jnp.arange(N_Y, dtype=jnp.int32)[:, None, None]
+    hop = (jnp.arange(N_ZH, dtype=jnp.int32)[None, :, None] - lax.axis_index("zh")) % N_ZH
     slot = jnp.arange(in_index.shape[0], dtype=jnp.int32)[None, None, :]
-    away = (source - y) % N_Y
+    away = (source - lax.axis_index("y")) % N_Y
     block = jnp.where(away == 4, 7, jnp.where(away < 4, 2 * away, 2 * (8 - away) - 1))
-    place = jnp.where(
-        hop == 0,
-        2 * source + slot,
-        jnp.where(
-            hop == 2,
-            48 + 2 * block + slot,
-            16 + 4 * block + slot + jnp.where(hop == 1, 2, 0),
-        ),
-    )
+    kind = jnp.where(hop == 0, 0, jnp.where(hop == 1, 4, 2))
+    place = jnp.where(hop == 2, 48 + 2 * source, 6 * block + kind) + slot
     matches = (
         (row[None, None, ..., 0] == out_index[:, 0][:, None, None, None, None])
         & (row[None, None, ..., 1] == column[:, 0][None, :, None, None, None])
@@ -124,35 +117,24 @@
     tiles, in_index, out_index = tiles[0], in_index[0], out_index[0]
     out_count = out_index.shape[0]
 
-    own = lax.all_gather(tiles, "y", axis=0, tiled=True)
     right = lax.all_gather(tiles, ROW, axis=0, tiled=True)
     pos = match_table(in_index, out_index)
 
     up = shift(tiles, "zh", N_ZH, 1)
     down = shift(tiles, "zh", N_ZH, -1)
-    near = [jnp.concatenate([up, down])]
-    far = [shift(up, "zh", N_ZH, 1)]
-
-    def step(ring, ahead, back):
+    up, down = lax.optimization_barrier((up, down))
+    far = shift(up, "zh", N_ZH, 1)
+    ahead = back = jnp.concatenate([tiles, up, down])
+    ring = [ahead]
+    for _ in range(3):
         ahead, back = shift(ahead, "y", N_Y, 1), shift(back, "y", N_Y, -1)
         ring += [ahead, back]
-        return ahead, back
+    far, right, _ = lax.optimization_barrier((far, right, ring[1:3]))
+    far = lax.all_gather(far, "y", axis=0, tiled=True)
+    ahead, back, pos = lax.optimization_barrier((ahead, back, pos))
+    ring += [shift(ahead[:3], "y", N_Y, 1), shift(back[3:], "y", N_Y, -1)]
 
-    near_ends = step(near, near[0], near[0])
-    far_ends = step(far, far[0], far[0])
-    near_ends, pos = lax.optimization_barrier((near_ends, pos))
-    near_ends = step(near, *near_ends)
-    far_ends, _ = lax.optimization_barrier((far_ends, near[1:3]))
-    far_ends = step(far, *far_ends)
-    near_ends, _ = lax.optimization_barrier((near_ends, far[1:3]))
-    near_ends = step(near, *near_ends)
-    far_ends, _ = lax.optimization_barrier((far_ends, near[3:5]))
-    far_ends = step(far, *far_ends)
-    near_ends, _ = lax.optimization_barrier((near_ends, far[3:5]))
-    near.append(shift(near_ends[1], "y", N_Y, -1))
-    far.append(shift(far_ends[0], "y", N_Y, 1))
-
-    lefts = [own] + near + far
+    lefts = ring + [far]
     squared, parts = pl.pallas_call(
         product_kernel,
         grid_spec=pltpu.PrefetchScalarGridSpec(

time: 172 us -> 181 us (1.052)
  waiting for transfers between devices: 54.4 us -> 76.3 us
  starting transfers between devices: 88.7 us -> 73.4 us
    ppermute x17 -> x11, starting transfers between devices: 61.3 us -> 42.6 us  [shift(): lax.ppermute(value, axis, [(i, (i + by) % size) for i in range(size)])]
    ppermute x17 -> x11, waiting for transfers between devices: 31.6 us -> 47.5 us  [shift(): lax.ppermute(value, axis, [(i, (i + by) % size) for i in range(size)])]
    all_gather x1, waiting for transfers between devices: 0.01 us -> 5.58 us  [shards(): right = lax.all_gather(tiles, ROW, axis=0, tiled=True)]
    all_to_all x1, starting transfers between devices: 10.1 us -> 11.9 us  [shards(): lax.all_to_all(parts, ROW, split_axis=0, concat_axis=0)]
    all_to_all x2 -> x3, starting transfers between devices: 17.2 us -> 18.9 us  [to_all(): return lax.all_to_all(every, axes, split_axis=0, concat_axis=0)]
    all_to_all x2 -> x3, waiting for transfers between devices: 15.6 us -> 16.6 us  [to_all(): return lax.all_to_all(every, axes, split_axis=0, concat_axis=0)]
  transfers between devices with their start and end apart: 22 -> 17, of which waited for: 10 -> 11; matrix products, arithmetic and copies ran while one was open for 4% -> 5% of each run, Pallas kernels for 0% -> 0%
where the time goes in v3:
time: 181 us
  waiting for transfers between devices  76.3 us (42%)
  starting transfers between devices  73.4 us (41%)
  between operations  13.6 us (8%)
  local copies, waits for them, and re-layouts  6.94 us (4%)
  other arithmetic  5.27 us (3%)
  Pallas kernels  5.02 us (3%)
    ppermute x11, waiting for transfers between devices, shift(): lax.ppermute(value, axis, [(i, (i + by) % size) for i in range(size)])  47.5 us
    ppermute x11, starting transfers between devices, shift(): lax.ppermute(value, axis, [(i, (i + by) % size) for i in range(size)])  42.6 us
    all_to_all x3, starting transfers between devices, to_all(): return lax.all_to_all(every, axes, split_axis=0, concat_axis=0)  18.9 us
    all_to_all x3, waiting for transfers between devices, to_all(): return lax.all_to_all(every, axes, split_axis=0, concat_axis=0)  16.6 us
    all_to_all x1, starting transfers between devices, shards(): lax.all_to_all(parts, ROW, split_axis=0, concat_axis=0)  11.9 us
    all_to_all x1, waiting for transfers between devices, shards(): lax.all_to_all(parts, ROW, split_axis=0, concat_axis=0)  5.78 us
    all_gather x1, waiting for transfers between devices, shards(): right = lax.all_gather(tiles, ROW, axis=0, tiled=True)  5.58 us
    pallas_call x1, Pallas kernels, shards(): pl.pallas_call(product_kernel, grid_spec=pltpu.PrefetchScalarGridSpec(num...  5.02 us
  transfers between devices with their start and end apart: 17, of which 11 were waited for; matrix products, arithmetic and copies ran while one was open for 5% of the time, Pallas kernels for 0%

profile of v3, /device:TPU:1, one launch (start us, length us, event | category | flops | bytes accessed | tf_op | source)
XLA Modules:
  0.0 180.5 jit_solution(3683573504650740757)
XLA Ops:
  6.5 0.0 all-gather.6.cloned.1.call-start
  6.5 0.7 all-gather.6.cloned.1.call-update
  7.3 0.0 all-gather.4.cloned.1.call-start
  7.3 6.6 %collective-permute-start = (bf16[2,256,256]{2,1,0:T(8,128)(2,1)}, bf16[2,256,256]{2,1,0:T(8,128)(2,1)S(1)}, u32[]{:S(2)}, u32[]{:S(2)}) collective-permute-start(bf16[2,256,256]{2,1,0:T(8,128)(2,1)} %bitcast.24), channel_id=1, source_target_pairs={{0,8},{8,16},{16,24},{24,0},{1,9},{9,17},{17,25},{25,1},{2,10},{10... | collective-permute-start | bytes 786440 | tf_op jit(solution)/shard_map/ppermute | solution.py:19
  13.9 6.8 %collective-permute-start.1 = (bf16[2,256,256]{2,1,0:T(8,128)(2,1)}, bf16[2,256,256]{2,1,0:T(8,128)(2,1)S(1)}, u32[]{:S(2)}, u32[]{:S(2)}) collective-permute-start(bf16[2,256,256]{2,1,0:T(8,128)(2,1)} %bitcast.25), channel_id=1, source_target_pairs={{0,24},{8,0},{16,8},{24,16},{1,25},{9,1},{17,9},{25,17},{2,26},{10... | collective-permute-start | bytes 786440 | tf_op jit(solution)/shard_map/ppermute | solution.py:19
  20.7 3.9 %collective-permute-done = bf16[2,256,256]{2,1,0:T(8,128)(2,1)S(1)} collective-permute-done((bf16[2,256,256]{2,1,0:T(8,128)(2,1)}, bf16[2,256,256]{2,1,0:T(8,128)(2,1)S(1)}, u32[]{:S(2)}, u32[]{:S(2)}) %collective-permute-start) | collective-permute-done | bytes 262176 | tf_op jit(solution)/shard_map/ppermute | solution.py:19
  24.6 7.4 %collective-permute-done.1 = bf16[2,256,256]{2,1,0:T(8,128)(2,1)S(1)} collective-permute-done((bf16[2,256,256]{2,1,0:T(8,128)(2,1)}, bf16[2,256,256]{2,1,0:T(8,128)(2,1)S(1)}, u32[]{:S(2)}, u32[]{:S(2)}) %collective-permute-start.1) | collective-permute-done | bytes 262176 | tf_op jit(solution)/shard_map/ppermute | solution.py:19
  32.0 1.0 pad_maximum_fusion.refs_0_
  33.1 0.0 copy-start
  33.1 3.2 %collective-permute-start.2 = (bf16[6,256,256]{2,1,0:T(8,128)(2,1)S(1)}, bf16[6,256,256]{2,1,0:T(8,128)(2,1)S(1)}, u32[]{:S(2)}, u32[]{:S(2)}) collective-permute-start(bf16[6,256,256]{2,1,0:T(8,128)(2,1)S(1)} %pad_maximum_fusion.refs_0_), channel_id=1, source_target_pairs={{0,1},{1,2},{2,3},{3,4},{4,5},{5,6},{6,7},{7,0},{8,9},{9,10},{10,1... | collective-permute-start | bytes 2359304 | tf_op jit(solution)/shard_map/ppermute | solution.py:19
  36.3 3.8 %collective-permute-start.5 = (bf16[6,256,256]{2,1,0:T(8,128)(2,1)S(1)}, bf16[6,256,256]{2,1,0:T(8,128)(2,1)S(1)}, u32[]{:S(2)}, u32[]{:S(2)}) collective-permute-start(bf16[6,256,256]{2,1,0:T(8,128)(2,1)S(1)} %pad_maximum_fusion.refs_0_), channel_id=1, source_target_pairs={{0,7},{1,0},{2,1},{3,2},{4,3},{5,4},{6,5},{7,6},{8,15},{9,8},{10,9... | collective-permute-start | bytes 2359304 | tf_op jit(solution)/shard_map/ppermute | solution.py:19
  40.1 2.7 %collective-permute-start.10 = (bf16[2,256,256]{2,1,0:T(8,128)(2,1)S(1)}, bf16[2,256,256]{2,1,0:T(8,128)(2,1)S(1)}, u32[]{:S(2)}, u32[]{:S(2)}) collective-permute-start(bf16[2,256,256]{2,1,0:T(8,128)(2,1)S(1)} %collective-permute-done), channel_id=1, source_target_pairs={{0,8},{8,16},{16,24},{24,0},{1,9},{9,17},{17,25},{25,1},{2,10},{10... | collective-permute-start | bytes 786440 | tf_op jit(solution)/shard_map/ppermute | solution.py:19
  42.8 19.5 %collective-permute-done.10 = bf16[2,256,256]{2,1,0:T(8,128)(2,1)S(1)} collective-permute-done((bf16[2,256,256]{2,1,0:T(8,128)(2,1)S(1)}, bf16[2,256,256]{2,1,0:T(8,128)(2,1)S(1)}, u32[]{:S(2)}, u32[]{:S(2)}) %collective-permute-start.10) | collective-permute-done | bytes 262176 | tf_op jit(solution)/shard_map/ppermute | solution.py:19
  62.3 0.0 collective-permute-done.2.refs_1_
  62.3 0.0 collective-permute-done.5.refs_2_
  62.4 0.0 copy-start.4
  62.4 5.6 %all-gather.6.cloned.1.call-done = bf16[1,32,256,256]{3,2,0,1:T(8,128)(2,1)} async-done(((bf16[1,2,256,256]{3,2,0,1:T(8,128)(2,1)}), bf16[1,32,256,256]{3,2,0,1:T(8,128)(2,1)}) %all-gather.6.cloned.1.call-update) | async-done | bytes 4194320 | tf_op jit(solution)/shard_map/all_gather | solution.py:120
  67.9 0.0 copy-done.5
  67.9 0.0 all-gather.4.cloned.1.call-update
  68.0 0.8 broadcast_in_dim.107
  68.7 0.6 broadcast_in_dim.108
  69.3 6.2 %all-to-all-start = ((s32[4,1,4]{2,1,0:T(1,128)}), s32[4,1,4]{2,1,0:T(1,128)S(1)}, u32[]{:S(2)}, u32[]{:S(2)}) async-start(s32[4,1,4]{2,1,0:T(1,128)} %broadcast_in_dim.108), calls=%async_computation | async-start | bytes 4096 | tf_op jit(solution)/shard_map/all_to_all | solution.py:24
  75.5 0.1 add_select_fusion
  75.6 2.4 %collective-permute-start.3 = (bf16[6,256,256]{2,1,0:T(8,128)(2,1)S(1)}, bf16[6,256,256]{2,1,0:T(8,128)(2,1)}, u32[]{:S(2)}, u32[]{:S(2)}) collective-permute-start(bf16[6,256,256]{2,1,0:T(8,128)(2,1)S(1)} %collective-permute-done.2.refs_1_), channel_id=1, source_target_pairs={{0,1},{1,2},{2,3},{3,4},{4,5},{5,6},{6,7},{7,0},{8,9},{9,10},{10,1... | collective-permute-start | bytes 2359304 | tf_op jit(solution)/shard_map/ppermute | solution.py:19
  78.0 4.1 %collective-permute-start.6 = (bf16[6,256,256]{2,1,0:T(8,128)(2,1)S(1)}, bf16[6,256,256]{2,1,0:T(8,128)(2,1)}, u32[]{:S(2)}, u32[]{:S(2)}) collective-permute-start(bf16[6,256,256]{2,1,0:T(8,128)(2,1)S(1)} %collective-permute-done.5.refs_2_), channel_id=1, source_target_pairs={{0,7},{1,0},{2,1},{3,2},{4,3},{5,4},{6,5},{7,6},{8,15},{9,8},{10,9... | collective-permute-start | bytes 2359304 | tf_op jit(solution)/shard_map/ppermute | solution.py:19
  82.1 0.8 slice_bitcast_fusion.1
  82.9 0.0 all-to-all-done
  82.9 0.6 broadcast_in_dim.111
  83.5 5.9 %all-to-all-start.2 = ((s32[16,1,4]{2,1,0:T(1,128)}), s32[16,1,4]{2,1,0:T(1,128)S(1)}, u32[]{:S(2)}, u32[]{:S(2)}) async-start(s32[16,1,4]{2,1,0:T(1,128)} %broadcast_in_dim.111), calls=%async_computation.2 | async-start | bytes 16384 | tf_op jit(solution)/shard_map/all_to_all | solution.py:24
  89.4 0.7 broadcast_compare_fusion.4
  90.0 4.7 %all-to-all-done.2 = s32[16,1,4]{2,1,0:T(1,128)S(1)} async-done(((s32[16,1,4]{2,1,0:T(1,128)}), s32[16,1,4]{2,1,0:T(1,128)S(1)}, u32[]{:S(2)}, u32[]{:S(2)}) %all-to-all-start.2) | async-done | bytes 288 | tf_op jit(solution)/shard_map/all_to_all | solution.py:24
  94.8 0.6 broadcast_in_dim.110
  95.4 6.8 %all-to-all-start.1 = ((s32[8,4,1,4]{3,1,2,0:T(4,128)}), s32[8,4,1,4]{3,1,2,0:T(4,128)S(1)}, u32[]{:S(2)}, u32[]{:S(2)}) async-start(s32[8,4,1,4]{3,1,2,0:T(4,128)} %broadcast_in_dim.110), calls=%async_computation.1 | async-start | bytes 32768 | tf_op jit(solution)/shard_map/all_to_all | solution.py:24
  102.2 0.5 broadcast.363
  102.7 0.6 reduce.7
  103.4 0.1 reshape.263
  103.4 0.2 slice_reduce_fusion.1
  103.6 0.1 broadcast_compare_fusion.2
  103.7 11.9 %all-to-all-done.1 = s32[8,4,1,4]{3,1,2,0:T(4,128)S(1)} async-done(((s32[8,4,1,4]{3,1,2,0:T(4,128)}), s32[8,4,1,4]{3,1,2,0:T(4,128)S(1)}, u32[]{:S(2)}, u32[]{:S(2)}) %all-to-all-start.1) | async-done | bytes 544 | tf_op jit(solution)/shard_map/all_to_all | solution.py:24
  115.6 0.1 copy.21
  115.7 0.0 collective-permute-done.3.refs_3_
  115.7 4.3 %collective-permute-start.4 = (bf16[6,256,256]{2,1,0:T(8,128)(2,1)}, bf16[6,256,256]{2,1,0:T(8,128)(2,1)S(1)}, u32[]{:S(2)}, u32[]{:S(2)}) collective-permute-start(bf16[6,256,256]{2,1,0:T(8,128)(2,1)} %collective-permute-done.3.refs_3_), channel_id=1, source_target_pairs={{0,1},{1,2},{2,3},{3,4},{4,5},{5,6},{6,7},{7,0},{8,9},{9,10},{10,1... | collective-permute-start | bytes 2359304 | tf_op jit(solution)/shard_map/ppermute | solution.py:19
  120.0 0.0 copy-done.4
  120.0 0.0 collective-permute-done.6.refs_4_
  120.0 2.2 %collective-permute-start.7 = (bf16[6,256,256]{2,1,0:T(8,128)(2,1)}, bf16[6,256,256]{2,1,0:T(8,128)(2,1)S(1)}, u32[]{:S(2)}, u32[]{:S(2)}) collective-permute-start(bf16[6,256,256]{2,1,0:T(8,128)(2,1)} %collective-permute-done.6.refs_4_), channel_id=1, source_target_pairs={{0,7},{1,0},{2,1},{3,2},{4,3},{5,4},{6,5},{7,6},{8,15},{9,8},{10,9... | collective-permute-start | bytes 2359304 | tf_op jit(solution)/shard_map/ppermute | solution.py:19
  122.2 0.1 broadcast_compare_fusion.1
  122.3 0.1 broadcast_compare_fusion
  122.4 0.1 select_reduce_fusion
  122.5 0.6 reshape.264.pos_ref
  123.2 12.4 %collective-permute-done.4.refs_5_ = bf16[6,256,256]{2,1,0:T(8,128)(2,1)S(1)} collective-permute-done((bf16[6,256,256]{2,1,0:T(8,128)(2,1)}, bf16[6,256,256]{2,1,0:T(8,128)(2,1)S(1)}, u32[]{:S(2)}, u32[]{:S(2)}) %collective-permute-start.4) | collective-permute-done | bytes 786464 | tf_op jit(solution)/shard_map/ppermute | solution.py:19
  135.6 0.6 collective-permute-done.7.refs_6_
  136.2 2.1 %collective-permute-start.8 = (bf16[3,256,256]{2,1,0:T(8,128)(2,1)S(1)}, bf16[3,256,256]{2,1,0:T(8,128)(2,1)}, u32[]{:S(2)}, u32[]{:S(2)}) collective-permute-start(bf16[3,256,256]{2,1,0:T(8,128)(2,1)S(1)} %slice.42), channel_id=1, source_target_pairs={{0,1},{1,2},{2,3},{3,4},{4,5},{5,6},{6,7},{7,0},{8,9},{9,10},{10,1... | collective-permute-start | bytes 1179656 | tf_op jit(solution)/shard_map/ppermute | solution.py:19
  138.3 0.8 slice.43
  139.1 4.4 %collective-permute-start.9 = (bf16[3,256,256]{2,1,0:T(8,128)(2,1)}, bf16[3,256,256]{2,1,0:T(8,128)(2,1)}, u32[]{:S(2)}, u32[]{:S(2)}) collective-permute-start(bf16[3,256,256]{2,1,0:T(8,128)(2,1)} %slice.43), channel_id=1, source_target_pairs={{0,7},{1,0},{2,1},{3,2},{4,3},{5,4},{6,5},{7,6},{8,15},{9,8},{10,9... | collective-permute-start | bytes 1179656 | tf_op jit(solution)/shard_map/ppermute | solution.py:19
  143.5 1.3 copy.27.out_index_ref
  144.8 1.3 collective-permute-done.8.refs_7_
  146.0 2.4 %collective-permute-done.9.refs_8_ = bf16[3,256,256]{2,1,0:T(8,128)(2,1)} collective-permute-done((bf16[3,256,256]{2,1,0:T(8,128)(2,1)}, bf16[3,256,256]{2,1,0:T(8,128)(2,1)}, u32[]{:S(2)}, u32[]{:S(2)}) %collective-permute-start.9) | collective-permute-done | bytes 393248 | tf_op jit(solution)/shard_map/ppermute | solution.py:19
  148.5 0.0 copy-done
  148.5 0.0 copy-done.3
  148.5 5.0 %shard_map.37 = (f32[4,256,256]{2,1,0:T(8,128)}, f32[16,2,256]{2,1,0:T(2,128)}) custom-call(s32[128]{0:T(128)} %reshape.264.pos_ref, s32[4,2]{1,0:T(4,128)} %copy.27.out_index_ref, bf16[6,256,256]{2,1,0:T(8,128)(2,1)} %copy-done, bf16[6,256,256]{2,1,0:T(8,128)(2,1)} %copy-done.3, bf16[6,256,256]{2,1,0:T(8,128)(2,1)} %copy-done.4, ...), custom_call_target="tpu_custom_call" | custom-call | tf_op jit(solution)/shard_map/pallas_call | solution.py:138
  153.5 11.9 %all-to-all-start.3 = ((f32[16,2,256]{2,1,0:T(2,128)}), f32[16,2,256]{2,1,0:T(2,128)S(1)}, u32[]{:S(2)}, u32[]{:S(2)}) async-start(f32[16,2,256]{2,1,0:T(2,128)} %get-tuple-element.22), calls=%async_computation.3 | async-start | bytes 65536 | tf_op jit(solution)/shard_map/all_to_all | solution.py:158
  165.5 5.8 %all-to-all-done.3 = f32[16,2,256]{2,1,0:T(2,128)S(1)} async-done(((f32[16,2,256]{2,1,0:T(2,128)}), f32[16,2,256]{2,1,0:T(2,128)S(1)}, u32[]{:S(2)}, u32[]{:S(2)}) %all-to-all-start.3) | async-done | bytes 32800 | tf_op jit(solution)/shard_map/all_to_all | solution.py:158
  171.3 0.1 select_select_fusion
  171.4 2.3 %divide_bitcast_fusion = f32[1,4,256,256]{3,2,1,0:T(8,128)} fusion(f32[4,256,256]{2,1,0:T(8,128)} %get-tuple-element.21, f32[4,256]{1,0:T(4,128)S(1)} %select_select_fusion), kind=kLoop, calls=%fused_computation | loop fusion | flops 524288 | bytes 2101248 | tf_op jit(solution)/shard_map/broadcast_in_dim | solution.py:163
  (18 shorter events, 0.1 us)
Async XLA Ops:
  6.5 61.4 %all-gather.6.cloned.1.call-start = ((), (), s32[]{:S(2)}) async-start(), calls=%async_computation.5 | async-start | bytes 4456448 | tf_op jit(solution)/shard_map/all_gather | solution.py:120
  7.3 141.2 %all-gather.4.cloned.1.call-start = ((), (), s32[]{:S(2)}) async-start(), calls=%async_computation.4 | async-start | bytes 2359296 | tf_op jit(solution)/shard_map/all_gather | solution.py:133
  7.3 17.3 %collective-permute-start = (bf16[2,256,256]{2,1,0:T(8,128)(2,1)}, bf16[2,256,256]{2,1,0:T(8,128)(2,1)S(1)}, u32[]{:S(2)}, u32[]{:S(2)}) collective-permute-start(bf16[2,256,256]{2,1,0:T(8,128)(2,1)} %bitcast.24), channel_id=1, source_target_pairs={{0,8},{8,16},{16,24},{24,0},{1,9},{9,17},{17,25},{25,1},{2,10},{10... | collective-permute-start | bytes 786440 | tf_op jit(solution)/shard_map/ppermute | solution.py:19
  13.9 18.1 %collective-permute-start.1 = (bf16[2,256,256]{2,1,0:T(8,128)(2,1)}, bf16[2,256,256]{2,1,0:T(8,128)(2,1)S(1)}, u32[]{:S(2)}, u32[]{:S(2)}) collective-permute-start(bf16[2,256,256]{2,1,0:T(8,128)(2,1)} %bitcast.25), channel_id=1, source_target_pairs={{0,24},{8,0},{16,8},{24,16},{1,25},{9,1},{17,9},{25,17},{2,26},{10... | collective-permute-start | bytes 786440 | tf_op jit(solution)/shard_map/ppermute | solution.py:19
  33.1 115.4 %copy-start = (bf16[6,256,256]{2,1,0:T(8,128)(2,1)}, bf16[6,256,256]{2,1,0:T(8,128)(2,1)S(1)}, u32[]{:S(2)}) copy-start(bf16[6,256,256]{2,1,0:T(8,128)(2,1)S(1)} %pad_maximum_fusion.refs_0_) | copy-start | bytes 2359300
  33.1 29.3 %collective-permute-start.2 = (bf16[6,256,256]{2,1,0:T(8,128)(2,1)S(1)}, bf16[6,256,256]{2,1,0:T(8,128)(2,1)S(1)}, u32[]{:S(2)}, u32[]{:S(2)}) collective-permute-start(bf16[6,256,256]{2,1,0:T(8,128)(2,1)S(1)} %pad_maximum_fusion.refs_0_), channel_id=1, source_target_pairs={{0,1},{1,2},{2,3},{3,4},{4,5},{5,6},{6,7},{7,0},{8,9},{9,10},{10,1... | collective-permute-start | bytes 2359304 | tf_op jit(solution)/shard_map/ppermute | solution.py:19
  36.3 26.0 %collective-permute-start.5 = (bf16[6,256,256]{2,1,0:T(8,128)(2,1)S(1)}, bf16[6,256,256]{2,1,0:T(8,128)(2,1)S(1)}, u32[]{:S(2)}, u32[]{:S(2)}) collective-permute-start(bf16[6,256,256]{2,1,0:T(8,128)(2,1)S(1)} %pad_maximum_fusion.refs_0_), channel_id=1, source_target_pairs={{0,7},{1,0},{2,1},{3,2},{4,3},{5,4},{6,5},{7,6},{8,15},{9,8},{10,9... | collective-permute-start | bytes 2359304 | tf_op jit(solution)/shard_map/ppermute | solution.py:19
  40.1 22.2 %collective-permute-start.10 = (bf16[2,256,256]{2,1,0:T(8,128)(2,1)S(1)}, bf16[2,256,256]{2,1,0:T(8,128)(2,1)S(1)}, u32[]{:S(2)}, u32[]{:S(2)}) collective-permute-start(bf16[2,256,256]{2,1,0:T(8,128)(2,1)S(1)} %collective-permute-done), channel_id=1, source_target_pairs={{0,8},{8,16},{16,24},{24,0},{1,9},{9,17},{17,25},{25,1},{2,10},{10... | collective-permute-start | bytes 786440 | tf_op jit(solution)/shard_map/ppermute | solution.py:19
  62.3 5.6 %copy-start.5 = (bf16[2,256,256]{2,1,0:T(8,128)(2,1)}, bf16[2,256,256]{2,1,0:T(8,128)(2,1)S(1)}, u32[]{:S(2)}) copy-start(bf16[2,256,256]{2,1,0:T(8,128)(2,1)S(1)} %collective-permute-done.10) | copy-start | bytes 786436
  62.3 86.1 %copy-start.3 = (bf16[6,256,256]{2,1,0:T(8,128)(2,1)}, bf16[6,256,256]{2,1,0:T(8,128)(2,1)S(1)}, u32[]{:S(2)}) copy-start(bf16[6,256,256]{2,1,0:T(8,128)(2,1)S(1)} %collective-permute-done.2.refs_1_) | copy-start | bytes 2359300
  62.4 57.7 %copy-start.4 = (bf16[6,256,256]{2,1,0:T(8,128)(2,1)}, bf16[6,256,256]{2,1,0:T(8,128)(2,1)S(1)}, u32[]{:S(2)}) copy-start(bf16[6,256,256]{2,1,0:T(8,128)(2,1)S(1)} %collective-permute-done.5.refs_2_) | copy-start | bytes 2359300
  69.3 13.6 %all-to-all-start = ((s32[4,1,4]{2,1,0:T(1,128)}), s32[4,1,4]{2,1,0:T(1,128)S(1)}, u32[]{:S(2)}, u32[]{:S(2)}) async-start(s32[4,1,4]{2,1,0:T(1,128)} %broadcast_in_dim.108), calls=%async_computation | async-start | bytes 4096 | tf_op jit(solution)/shard_map/all_to_all | solution.py:24
  75.6 40.1 %collective-permute-start.3 = (bf16[6,256,256]{2,1,0:T(8,128)(2,1)S(1)}, bf16[6,256,256]{2,1,0:T(8,128)(2,1)}, u32[]{:S(2)}, u32[]{:S(2)}) collective-permute-start(bf16[6,256,256]{2,1,0:T(8,128)(2,1)S(1)} %collective-permute-done.2.refs_1_), channel_id=1, source_target_pairs={{0,1},{1,2},{2,3},{3,4},{4,5},{5,6},{6,7},{7,0},{8,9},{9,10},{10,1... | collective-permute-start | bytes 2359304 | tf_op jit(solution)/shard_map/ppermute | solution.py:19
  78.0 42.0 %collective-permute-start.6 = (bf16[6,256,256]{2,1,0:T(8,128)(2,1)S(1)}, bf16[6,256,256]{2,1,0:T(8,128)(2,1)}, u32[]{:S(2)}, u32[]{:S(2)}) collective-permute-start(bf16[6,256,256]{2,1,0:T(8,128)(2,1)S(1)} %collective-permute-done.5.refs_2_), channel_id=1, source_target_pairs={{0,7},{1,0},{2,1},{3,2},{4,3},{5,4},{6,5},{7,6},{8,15},{9,8},{10,9... | collective-permute-start | bytes 2359304 | tf_op jit(solution)/shard_map/ppermute | solution.py:19
  83.5 11.3 %all-to-all-start.2 = ((s32[16,1,4]{2,1,0:T(1,128)}), s32[16,1,4]{2,1,0:T(1,128)S(1)}, u32[]{:S(2)}, u32[]{:S(2)}) async-start(s32[16,1,4]{2,1,0:T(1,128)} %broadcast_in_dim.111), calls=%async_computation.2 | async-start | bytes 16384 | tf_op jit(solution)/shard_map/all_to_all | solution.py:24
  95.4 20.2 %all-to-all-start.1 = ((s32[8,4,1,4]{3,1,2,0:T(4,128)}), s32[8,4,1,4]{3,1,2,0:T(4,128)S(1)}, u32[]{:S(2)}, u32[]{:S(2)}) async-start(s32[8,4,1,4]{3,1,2,0:T(4,128)} %broadcast_in_dim.110), calls=%async_computation.1 | async-start | bytes 32768 | tf_op jit(solution)/shard_map/all_to_all | solution.py:24
  115.7 19.9 %collective-permute-start.4 = (bf16[6,256,256]{2,1,0:T(8,128)(2,1)}, bf16[6,256,256]{2,1,0:T(8,128)(2,1)S(1)}, u32[]{:S(2)}, u32[]{:S(2)}) collective-permute-start(bf16[6,256,256]{2,1,0:T(8,128)(2,1)} %collective-permute-done.3.refs_3_), channel_id=1, source_target_pairs={{0,1},{1,2},{2,3},{3,4},{4,5},{5,6},{6,7},{7,0},{8,9},{9,10},{10,1... | collective-permute-start | bytes 2359304 | tf_op jit(solution)/shard_map/ppermute | solution.py:19
  120.0 16.1 %collective-permute-start.7 = (bf16[6,256,256]{2,1,0:T(8,128)(2,1)}, bf16[6,256,256]{2,1,0:T(8,128)(2,1)S(1)}, u32[]{:S(2)}, u32[]{:S(2)}) collective-permute-start(bf16[6,256,256]{2,1,0:T(8,128)(2,1)} %collective-permute-done.6.refs_4_), channel_id=1, source_target_pairs={{0,7},{1,0},{2,1},{3,2},{4,3},{5,4},{6,5},{7,6},{8,15},{9,8},{10,9... | collective-permute-start | bytes 2359304 | tf_op jit(solution)/shard_map/ppermute | solution.py:19
  135.6 12.9 %copy-start.1 = (bf16[6,256,256]{2,1,0:T(8,128)(2,1)}, bf16[6,256,256]{2,1,0:T(8,128)(2,1)S(1)}, u32[]{:S(2)}) copy-start(bf16[6,256,256]{2,1,0:T(8,128)(2,1)S(1)} %collective-permute-done.4.refs_5_) | copy-start | bytes 2359300
  136.2 12.3 %copy-start.2 = (bf16[6,256,256]{2,1,0:T(8,128)(2,1)}, bf16[6,256,256]{2,1,0:T(8,128)(2,1)S(1)}, u32[]{:S(2)}) copy-start(bf16[6,256,256]{2,1,0:T(8,128)(2,1)S(1)} %collective-permute-done.7.refs_6_) | copy-start | bytes 2359300
  136.2 9.8 %collective-permute-start.8 = (bf16[3,256,256]{2,1,0:T(8,128)(2,1)S(1)}, bf16[3,256,256]{2,1,0:T(8,128)(2,1)}, u32[]{:S(2)}, u32[]{:S(2)}) collective-permute-start(bf16[3,256,256]{2,1,0:T(8,128)(2,1)S(1)} %slice.42), channel_id=1, source_target_pairs={{0,1},{1,2},{2,3},{3,4},{4,5},{5,6},{6,7},{7,0},{8,9},{9,10},{10,1... | collective-permute-start | bytes 1179656 | tf_op jit(solution)/shard_map/ppermute | solution.py:19
  139.1 9.4 %collective-permute-start.9 = (bf16[3,256,256]{2,1,0:T(8,128)(2,1)}, bf16[3,256,256]{2,1,0:T(8,128)(2,1)}, u32[]{:S(2)}, u32[]{:S(2)}) collective-permute-start(bf16[3,256,256]{2,1,0:T(8,128)(2,1)} %slice.43), channel_id=1, source_target_pairs={{0,7},{1,0},{2,1},{3,2},{4,3},{5,4},{6,5},{7,6},{8,15},{9,8},{10,9... | collective-permute-start | bytes 1179656 | tf_op jit(solution)/shard_map/ppermute | solution.py:19
  144.8 20.7 %copy-start.6 = (s32[1,4,2]{1,2,0:T(2,128)S(1)}, s32[1,4,2]{1,2,0:T(2,128)}, u32[]{:S(2)}) copy-start(s32[1,4,2]{1,2,0:T(2,128)} %param.5) | copy-start | bytes 100
  153.5 17.7 %all-to-all-start.3 = ((f32[16,2,256]{2,1,0:T(2,128)}), f32[16,2,256]{2,1,0:T(2,128)S(1)}, u32[]{:S(2)}, u32[]{:S(2)}) async-start(f32[16,2,256]{2,1,0:T(2,128)} %get-tuple-element.22), calls=%async_computation.3 | async-start | bytes 65536 | tf_op jit(solution)/shard_map/all_to_all | solution.py:158
Sparse Core Ops, SparseCore 0:
  9.5 58.3 all-gather.5
  70.0 51.8 all-gather.3

commit v4 on v3

--- a/solution.py
+++ b/solution.py
@@ -11,7 +11,10 @@
 ROW = ("zl", "x", "core")
 COL = ("zh", "y")
 N_ROW, N_ZH, N_Y = 16, 4, 8
+SLOTS = 2
 RIGHTS = 32
+PAD = 8
+PACK = SLOTS * TILE + PAD
 BUFS = 8
 
 
@@ -19,9 +22,9 @@
     return lax.ppermute(value, axis, [(i, (i + by) % size) for i in range(size)])
 
 
-def to_all(value, axes, size):
-    every = jnp.broadcast_to(value[None], (size,) + value.shape)
-    return lax.all_to_all(every, axes, split_axis=0, concat_axis=0)
+def tile_rows(tile, packed):
+    start = tile // SLOTS * PACK + tile % SLOTS * TILE if packed else tile * TILE
+    return pl.ds(pl.multiple_of(start, PAD), TILE)
 
 
 def product_kernel(pos_ref, out_index_ref, *refs):
@@ -48,15 +51,18 @@
         code = todo[0, n]
         first = 0
         for ref in lefts:
-            count = ref.shape[0]
+            rows = ref.shape[0]
+            each = rows // PACK * SLOTS if rows % PACK == 0 else rows // TILE
 
-            @pl.when((code >= first) & (code < first + count))
-            def _(ref=ref, first=first):
-                pltpu.make_async_copy(ref.at[code - first], lbuf.at[slot], sem.at[0, slot]).start()
+            @pl.when((code >= first) & (code < first + each))
+            def _(ref=ref, first=first, rows=rows):
+                pltpu.make_async_copy(
+                    ref.at[tile_rows(code - first, rows % PACK == 0)], lbuf.at[slot], sem.at[0, slot]
+                ).start()
 
-            first += count
+            first += each
         pltpu.make_async_copy(
-            right.at[todo[1, n] % RIGHTS], rbuf.at[slot], sem.at[1, slot]
+            right.at[tile_rows(todo[1, n] % RIGHTS, True)], rbuf.at[slot], sem.at[1, slot]
         ).start()
 
     def prime(n, carry):
@@ -67,8 +73,8 @@
 
     def multiply(n, carry):
         slot = n % BUFS
-        pltpu.make_async_copy(right.at[0], lbuf.at[slot], sem.at[0, slot]).wait()
-        pltpu.make_async_copy(right.at[0], rbuf.at[slot], sem.at[1, slot]).wait()
+        pltpu.make_async_copy(right.at[pl.ds(0, TILE)], lbuf.at[slot], sem.at[0, slot]).wait()
+        pltpu.make_async_copy(right.at[pl.ds(0, TILE)], rbuf.at[slot], sem.at[1, slot]).wait()
         o = todo[1, n] // RIGHTS
         exp_ref[o] += jnp.dot(lbuf[slot], rbuf[slot], preferred_element_type=jnp.float32)
 
@@ -93,48 +99,58 @@
                 part_ref[:, j : j + 1, :] += jnp.sum(squared, axis=0, keepdims=True)[None]
 
 
-def match_table(in_index, out_index):
-    row = to_all(to_all(in_index.reshape(1, -1), "zh", N_ZH), "y", N_Y)
-    row = row.reshape(N_Y, N_ZH, -1, 2)
-    column = to_all(in_index.reshape(1, -1), ROW, N_ROW).reshape(-1, 2)
-    source = jnp.arange(N_Y, dtype=jnp.int32)[:, None, None]
-    hop = (jnp.arange(N_ZH, dtype=jnp.int32)[None, :, None] - lax.axis_index("zh")) % N_ZH
-    slot = jnp.arange(in_index.shape[0], dtype=jnp.int32)[None, None, :]
-    away = (source - lax.axis_index("y")) % N_Y
-    block = jnp.where(away == 4, 7, jnp.where(away < 4, 2 * away, 2 * (8 - away) - 1))
-    kind = jnp.where(hop == 0, 0, jnp.where(hop == 1, 4, 2))
-    place = jnp.where(hop == 2, 48 + 2 * source, 6 * block + kind) + slot
+def match_table(row_index, column_index, out_index):
     matches = (
-        (row[None, None, ..., 0] == out_index[:, 0][:, None, None, None, None])
-        & (row[None, None, ..., 1] == column[:, 0][None, :, None, None, None])
-        & (column[:, 1][None, :] == out_index[:, 1][:, None])[..., None, None, None]
-        & (out_index[:, 0] >= 0)[:, None, None, None, None]
+        (row_index[None, None, :, 0] == out_index[:, None, None, 0])
+        & (row_index[None, None, :, 1] == column_index[None, :, None, 0])
+        & (column_index[None, :, None, 1] == out_index[:, None, None, 1])
+        & (out_index[:, None, None, 0] >= 0)
     )
-    return jnp.max(jnp.where(matches, place, -1), axis=(2, 3, 4)).reshape(-1)
+    places = jnp.arange(row_index.shape[0], dtype=jnp.int32)
+    return jnp.max(jnp.where(matches, places, -1), axis=2).reshape(-1)
 
 
 def shards(tiles, in_index, out_index):
-    tiles, in_index, out_index = tiles[0], in_index[0], out_index[0]
+    out_index = out_index[0]
     out_count = out_index.shape[0]
+    bare = SLOTS * TILE
+    marks = jnp.pad(
+        in_index.reshape(1, -1).astype(tiles.dtype), ((0, PAD - 1), (0, TILE - 2 * SLOTS))
+    )
+    mine = jnp.concatenate([tiles.reshape(bare, TILE), marks])
 
-    right = lax.all_gather(tiles, ROW, axis=0, tiled=True)
-    pos = match_table(in_index, out_index)
+    right = lax.all_gather(mine, ROW, axis=0, tiled=True)
 
-    up = shift(tiles, "zh", N_ZH, 1)
-    down = shift(tiles, "zh", N_ZH, -1)
+    up = shift(mine, "zh", N_ZH, 1)
+    down = shift(mine, "zh", N_ZH, -1)
     up, down = lax.optimization_barrier((up, down))
     far = shift(up, "zh", N_ZH, 1)
-    ahead = back = jnp.concatenate([tiles, up, down])
+    packs = (mine, up, down)
+    signs = [pack[bare : bare + 1] for pack in packs]
+    signs.append(jnp.zeros((PAD - len(packs), TILE), tiles.dtype))
+    ahead = back = jnp.concatenate([pack[:bare] for pack in packs] + signs)
     ring = [ahead]
-    for _ in range(3):
+    for turn in range(3):
+        if turn == 2:
+            ahead, back, right = lax.optimization_barrier((ahead, back, right))
         ahead, back = shift(ahead, "y", N_Y, 1), shift(back, "y", N_Y, -1)
         ring += [ahead, back]
-    far, right, _ = lax.optimization_barrier((far, right, ring[1:3]))
+    far, _ = lax.optimization_barrier((far, ring[1:3]))
     far = lax.all_gather(far, "y", axis=0, tiled=True)
-    ahead, back, pos = lax.optimization_barrier((ahead, back, pos))
-    ring += [shift(ahead[:3], "y", N_Y, 1), shift(back[3:], "y", N_Y, -1)]
+    half = 3 * TILE
+    last = [shift(ahead[:half], "y", N_Y, 1), shift(back[half:], "y", N_Y, -1)]
+    far, last = lax.optimization_barrier((far, last))
 
-    lefts = ring + [far]
+    def signs_of(stack, first, count):
+        return stack[first : first + count, : 2 * SLOTS]
+
+    row_signs = [signs_of(block, 2 * half, 3) for block in ring] + [signs_of(last[1], half, 3)]
+    row_signs.append(signs_of(far.reshape(N_Y, PACK, TILE)[:, bare], 0, N_Y))
+    row_index = jnp.concatenate(row_signs).astype(jnp.int32).reshape(-1, 2)
+    column_index = signs_of(right.reshape(N_ROW, PACK, TILE)[:, bare], 0, N_ROW)
+    pos = match_table(row_index, column_index.astype(jnp.int32).reshape(-1, 2), out_index)
+
+    lefts = ring + last + [far]
     squared, parts = pl.pallas_call(
         product_kernel,
         grid_spec=pltpu.PrefetchScalarGridSpec(

time: 181 us -> 188 us (1.039)
  local copies, waits for them, and re-layouts: 6.94 us -> 33.1 us
  starting transfers between devices: 73.4 us -> 54.1 us
  other arithmetic: 5.27 us -> 12.6 us
  waiting for transfers between devices: 76.3 us -> 69.8 us
    all_to_all x3 -> x0, starting transfers between devices: 18.9 us -> none  [to_all(): return lax.all_to_all(every, axes, split_axis=0, concat_axis=0)]
    slice x4 -> x27, local copies, waits for them, and re-layouts: 0.98 us -> 19.2 us  [the longest x16 12.8 us: signs_of(): return stack[first:first + count, :2 * SLOTS]]
    ppermute x11, waiting for transfers between devices: 47.5 us -> 64.6 us  [shift(): lax.ppermute(value, axis, [(i, (i + by) % size) for i in range(size)])]
    all_to_all x3 -> x0, waiting for transfers between devices: 16.6 us -> none  [to_all(): return lax.all_to_all(every, axes, split_axis=0, concat_axis=0)]
    all_gather x1, waiting for transfers between devices: 5.58 us -> 0.01 us  [shards(): right = lax.all_gather(mine, ROW, axis=0, tiled=True)]
    unnamed x14 -> x18, local copies, waits for them, and re-layouts: 0.03 us -> 3.11 us
    convert_element_type x0 -> x3, local copies, waits for them, and re-layouts: none -> 2.85 us  [the longest x2 2.76 us: shards(): row_index = jnp.concatenate(row_signs).astype(jnp.int32).reshape(-1, 2)]
    broadcast_in_dim x4 -> x1, local copies, waits for them, and re-layouts: 2.55 us -> 0.01 us  [shards(): signs.append(jnp.zeros((PAD - len(packs), TILE), tiles.dtype))]
  transfers between devices with their start and end apart: 17 -> 14, of which waited for: 11 -> 7; matrix products, arithmetic and copies ran while one was open for 5% -> 12% of each run, Pallas kernels for 0% -> 0%
where the time goes in v4:
time: 188 us; the launch traced here: 187 us
  waiting for transfers between devices  69.8 us (37%)
  starting transfers between devices  54.1 us (29%)
  local copies, waits for them, and re-layouts  33.1 us (18%)
  between operations  13.6 us (7%)
  other arithmetic  12.6 us (7%)
  Pallas kernels  3.45 us (2%)
    ppermute x11, waiting for transfers between devices, shift(): lax.ppermute(value, axis, [(i, (i + by) % size) for i in range(size)])  64.6 us
    ppermute x11, starting transfers between devices, shift(): lax.ppermute(value, axis, [(i, (i + by) % size) for i in range(size)])  44.1 us
    slice x16, local copies, waits for them, and re-layouts, signs_of(): return stack[first:first + count, :2 * SLOTS]  12.8 us
    all_to_all x1, starting transfers between devices, shards(): lax.all_to_all(parts, ROW, split_axis=0, concat_axis=0)  10 us
    all_to_all x1, waiting for transfers between devices, shards(): lax.all_to_all(parts, ROW, split_axis=0, concat_axis=0)  5.1 us
  transfers between devices with their start and end apart: 14, of which 7 were waited for; matrix products, arithmetic and copies ran while one was open for 12% of the time, Pallas kernels for 0%

profile of v4, /device:TPU:1, one launch (start us, length us, event | category | flops | bytes accessed | tf_op | source)
XLA Modules:
  0.0 186.6 jit_solution(1867453053856048948)
XLA Ops:
  6.5 0.7 convert_element_type.24
  7.2 0.1 convert_element_type.25
  7.3 1.7 pad_maximum_fusion
  9.1 6.6 %collective-permute-start = (bf16[520,256]{1,0:T(8,128)(2,1)}, bf16[520,256]{1,0:T(8,128)(2,1)S(1)}, u32[]{:S(2)}, u32[]{:S(2)}) collective-permute-start(bf16[520,256]{1,0:T(8,128)(2,1)} %pad_maximum_fusion), channel_id=1, source_target_pairs={{0,8},{8,16},{16,24},{24,0},{1,9},{9,17},{17,25},{25,1},{2,10},{10... | collective-permute-start | bytes 798728 | tf_op jit(solution)/shard_map/ppermute | solution.py:22
  15.7 6.8 %collective-permute-start.1 = (bf16[520,256]{1,0:T(8,128)(2,1)}, bf16[520,256]{1,0:T(8,128)(2,1)S(1)}, u32[]{:S(2)}, u32[]{:S(2)}) collective-permute-start(bf16[520,256]{1,0:T(8,128)(2,1)} %pad_maximum_fusion), channel_id=1, source_target_pairs={{0,24},{8,0},{16,8},{24,16},{1,25},{9,1},{17,9},{25,17},{2,26},{10... | collective-permute-start | bytes 798728 | tf_op jit(solution)/shard_map/ppermute | solution.py:22
  22.5 4.0 %collective-permute-done = bf16[520,256]{1,0:T(8,128)(2,1)S(1)} collective-permute-done((bf16[520,256]{1,0:T(8,128)(2,1)}, bf16[520,256]{1,0:T(8,128)(2,1)S(1)}, u32[]{:S(2)}, u32[]{:S(2)}) %collective-permute-start) | collective-permute-done | bytes 266272 | tf_op jit(solution)/shard_map/ppermute | solution.py:22
  26.5 7.4 %collective-permute-done.1 = bf16[520,256]{1,0:T(8,128)(2,1)S(1)} collective-permute-done((bf16[520,256]{1,0:T(8,128)(2,1)}, bf16[520,256]{1,0:T(8,128)(2,1)S(1)}, u32[]{:S(2)}, u32[]{:S(2)}) %collective-permute-start.1) | collective-permute-done | bytes 266272 | tf_op jit(solution)/shard_map/ppermute | solution.py:22
  34.0 1.2 concatenate.14.refs_0_
  35.2 3.2 %collective-permute-start.2 = (bf16[1544,256]{1,0:T(8,128)(2,1)S(1)}, bf16[1544,256]{1,0:T(8,128)(2,1)S(1)}, u32[]{:S(2)}, u32[]{:S(2)}) collective-permute-start(bf16[1544,256]{1,0:T(8,128)(2,1)S(1)} %concatenate.14.refs_0_), channel_id=1, source_target_pairs={{0,1},{1,2},{2,3},{3,4},{4,5},{5,6},{6,7},{7,0},{8,9},{9,10},{10,1... | collective-permute-start | bytes 2371592 | tf_op jit(solution)/shard_map/ppermute | solution.py:22
  38.4 3.8 %collective-permute-start.3 = (bf16[1544,256]{1,0:T(8,128)(2,1)S(1)}, bf16[1544,256]{1,0:T(8,128)(2,1)S(1)}, u32[]{:S(2)}, u32[]{:S(2)}) collective-permute-start(bf16[1544,256]{1,0:T(8,128)(2,1)S(1)} %concatenate.14.refs_0_), channel_id=1, source_target_pairs={{0,7},{1,0},{2,1},{3,2},{4,3},{5,4},{6,5},{7,6},{8,15},{9,8},{10,9... | collective-permute-start | bytes 2371592 | tf_op jit(solution)/shard_map/ppermute | solution.py:22
  42.2 2.7 %collective-permute-start.8 = (bf16[520,256]{1,0:T(8,128)(2,1)S(1)}, bf16[520,256]{1,0:T(8,128)(2,1)S(1)}, u32[]{:S(2)}, u32[]{:S(2)}) collective-permute-start(bf16[520,256]{1,0:T(8,128)(2,1)S(1)} %collective-permute-done), channel_id=1, source_target_pairs={{0,8},{8,16},{16,24},{24,0},{1,9},{9,17},{17,25},{25,1},{2,10},{10... | collective-permute-start | bytes 798728 | tf_op jit(solution)/shard_map/ppermute | solution.py:22
  44.9 20.4 %collective-permute-done.8 = bf16[520,256]{1,0:T(8,128)(2,1)S(1)} collective-permute-done((bf16[520,256]{1,0:T(8,128)(2,1)S(1)}, bf16[520,256]{1,0:T(8,128)(2,1)S(1)}, u32[]{:S(2)}, u32[]{:S(2)}) %collective-permute-start.8) | collective-permute-done | bytes 266272 | tf_op jit(solution)/shard_map/ppermute | solution.py:22
  65.4 0.7 copy-done.7
  66.1 1.9 %collective-permute-start.4 = (bf16[1544,256]{1,0:T(8,128)(2,1)S(1)}, bf16[1544,256]{1,0:T(8,128)(2,1)S(1)}, u32[]{:S(2)}, u32[]{:S(2)}) collective-permute-start(bf16[1544,256]{1,0:T(8,128)(2,1)S(1)} %collective-permute-done.2.refs_1_), channel_id=1, source_target_pairs={{0,1},{1,2},{2,3},{3,4},{4,5},{5,6},{6,7},{7,0},{8,9},{9,10},{10,1... | collective-permute-start | bytes 2371592 | tf_op jit(solution)/shard_map/ppermute | solution.py:22
  68.0 4.6 %collective-permute-start.5 = (bf16[1544,256]{1,0:T(8,128)(2,1)S(1)}, bf16[1544,256]{1,0:T(8,128)(2,1)}, u32[]{:S(2)}, u32[]{:S(2)}) collective-permute-start(bf16[1544,256]{1,0:T(8,128)(2,1)S(1)} %collective-permute-done.3.refs_2_), channel_id=1, source_target_pairs={{0,7},{1,0},{2,1},{3,2},{4,3},{5,4},{6,5},{7,6},{8,15},{9,8},{10,9... | collective-permute-start | bytes 2371592 | tf_op jit(solution)/shard_map/ppermute | solution.py:22
  72.6 13.4 %collective-permute-done.4.refs_3_ = bf16[1544,256]{1,0:T(8,128)(2,1)S(1)} collective-permute-done((bf16[1544,256]{1,0:T(8,128)(2,1)S(1)}, bf16[1544,256]{1,0:T(8,128)(2,1)S(1)}, u32[]{:S(2)}, u32[]{:S(2)}) %collective-permute-start.4) | collective-permute-done | bytes 790560 | tf_op jit(solution)/shard_map/ppermute | solution.py:22
  86.1 0.9 copy-done.5
  87.0 1.2 collective-permute-done.5.refs_4_
  88.2 5.4 %collective-permute-start.7 = (bf16[1544,256]{1,0:T(8,128)(2,1)}, bf16[1544,256]{1,0:T(8,128)(2,1)S(1)}, u32[]{:S(2)}, u32[]{:S(2)}) collective-permute-start(bf16[1544,256]{1,0:T(8,128)(2,1)} %collective-permute-done.5.refs_4_), channel_id=1, source_target_pairs={{0,7},{1,0},{2,1},{3,2},{4,3},{5,4},{6,5},{7,6},{8,15},{9,8},{10,9... | collective-permute-start | bytes 2371592 | tf_op jit(solution)/shard_map/ppermute | solution.py:22
  93.6 1.9 %collective-permute-start.6 = (bf16[1544,256]{1,0:T(8,128)(2,1)}, bf16[1544,256]{1,0:T(8,128)(2,1)S(1)}, u32[]{:S(2)}, u32[]{:S(2)}) collective-permute-start(bf16[1544,256]{1,0:T(8,128)(2,1)} %copy-done.5), channel_id=1, source_target_pairs={{0,1},{1,2},{2,3},{3,4},{4,5},{5,6},{6,7},{7,0},{8,9},{9,10},{10,1... | collective-permute-start | bytes 2371592 | tf_op jit(solution)/shard_map/ppermute | solution.py:22
  95.5 1.4 copy.33.out_index_ref
  96.9 1.3 broadcast_compare_fusion.3
  98.2 1.3 slice_bitcast_fusion.1
  99.4 0.7 copy.23
  100.1 0.7 copy.24
  100.8 0.7 slice.116
  101.5 0.7 copy.25
  102.1 0.7 slice.117
  102.8 0.7 copy.26
  103.5 0.6 slice.118
  104.1 0.6 copy.27
  104.8 0.9 slice.127
  105.6 18.2 %collective-permute-done.7.refs_6_ = bf16[1544,256]{1,0:T(8,128)(2,1)S(1)} collective-permute-done((bf16[1544,256]{1,0:T(8,128)(2,1)}, bf16[1544,256]{1,0:T(8,128)(2,1)S(1)}, u32[]{:S(2)}, u32[]{:S(2)}) %collective-permute-start.7) | collective-permute-done | bytes 790560 | tf_op jit(solution)/shard_map/ppermute | solution.py:22
  123.8 0.8 slice.122
  124.6 5.2 %collective-permute-start.10 = (bf16[776,256]{1,0:T(8,128)(2,1)}, bf16[776,256]{1,0:T(8,128)(2,1)}, u32[]{:S(2)}, u32[]{:S(2)}) collective-permute-start(bf16[776,256]{1,0:T(8,128)(2,1)} %slice.122), channel_id=1, source_target_pairs={{0,7},{1,0},{2,1},{3,2},{4,3},{5,4},{6,5},{7,6},{8,15},{9,8},{10,9... | collective-permute-start | bytes 1191944 | tf_op jit(solution)/shard_map/ppermute | solution.py:22
  129.8 0.9 slice.121
  130.7 1.9 %collective-permute-start.9 = (bf16[768,256]{1,0:T(8,128)(2,1)}, bf16[768,256]{1,0:T(8,128)(2,1)S(1)}, u32[]{:S(2)}, u32[]{:S(2)}) collective-permute-start(bf16[768,256]{1,0:T(8,128)(2,1)} %slice.121), channel_id=1, source_target_pairs={{0,1},{1,2},{2,3},{3,4},{4,5},{5,6},{6,7},{7,0},{8,9},{9,10},{10,1... | collective-permute-start | bytes 1179656 | tf_op jit(solution)/shard_map/ppermute | solution.py:22
  132.6 0.6 slice_convert_fusion
  133.2 1.4 reshape.208
  134.6 1.5 slice_reduce_fusion.3
  136.0 1.2 broadcast_compare_fusion.1
  137.2 0.6 slice.119
  137.8 1.3 copy.28
  139.1 0.5 slice.120
  139.7 1.3 copy.29
  141.0 1.4 slice.123
  142.4 1.4 copy.34
  143.8 1.2 slice.124
  145.0 1.2 slice.101
  146.2 1.3 copy.30
  147.6 1.3 concatenate.15
  148.9 1.2 convert_element_type.28
  150.1 1.4 copy.31
  151.5 1.4 reshape.206
  152.9 1.0 slice_reduce_fusion.1
  153.9 0.7 broadcast_compare_fusion
  154.5 0.7 broadcast_compare_fusion.2
  155.2 1.5 select_reduce_fusion
  156.7 1.3 reshape.205.pos_ref
  158.0 3.5 %shard_map.37 = (f32[4,256,256]{2,1,0:T(8,128)}, f32[16,2,256]{2,1,0:T(2,128)}) custom-call(s32[128]{0:T(128)} %reshape.205.pos_ref, s32[4,2]{1,0:T(4,128)} %copy.33.out_index_ref, bf16[1544,256]{1,0:T(8,128)(2,1)} %copy-done, bf16[1544,256]{1,0:T(8,128)(2,1)} %copy-done.3, bf16[1544,256]{1,0:T(8,128)(2,1)} %copy-done.4, bf16[1544,256]{1,0:T(8,128)(2,1)} %copy-done.5, ...), custom_call_target="tpu_custom_call" | custom-call | tf_op jit(solution)/shard_map/pallas_call | solution.py:154
  161.5 10.0 %all-to-all-start = ((f32[16,2,256]{2,1,0:T(2,128)}), f32[16,2,256]{2,1,0:T(2,128)S(1)}, u32[]{:S(2)}, u32[]{:S(2)}) async-start(f32[16,2,256]{2,1,0:T(2,128)} %get-tuple-element.26), calls=%async_computation | async-start | bytes 65536 | tf_op jit(solution)/shard_map/all_to_all | solution.py:174
  171.5 0.8 compare_bitcast_fusion.1
  172.3 5.1 %all-to-all-done = f32[16,2,256]{2,1,0:T(2,128)S(1)} async-done(((f32[16,2,256]{2,1,0:T(2,128)}), f32[16,2,256]{2,1,0:T(2,128)S(1)}, u32[]{:S(2)}, u32[]{:S(2)}) %all-to-all-start) | async-done | bytes 32800 | tf_op jit(solution)/shard_map/all_to_all | solution.py:174
  177.5 2.3 %divide_bitcast_fusion = f32[1,4,256,256]{3,2,1,0:T(8,128)} fusion(f32[4,256,256]{2,1,0:T(8,128)} %get-tuple-element.25, f32[4,256]{1,0:T(4,128)S(1)} %select_select_fusion), kind=kLoop, calls=%fused_computation | loop fusion | flops 524288 | bytes 2101248 | tf_op jit(solution)/shard_map/broadcast_in_dim | solution.py:179
  (38 shorter events, 0.3 us)
Async XLA Ops:
  6.5 81.7 %all-gather.3.cloned.1.call-start = ((), (), s32[]{:S(2)}) async-start(), calls=%async_computation.1 | async-start | bytes 4526080 | tf_op jit(solution)/shard_map/all_gather | solution.py:122
  9.0 132.0 %all-gather.5.cloned.1.call-start = ((), (), s32[]{:S(2)}) async-start(), calls=%async_computation.2 | async-start | bytes 2396160 | tf_op jit(solution)/shard_map/all_gather | solution.py:139
  9.1 17.4 %collective-permute-start = (bf16[520,256]{1,0:T(8,128)(2,1)}, bf16[520,256]{1,0:T(8,128)(2,1)S(1)}, u32[]{:S(2)}, u32[]{:S(2)}) collective-permute-start(bf16[520,256]{1,0:T(8,128)(2,1)} %pad_maximum_fusion), channel_id=1, source_target_pairs={{0,8},{8,16},{16,24},{24,0},{1,9},{9,17},{17,25},{25,1},{2,10},{10... | collective-permute-start | bytes 798728 | tf_op jit(solution)/shard_map/ppermute | solution.py:22
  15.7 18.2 %collective-permute-start.1 = (bf16[520,256]{1,0:T(8,128)(2,1)}, bf16[520,256]{1,0:T(8,128)(2,1)S(1)}, u32[]{:S(2)}, u32[]{:S(2)}) collective-permute-start(bf16[520,256]{1,0:T(8,128)(2,1)} %pad_maximum_fusion), channel_id=1, source_target_pairs={{0,24},{8,0},{16,8},{24,16},{1,25},{9,1},{17,9},{25,17},{2,26},{10... | collective-permute-start | bytes 798728 | tf_op jit(solution)/shard_map/ppermute | solution.py:22
  35.2 122.8 %copy-start = (bf16[1544,256]{1,0:T(8,128)(2,1)}, bf16[1544,256]{1,0:T(8,128)(2,1)S(1)}, u32[]{:S(2)}) copy-start(bf16[1544,256]{1,0:T(8,128)(2,1)S(1)} %concatenate.14.refs_0_) | copy-start | bytes 2371588
  35.2 30.2 %collective-permute-start.2 = (bf16[1544,256]{1,0:T(8,128)(2,1)S(1)}, bf16[1544,256]{1,0:T(8,128)(2,1)S(1)}, u32[]{:S(2)}, u32[]{:S(2)}) collective-permute-start(bf16[1544,256]{1,0:T(8,128)(2,1)S(1)} %concatenate.14.refs_0_), channel_id=1, source_target_pairs={{0,1},{1,2},{2,3},{3,4},{4,5},{5,6},{6,7},{7,0},{8,9},{9,10},{10,1... | collective-permute-start | bytes 2371592 | tf_op jit(solution)/shard_map/ppermute | solution.py:22
  38.4 27.0 %collective-permute-start.3 = (bf16[1544,256]{1,0:T(8,128)(2,1)S(1)}, bf16[1544,256]{1,0:T(8,128)(2,1)S(1)}, u32[]{:S(2)}, u32[]{:S(2)}) collective-permute-start(bf16[1544,256]{1,0:T(8,128)(2,1)S(1)} %concatenate.14.refs_0_), channel_id=1, source_target_pairs={{0,7},{1,0},{2,1},{3,2},{4,3},{5,4},{6,5},{7,6},{8,15},{9,8},{10,9... | collective-permute-start | bytes 2371592 | tf_op jit(solution)/shard_map/ppermute | solution.py:22
  42.2 23.2 %collective-permute-start.8 = (bf16[520,256]{1,0:T(8,128)(2,1)S(1)}, bf16[520,256]{1,0:T(8,128)(2,1)S(1)}, u32[]{:S(2)}, u32[]{:S(2)}) collective-permute-start(bf16[520,256]{1,0:T(8,128)(2,1)S(1)} %collective-permute-done), channel_id=1, source_target_pairs={{0,8},{8,16},{16,24},{24,0},{1,9},{9,17},{17,25},{25,1},{2,10},{10... | collective-permute-start | bytes 798728 | tf_op jit(solution)/shard_map/ppermute | solution.py:22
  65.4 0.7 copy-start.7
  65.4 92.6 %copy-start.3 = (bf16[1544,256]{1,0:T(8,128)(2,1)}, bf16[1544,256]{1,0:T(8,128)(2,1)S(1)}, u32[]{:S(2)}) copy-start(bf16[1544,256]{1,0:T(8,128)(2,1)S(1)} %collective-permute-done.2.refs_1_) | copy-start | bytes 2371588
  65.4 22.8 %copy-start.4 = (bf16[1544,256]{1,0:T(8,128)(2,1)}, bf16[1544,256]{1,0:T(8,128)(2,1)S(1)}, u32[]{:S(2)}) copy-start(bf16[1544,256]{1,0:T(8,128)(2,1)S(1)} %collective-permute-done.3.refs_2_) | copy-start | bytes 2371588
  66.1 20.0 %collective-permute-start.4 = (bf16[1544,256]{1,0:T(8,128)(2,1)S(1)}, bf16[1544,256]{1,0:T(8,128)(2,1)S(1)}, u32[]{:S(2)}, u32[]{:S(2)}) collective-permute-start(bf16[1544,256]{1,0:T(8,128)(2,1)S(1)} %collective-permute-done.2.refs_1_), channel_id=1, source_target_pairs={{0,1},{1,2},{2,3},{3,4},{4,5},{5,6},{6,7},{7,0},{8,9},{9,10},{10,1... | collective-permute-start | bytes 2371592 | tf_op jit(solution)/shard_map/ppermute | solution.py:22
  68.0 20.2 %collective-permute-start.5 = (bf16[1544,256]{1,0:T(8,128)(2,1)S(1)}, bf16[1544,256]{1,0:T(8,128)(2,1)}, u32[]{:S(2)}, u32[]{:S(2)}) collective-permute-start(bf16[1544,256]{1,0:T(8,128)(2,1)S(1)} %collective-permute-done.3.refs_2_), channel_id=1, source_target_pairs={{0,7},{1,0},{2,1},{3,2},{4,3},{5,4},{6,5},{7,6},{8,15},{9,8},{10,9... | collective-permute-start | bytes 2371592 | tf_op jit(solution)/shard_map/ppermute | solution.py:22
  86.1 1.0 copy-start.5
  88.2 35.6 %collective-permute-start.7 = (bf16[1544,256]{1,0:T(8,128)(2,1)}, bf16[1544,256]{1,0:T(8,128)(2,1)S(1)}, u32[]{:S(2)}, u32[]{:S(2)}) collective-permute-start(bf16[1544,256]{1,0:T(8,128)(2,1)} %collective-permute-done.5.refs_4_), channel_id=1, source_target_pairs={{0,7},{1,0},{2,1},{3,2},{4,3},{5,4},{6,5},{7,6},{8,15},{9,8},{10,9... | collective-permute-start | bytes 2371592 | tf_op jit(solution)/shard_map/ppermute | solution.py:22
  93.6 36.2 %collective-permute-start.6 = (bf16[1544,256]{1,0:T(8,128)(2,1)}, bf16[1544,256]{1,0:T(8,128)(2,1)S(1)}, u32[]{:S(2)}, u32[]{:S(2)}) collective-permute-start(bf16[1544,256]{1,0:T(8,128)(2,1)} %copy-done.5), channel_id=1, source_target_pairs={{0,1},{1,2},{2,3},{3,4},{4,5},{5,6},{6,7},{7,0},{8,9},{9,10},{10,1... | collective-permute-start | bytes 2371592 | tf_op jit(solution)/shard_map/ppermute | solution.py:22
  123.8 34.2 %copy-start.1 = (bf16[1544,256]{1,0:T(8,128)(2,1)}, bf16[1544,256]{1,0:T(8,128)(2,1)S(1)}, u32[]{:S(2)}) copy-start(bf16[1544,256]{1,0:T(8,128)(2,1)S(1)} %collective-permute-done.7.refs_6_) | copy-start | bytes 2371588
  124.6 16.4 %collective-permute-start.10 = (bf16[776,256]{1,0:T(8,128)(2,1)}, bf16[776,256]{1,0:T(8,128)(2,1)}, u32[]{:S(2)}, u32[]{:S(2)}) collective-permute-start(bf16[776,256]{1,0:T(8,128)(2,1)} %slice.122), channel_id=1, source_target_pairs={{0,7},{1,0},{2,1},{3,2},{4,3},{5,4},{6,5},{7,6},{8,15},{9,8},{10,9... | collective-permute-start | bytes 1191944 | tf_op jit(solution)/shard_map/ppermute | solution.py:22
  129.8 28.2 %copy-start.2 = (bf16[1544,256]{1,0:T(8,128)(2,1)}, bf16[1544,256]{1,0:T(8,128)(2,1)S(1)}, u32[]{:S(2)}) copy-start(bf16[1544,256]{1,0:T(8,128)(2,1)S(1)} %collective-permute-done.6.refs_5_) | copy-start | bytes 2371588
  130.7 10.3 %collective-permute-start.9 = (bf16[768,256]{1,0:T(8,128)(2,1)}, bf16[768,256]{1,0:T(8,128)(2,1)S(1)}, u32[]{:S(2)}, u32[]{:S(2)}) collective-permute-start(bf16[768,256]{1,0:T(8,128)(2,1)} %slice.121), channel_id=1, source_target_pairs={{0,1},{1,2},{2,3},{3,4},{4,5},{5,6},{6,7},{7,0},{8,9},{9,10},{10,1... | collective-permute-start | bytes 1179656 | tf_op jit(solution)/shard_map/ppermute | solution.py:22
  141.0 17.1 %copy-start.6 = (bf16[768,256]{1,0:T(8,128)(2,1)}, bf16[768,256]{1,0:T(8,128)(2,1)S(1)}, u32[]{:S(2)}) copy-start(bf16[768,256]{1,0:T(8,128)(2,1)S(1)} %collective-permute-done.9.refs_7_) | copy-start | bytes 1179652
  161.5 15.9 %all-to-all-start = ((f32[16,2,256]{2,1,0:T(2,128)}), f32[16,2,256]{2,1,0:T(2,128)S(1)}, u32[]{:S(2)}, u32[]{:S(2)}) async-start(f32[16,2,256]{2,1,0:T(2,128)} %get-tuple-element.26), calls=%async_computation | async-start | bytes 65536 | tf_op jit(solution)/shard_map/all_to_all | solution.py:174
Sparse Core Ops, SparseCore 0:
  9.5 59.8 all-gather.2
  71.4 51.5 all-gather.4

commit v5 on v0

--- a/solution.py
+++ b/solution.py
@@ -86,7 +86,7 @@
 
             @pl.when((column >= 0) & (column % COL_BLOCKS == j))
             def _():
-                part_ref[j : j + 1, :] += jnp.sum(squared, axis=0, keepdims=True)
+                part_ref[:, j : j + 1, :] += jnp.sum(squared, axis=0, keepdims=True)[None]
 
 
 def shards(tiles, in_index, out_index):
@@ -98,21 +98,26 @@
     )
     mine = jnp.concatenate([tiles[0], marks], axis=1)
 
-    pair = jnp.concatenate([mine, shift(mine, "zl", 2, 1)])
-
     own = lax.all_gather(mine, "y", axis=0, tiled=False)
-    right = lax.all_gather(pair, ("x", "core"), axis=0, tiled=True)
     up = shift(mine[0], "zh", 4, 1)
     down = shift(mine[1], "zh", 4, -1)
+    other = shift(mine, "zl", 2, 1)
+    up, down, other = lax.optimization_barrier((up, down, other))
     early = jnp.stack([up, down, shift(up, "zh", 4, 1), shift(down, "zh", 4, -1)])
+    other, _ = lax.optimization_barrier((other, early))
+    right = lax.all_gather(jnp.concatenate([mine, other]), ("x", "core"), axis=0, tiled=True)
     ring = [early]
     ahead = back = early
-    for _ in range(3):
+    for turn in range(3):
+        if turn == 1:
+            first, second, ahead, back = lax.optimization_barrier(
+                (own[:, 0], own[:, 1], ahead, back)
+            )
+            late_up = shift(second, "zh", 4, 1)
+            late_down = shift(first, "zh", 4, -1)
         ahead, back = shift(ahead, "y", 8, 1), shift(back, "y", 8, -1)
         ring += [ahead, back]
     ring += [shift(ahead[:2], "y", 8, 1), shift(back[2:], "y", 8, -1)]
-    late_up = shift(own[:, 1], "zh", 4, 1)
-    late_down = shift(own[:, 0], "zh", 4, -1)
     lefts = [own.reshape(-1, TILE + PAD, TILE)] + ring + [late_up, late_down]
 
     def index_of(stack):
@@ -129,7 +134,7 @@
     places = jnp.arange(left_index.shape[0], dtype=jnp.int32)
     pos = jnp.max(jnp.where(matches, places, -1), axis=2).reshape(-1)
 
-    squared, part = pl.pallas_call(
+    squared, parts = pl.pallas_call(
         product_kernel,
         grid_spec=pltpu.PrefetchScalarGridSpec(
             num_scalar_prefetch=2,
@@ -145,11 +150,11 @@
         ),
         out_shape=[
             jax.ShapeDtypeStruct((out_count, TILE, TILE), jnp.float32),
-            jax.ShapeDtypeStruct((COL_BLOCKS, TILE), jnp.float32),
+            jax.ShapeDtypeStruct((16, COL_BLOCKS, TILE), jnp.float32),
         ],
     )(pos, out_index, *lefts, right)
 
-    totals = jnp.sum(lax.all_gather(part, ROW, axis=0, tiled=False), axis=0)
+    totals = jnp.sum(lax.all_to_all(parts, ROW, split_axis=0, concat_axis=0), axis=0)
     out_used = out_index[:, 0] >= 0
     second = (out_index[:, 1] % COL_BLOCKS == 1)[:, None]
     divisor = jnp.where(second, totals[1][None], totals[0][None])

time: 172 us -> 160 us (0.930)
  blocking collectives: 28.3 us -> 0 us
  waiting for transfers between devices: 40.6 us -> 56.7 us
    all_gather x1 -> x0, blocking collectives: 28.3 us -> none  [shards(): totals = jnp.sum(lax.all_gather(part, ROW, axis=0, tiled=False), axis=0)]
    ppermute x15, waiting for transfers between devices: 40.5 us -> 50.4 us  [shift(): lax.ppermute(value, axis, [(i, (i + by) % size) for i in range(size)])]
    all_to_all x0 -> x1, waiting for transfers between devices: none -> 5.79 us  [shards(): lax.all_to_all(parts, ROW, split_axis=0, concat_axis=0)]
    all_to_all x0 -> x1, starting transfers between devices: none -> 5.04 us  [shards(): lax.all_to_all(parts, ROW, split_axis=0, concat_axis=0)]
    ppermute x15, starting transfers between devices: 61.8 us -> 57.8 us  [shift(): lax.ppermute(value, axis, [(i, (i + by) % size) for i in range(size)])]
  transfers between devices with their start and end apart: 17 -> 18, of which waited for: 7 -> 11; matrix products, arithmetic and copies ran while one was open for 8% -> 8% of each run, Pallas kernels for 0% -> 0%
where the time goes in v5:
time: 160 us; the launch traced here: 159 us
  starting transfers between devices  62.8 us (39%)
  waiting for transfers between devices  56.7 us (35%)
  between operations  13.7 us (9%)
  local copies, waits for them, and re-layouts  12.6 us (8%)
  other arithmetic  7.22 us (5%)
  Pallas kernels  5.49 us (3%)
    ppermute x15, starting transfers between devices, shift(): lax.ppermute(value, axis, [(i, (i + by) % size) for i in range(size)])  57.8 us
    ppermute x15, waiting for transfers between devices, shift(): lax.ppermute(value, axis, [(i, (i + by) % size) for i in range(size)])  50.4 us
    slice x23, local copies, waits for them, and re-layouts, index_of(): return stack[:, TILE, :2].astype(jnp.int32)  6.21 us
    all_to_all x1, waiting for transfers between devices, shards(): lax.all_to_all(parts, ROW, split_axis=0, concat_axis=0)  5.79 us
    pallas_call x1, Pallas kernels, shards(): pl.pallas_call(product_kernel, grid_spec=pltpu.PrefetchScalarGridSpec(num...  5.49 us
    all_to_all x1, starting transfers between devices, shards(): lax.all_to_all(parts, ROW, split_axis=0, concat_axis=0)  5.04 us
  transfers between devices with their start and end apart: 18, of which 11 were waited for; matrix products, arithmetic and copies ran while one was open for 8% of the time, Pallas kernels for 0%

profile of v5, /device:TPU:1, one launch (start us, length us, event | category | flops | bytes accessed | tf_op | source)
XLA Modules:
  0.0 158.5 jit_solution(15119900726568950069)
XLA Ops:
  6.5 0.7 convert_bitcast_fusion
  7.2 1.7 %pad_maximum_fusion.2 = bf16[2,264,256]{2,1,0:T(8,128)(2,1)} fusion(bf16[2,8,256]{2,1,0:T(8,128)(2,1)S(1)} %pad.4, bf16[2,256,256]{2,1,0:T(8,128)(2,1)} %bitcast.59), kind=kLoop, calls=%fused_computation.7 | loop fusion | flops 540672 | bytes 540672 | tf_op jit(solution)/shard_map/concatenate | solution.py:99
  9.0 4.8 %collective-permute-start.2 = (bf16[2,264,256]{2,1,0:T(8,128)(2,1)}, bf16[2,264,256]{2,1,0:T(8,128)(2,1)S(1)}, u32[]{:S(2)}, u32[]{:S(2)}) collective-permute-start(bf16[2,264,256]{2,1,0:T(8,128)(2,1)} %pad_maximum_fusion.2), channel_id=1, source_target_pairs={{0,256},{256,0},{1,257},{257,1},{2,258},{258,2},{3,259},{259,3},{4... | collective-permute-start | bytes 811016 | tf_op jit(solution)/shard_map/ppermute | solution.py:18
  13.8 1.0 fusion.3
  14.8 5.8 %collective-permute-start = (bf16[264,256]{1,0:T(8,128)(2,1)S(1)}, bf16[264,256]{1,0:T(8,128)(2,1)S(1)}, u32[]{:S(2)}, u32[]{:S(2)}) collective-permute-start(bf16[264,256]{1,0:T(8,128)(2,1)S(1)} %get-tuple-element.28), channel_id=1, source_target_pairs={{0,8},{8,16},{16,24},{24,0},{1,9},{9,17},{17,25},{25,1},{2,10},{10... | collective-permute-start | bytes 405512 | tf_op jit(solution)/shard_map/ppermute | solution.py:18
  20.6 5.9 %collective-permute-start.1 = (bf16[264,256]{1,0:T(8,128)(2,1)S(1)}, bf16[264,256]{1,0:T(8,128)(2,1)S(1)}, u32[]{:S(2)}, u32[]{:S(2)}) collective-permute-start(bf16[264,256]{1,0:T(8,128)(2,1)S(1)} %get-tuple-element.27), channel_id=1, source_target_pairs={{0,24},{8,0},{16,8},{24,16},{1,25},{9,1},{17,9},{25,17},{2,26},{10... | collective-permute-start | bytes 405512 | tf_op jit(solution)/shard_map/ppermute | solution.py:18
  26.5 7.0 %collective-permute-done = bf16[264,256]{1,0:T(8,128)(2,1)S(1)} collective-permute-done((bf16[264,256]{1,0:T(8,128)(2,1)S(1)}, bf16[264,256]{1,0:T(8,128)(2,1)S(1)}, u32[]{:S(2)}, u32[]{:S(2)}) %collective-permute-start) | collective-permute-done | bytes 135200 | tf_op jit(solution)/shard_map/ppermute | solution.py:18
  33.5 0.3 collective-permute-done.1
  33.8 5.2 %collective-permute-start.3 = (bf16[264,256]{1,0:T(8,128)(2,1)S(1)}, bf16[264,256]{1,0:T(8,128)(2,1)S(1)}, u32[]{:S(2)}, u32[]{:S(2)}) collective-permute-start(bf16[264,256]{1,0:T(8,128)(2,1)S(1)} %collective-permute-done), channel_id=1, source_target_pairs={{0,8},{8,16},{16,24},{24,0},{1,9},{9,17},{17,25},{25,1},{2,10},{10... | collective-permute-start | bytes 405512 | tf_op jit(solution)/shard_map/ppermute | solution.py:18
  39.0 2.2 %collective-permute-start.4 = (bf16[264,256]{1,0:T(8,128)(2,1)S(1)}, bf16[264,256]{1,0:T(8,128)(2,1)S(1)}, u32[]{:S(2)}, u32[]{:S(2)}) collective-permute-start(bf16[264,256]{1,0:T(8,128)(2,1)S(1)} %collective-permute-done.1), channel_id=1, source_target_pairs={{0,24},{8,0},{16,8},{24,16},{1,25},{9,1},{17,9},{25,17},{2,26},{10... | collective-permute-start | bytes 405512 | tf_op jit(solution)/shard_map/ppermute | solution.py:18
  41.2 0.6 collective-permute-done.3
  41.8 5.7 %collective-permute-done.4 = bf16[264,256]{1,0:T(8,128)(2,1)S(1)} collective-permute-done((bf16[264,256]{1,0:T(8,128)(2,1)S(1)}, bf16[264,256]{1,0:T(8,128)(2,1)S(1)}, u32[]{:S(2)}, u32[]{:S(2)}) %collective-permute-start.4) | collective-permute-done | bytes 135200 | tf_op jit(solution)/shard_map/ppermute | solution.py:18
  47.6 0.9 pad_maximum_fusion.1
  48.5 2.4 %collective-permute-start.5 = (bf16[4,264,256]{2,1,0:T(8,128)(2,1)S(1)}, bf16[4,264,256]{2,1,0:T(8,128)(2,1)S(1)}, u32[]{:S(2)}, u32[]{:S(2)}) collective-permute-start(bf16[4,264,256]{2,1,0:T(8,128)(2,1)S(1)} %pad_maximum_fusion.refs_1_), channel_id=1, source_target_pairs={{0,1},{1,2},{2,3},{3,4},{4,5},{5,6},{6,7},{7,0},{8,9},{9,10},{10,1... | collective-permute-start | bytes 1622024 | tf_op jit(solution)/shard_map/ppermute | solution.py:18
  50.9 4.0 %collective-permute-start.6 = (bf16[4,264,256]{2,1,0:T(8,128)(2,1)S(1)}, bf16[4,264,256]{2,1,0:T(8,128)(2,1)S(1)}, u32[]{:S(2)}, u32[]{:S(2)}) collective-permute-start(bf16[4,264,256]{2,1,0:T(8,128)(2,1)S(1)} %pad_maximum_fusion.refs_1_), channel_id=1, source_target_pairs={{0,7},{1,0},{2,1},{3,2},{4,3},{5,4},{6,5},{7,6},{8,15},{9,8},{10,9... | collective-permute-start | bytes 1622024 | tf_op jit(solution)/shard_map/ppermute | solution.py:18
  55.0 0.5 all-gather.6.cloned.1.call-done.refs_0_
  55.5 3.1 %slice_bitcast_fusion = (bf16[8,264,256]{2,1,0:T(8,128)(2,1)}, bf16[8,264,256]{2,1,0:T(8,128)(2,1)}) fusion(bf16[8,2,264,256]{3,2,1,0:T(8,128)(2,1)} %bitcast.58), kind=kLoop, calls=%fused_computation | loop fusion | bytes 4325376 | tf_op jit(solution)/shard_map/squeeze | solution.py:114
  58.6 8.5 %collective-permute-done.5.refs_2_ = bf16[4,264,256]{2,1,0:T(8,128)(2,1)S(1)} collective-permute-done((bf16[4,264,256]{2,1,0:T(8,128)(2,1)S(1)}, bf16[4,264,256]{2,1,0:T(8,128)(2,1)S(1)}, u32[]{:S(2)}, u32[]{:S(2)}) %collective-permute-start.5) | collective-permute-done | bytes 540704 | tf_op jit(solution)/shard_map/ppermute | solution.py:18
  67.1 2.8 %collective-permute-start.7 = (bf16[4,264,256]{2,1,0:T(8,128)(2,1)S(1)}, bf16[4,264,256]{2,1,0:T(8,128)(2,1)S(1)}, u32[]{:S(2)}, u32[]{:S(2)}) collective-permute-start(bf16[4,264,256]{2,1,0:T(8,128)(2,1)S(1)} %collective-permute-done.5.refs_2_), channel_id=1, source_target_pairs={{0,1},{1,2},{2,3},{3,4},{4,5},{5,6},{6,7},{7,0},{8,9},{9,10},{10,1... | collective-permute-start | bytes 1622024 | tf_op jit(solution)/shard_map/ppermute | solution.py:18
  69.9 4.2 %collective-permute-start.8 = (bf16[4,264,256]{2,1,0:T(8,128)(2,1)S(1)}, bf16[4,264,256]{2,1,0:T(8,128)(2,1)S(1)}, u32[]{:S(2)}, u32[]{:S(2)}) collective-permute-start(bf16[4,264,256]{2,1,0:T(8,128)(2,1)S(1)} %collective-permute-done.6.refs_3_), channel_id=1, source_target_pairs={{0,7},{1,0},{2,1},{3,2},{4,3},{5,4},{6,5},{7,6},{8,15},{9,8},{10,9... | collective-permute-start | bytes 1622024 | tf_op jit(solution)/shard_map/ppermute | solution.py:18
  74.2 3.7 %collective-permute-start.13 = (bf16[8,264,256]{2,1,0:T(8,128)(2,1)}, bf16[8,264,256]{2,1,0:T(8,128)(2,1)S(1)}, u32[]{:S(2)}, u32[]{:S(2)}) collective-permute-start(bf16[8,264,256]{2,1,0:T(8,128)(2,1)} %get-tuple-element.19), channel_id=1, source_target_pairs={{0,8},{8,16},{16,24},{24,0},{1,9},{9,17},{17,25},{25,1},{2,10},{10... | collective-permute-start | bytes 3244040 | tf_op jit(solution)/shard_map/ppermute | solution.py:18
  77.8 3.7 %collective-permute-start.14 = (bf16[8,264,256]{2,1,0:T(8,128)(2,1)}, bf16[8,264,256]{2,1,0:T(8,128)(2,1)}, u32[]{:S(2)}, u32[]{:S(2)}) collective-permute-start(bf16[8,264,256]{2,1,0:T(8,128)(2,1)} %get-tuple-element.20), channel_id=1, source_target_pairs={{0,24},{8,0},{16,8},{24,16},{1,25},{9,1},{17,9},{25,17},{2,26},{10... | collective-permute-start | bytes 3244040 | tf_op jit(solution)/shard_map/ppermute | solution.py:18
  81.6 1.9 %collective-permute-done.7.refs_4_ = bf16[4,264,256]{2,1,0:T(8,128)(2,1)S(1)} collective-permute-done((bf16[4,264,256]{2,1,0:T(8,128)(2,1)S(1)}, bf16[4,264,256]{2,1,0:T(8,128)(2,1)S(1)}, u32[]{:S(2)}, u32[]{:S(2)}) %collective-permute-start.7) | collective-permute-done | bytes 540704 | tf_op jit(solution)/shard_map/ppermute | solution.py:18
  83.5 1.9 %collective-permute-start.9 = (bf16[4,264,256]{2,1,0:T(8,128)(2,1)S(1)}, bf16[4,264,256]{2,1,0:T(8,128)(2,1)S(1)}, u32[]{:S(2)}, u32[]{:S(2)}) collective-permute-start(bf16[4,264,256]{2,1,0:T(8,128)(2,1)S(1)} %collective-permute-done.7.refs_4_), channel_id=1, source_target_pairs={{0,1},{1,2},{2,3},{3,4},{4,5},{5,6},{6,7},{7,0},{8,9},{9,10},{10,1... | collective-permute-start | bytes 1622024 | tf_op jit(solution)/shard_map/ppermute | solution.py:18
  85.4 4.6 %collective-permute-start.10 = (bf16[4,264,256]{2,1,0:T(8,128)(2,1)S(1)}, bf16[4,264,256]{2,1,0:T(8,128)(2,1)S(1)}, u32[]{:S(2)}, u32[]{:S(2)}) collective-permute-start(bf16[4,264,256]{2,1,0:T(8,128)(2,1)S(1)} %collective-permute-done.8.refs_5_), channel_id=1, source_target_pairs={{0,7},{1,0},{2,1},{3,2},{4,3},{5,4},{6,5},{7,6},{8,15},{9,8},{10,9... | collective-permute-start | bytes 1622024 | tf_op jit(solution)/shard_map/ppermute | solution.py:18
  90.0 8.5 %collective-permute-done.9.refs_6_ = bf16[4,264,256]{2,1,0:T(8,128)(2,1)S(1)} collective-permute-done((bf16[4,264,256]{2,1,0:T(8,128)(2,1)S(1)}, bf16[4,264,256]{2,1,0:T(8,128)(2,1)S(1)}, u32[]{:S(2)}, u32[]{:S(2)}) %collective-permute-start.9) | collective-permute-done | bytes 540704 | tf_op jit(solution)/shard_map/ppermute | solution.py:18
  98.5 0.8 slice.128
  99.3 1.9 %collective-permute-start.11 = (bf16[2,264,256]{2,1,0:T(8,128)(2,1)}, bf16[2,264,256]{2,1,0:T(8,128)(2,1)S(1)}, u32[]{:S(2)}, u32[]{:S(2)}) collective-permute-start(bf16[2,264,256]{2,1,0:T(8,128)(2,1)} %slice.128), channel_id=1, source_target_pairs={{0,1},{1,2},{2,3},{3,4},{4,5},{5,6},{6,7},{7,0},{8,9},{9,10},{10,1... | collective-permute-start | bytes 811016 | tf_op jit(solution)/shard_map/ppermute | solution.py:18
  101.2 0.8 slice.130
  102.0 4.6 %collective-permute-start.12 = (bf16[2,264,256]{2,1,0:T(8,128)(2,1)}, bf16[2,264,256]{2,1,0:T(8,128)(2,1)}, u32[]{:S(2)}, u32[]{:S(2)}) collective-permute-start(bf16[2,264,256]{2,1,0:T(8,128)(2,1)} %slice.130), channel_id=1, source_target_pairs={{0,7},{1,0},{2,1},{3,2},{4,3},{5,4},{6,5},{7,6},{8,15},{9,8},{10,9... | collective-permute-start | bytes 811016 | tf_op jit(solution)/shard_map/ppermute | solution.py:18
  106.6 0.6 copy.103.out_ref_index
  107.2 0.1 copy.89
  107.3 0.1 copy.90
  107.5 0.7 slice.121
  108.2 0.1 copy.91
  108.3 0.8 slice.114
  109.0 0.1 copy.88
  109.1 0.7 slice.124
  109.8 0.1 copy.94
  109.9 0.7 slice.125
  110.6 0.1 copy.95
  110.8 0.1 copy.96
  110.9 0.1 copy.97
  111.0 15.6 %collective-permute-done.13.refs_10_ = bf16[8,264,256]{2,1,0:T(8,128)(2,1)S(1)} collective-permute-done((bf16[8,264,256]{2,1,0:T(8,128)(2,1)}, bf16[8,264,256]{2,1,0:T(8,128)(2,1)S(1)}, u32[]{:S(2)}, u32[]{:S(2)}) %collective-permute-start.13) | collective-permute-done | bytes 1081376 | tf_op jit(solution)/shard_map/ppermute | solution.py:18
  126.6 0.1 copy.98
  126.7 2.3 %collective-permute-done.14.refs_11_ = bf16[8,264,256]{2,1,0:T(8,128)(2,1)} collective-permute-done((bf16[8,264,256]{2,1,0:T(8,128)(2,1)}, bf16[8,264,256]{2,1,0:T(8,128)(2,1)}, u32[]{:S(2)}, u32[]{:S(2)}) %collective-permute-start.14) | collective-permute-done | bytes 1081376 | tf_op jit(solution)/shard_map/ppermute | solution.py:18
  129.0 0.7 slice.133
  129.8 0.1 copy.99
  129.9 0.1 copy.104
  130.0 0.7 slice.131
  130.7 0.1 copy.105
  130.8 0.1 concatenate.13
  130.9 0.1 broadcast_compare_fusion.2
  131.0 0.9 slice.134
  131.8 0.1 copy.108
  131.9 0.1 broadcast_compare_fusion
  132.0 0.1 broadcast_compare_fusion.1
  132.1 0.2 select_reduce_fusion
  132.3 0.6 reshape.208.pos_ref
  133.0 5.5 %shard_map.37 = (f32[4,256,256]{2,1,0:T(8,128)}, f32[16,2,256]{2,1,0:T(2,128)}) custom-call(s32[128]{0:T(128)} %reshape.208.pos_ref, s32[4,2]{1,0:T(4,128)} %copy.103.out_ref_index, bf16[16,264,256]{2,1,0:T(8,128)(2,1)} %all-gather.6.cloned.1.call-done.refs_0_, bf16[4,264,256]{2,1,0:T(8,128)(2,1)} %copy-done.1, bf16[4,264,256]{2,1,0:T(8,128)(2,1)} %copy-done.5, ...), custom_call_target="tpu_custom_call" | custom-call | tf_op jit(solution)/shard_map/pallas_call | solution.py:137
  138.5 5.0 %all-to-all-start = ((f32[16,2,256]{2,1,0:T(2,128)}), f32[16,2,256]{2,1,0:T(2,128)S(1)}, u32[]{:S(2)}, u32[]{:S(2)}) async-start(f32[16,2,256]{2,1,0:T(2,128)} %get-tuple-element.24), calls=%async_computation | async-start | bytes 65536 | tf_op jit(solution)/shard_map/all_to_all | solution.py:157
  143.5 5.8 %all-to-all-done = f32[16,2,256]{2,1,0:T(2,128)S(1)} async-done(((f32[16,2,256]{2,1,0:T(2,128)}), f32[16,2,256]{2,1,0:T(2,128)S(1)}, u32[]{:S(2)}, u32[]{:S(2)}) %all-to-all-start) | async-done | bytes 32800 | tf_op jit(solution)/shard_map/all_to_all | solution.py:157
  149.3 0.1 select_select_fusion
  149.4 2.3 %divide_bitcast_fusion = f32[1,4,256,256]{3,2,1,0:T(8,128)} fusion(f32[4,256,256]{2,1,0:T(8,128)} %get-tuple-element.23, f32[4,256]{1,0:T(4,128)S(1)} %select_select_fusion), kind=kLoop, calls=%fused_computation.2 | loop fusion | flops 524288 | bytes 2101248 | tf_op jit(solution)/shard_map/broadcast_in_dim | solution.py:162
  (51 shorter events, 0.3 us)
Async XLA Ops:
  6.5 49.0 %all-gather.6.cloned.1.call-start = ((), (), s32[]{:S(2)}) async-start(), calls=%async_computation.2 | async-start | bytes 2433024 | tf_op jit(solution)/shard_map/all_gather | solution.py:101
  8.9 38.6 %copy-start = (bf16[1,2,256,256]{3,2,1,0:T(8,128)(2,1)S(1)}, bf16[1,2,256,256]{3,2,1,0:T(8,128)(2,1)}, u32[]{:S(2)}) copy-start(bf16[1,2,256,256]{3,2,1,0:T(8,128)(2,1)} %param.3) | copy-start | bytes 786436
  8.9 122.0 %all-gather.4.cloned.1.call-start = ((), (), s32[]{:S(2)}) async-start(), calls=%async_computation.1 | async-start | bytes 4866048 | tf_op jit(solution)/shard_map/all_gather | solution.py:108
  9.0 24.8 %collective-permute-start.2 = (bf16[2,264,256]{2,1,0:T(8,128)(2,1)}, bf16[2,264,256]{2,1,0:T(8,128)(2,1)S(1)}, u32[]{:S(2)}, u32[]{:S(2)}) collective-permute-start(bf16[2,264,256]{2,1,0:T(8,128)(2,1)} %pad_maximum_fusion.2), channel_id=1, source_target_pairs={{0,256},{256,0},{1,257},{257,1},{2,258},{258,2},{3,259},{259,3},{4... | collective-permute-start | bytes 811016 | tf_op jit(solution)/shard_map/ppermute | solution.py:18
  14.8 18.7 %collective-permute-start = (bf16[264,256]{1,0:T(8,128)(2,1)S(1)}, bf16[264,256]{1,0:T(8,128)(2,1)S(1)}, u32[]{:S(2)}, u32[]{:S(2)}) collective-permute-start(bf16[264,256]{1,0:T(8,128)(2,1)S(1)} %get-tuple-element.28), channel_id=1, source_target_pairs={{0,8},{8,16},{16,24},{24,0},{1,9},{9,17},{17,25},{25,1},{2,10},{10... | collective-permute-start | bytes 405512 | tf_op jit(solution)/shard_map/ppermute | solution.py:18
  20.6 13.2 %collective-permute-start.1 = (bf16[264,256]{1,0:T(8,128)(2,1)S(1)}, bf16[264,256]{1,0:T(8,128)(2,1)S(1)}, u32[]{:S(2)}, u32[]{:S(2)}) collective-permute-start(bf16[264,256]{1,0:T(8,128)(2,1)S(1)} %get-tuple-element.27), channel_id=1, source_target_pairs={{0,24},{8,0},{16,8},{24,16},{1,25},{9,1},{17,9},{25,17},{2,26},{10... | collective-permute-start | bytes 405512 | tf_op jit(solution)/shard_map/ppermute | solution.py:18
  33.8 8.0 %collective-permute-start.3 = (bf16[264,256]{1,0:T(8,128)(2,1)S(1)}, bf16[264,256]{1,0:T(8,128)(2,1)S(1)}, u32[]{:S(2)}, u32[]{:S(2)}) collective-permute-start(bf16[264,256]{1,0:T(8,128)(2,1)S(1)} %collective-permute-done), channel_id=1, source_target_pairs={{0,8},{8,16},{16,24},{24,0},{1,9},{9,17},{17,25},{25,1},{2,10},{10... | collective-permute-start | bytes 405512 | tf_op jit(solution)/shard_map/ppermute | solution.py:18
  39.0 8.5 %collective-permute-start.4 = (bf16[264,256]{1,0:T(8,128)(2,1)S(1)}, bf16[264,256]{1,0:T(8,128)(2,1)S(1)}, u32[]{:S(2)}, u32[]{:S(2)}) collective-permute-start(bf16[264,256]{1,0:T(8,128)(2,1)S(1)} %collective-permute-done.1), channel_id=1, source_target_pairs={{0,24},{8,0},{16,8},{24,16},{1,25},{9,1},{17,9},{25,17},{2,26},{10... | collective-permute-start | bytes 405512 | tf_op jit(solution)/shard_map/ppermute | solution.py:18
  47.6 59.7 %copy-start.1 = (bf16[4,264,256]{2,1,0:T(8,128)(2,1)}, bf16[4,264,256]{2,1,0:T(8,128)(2,1)S(1)}, u32[]{:S(2)}) copy-start(bf16[4,264,256]{2,1,0:T(8,128)(2,1)S(1)} %pad_maximum_fusion.refs_1_) | copy-start | bytes 1622020
  48.5 18.6 %collective-permute-start.5 = (bf16[4,264,256]{2,1,0:T(8,128)(2,1)S(1)}, bf16[4,264,256]{2,1,0:T(8,128)(2,1)S(1)}, u32[]{:S(2)}, u32[]{:S(2)}) collective-permute-start(bf16[4,264,256]{2,1,0:T(8,128)(2,1)S(1)} %pad_maximum_fusion.refs_1_), channel_id=1, source_target_pairs={{0,1},{1,2},{2,3},{3,4},{4,5},{5,6},{6,7},{7,0},{8,9},{9,10},{10,1... | collective-permute-start | bytes 1622024 | tf_op jit(solution)/shard_map/ppermute | solution.py:18
  50.9 16.2 %collective-permute-start.6 = (bf16[4,264,256]{2,1,0:T(8,128)(2,1)S(1)}, bf16[4,264,256]{2,1,0:T(8,128)(2,1)S(1)}, u32[]{:S(2)}, u32[]{:S(2)}) collective-permute-start(bf16[4,264,256]{2,1,0:T(8,128)(2,1)S(1)} %pad_maximum_fusion.refs_1_), channel_id=1, source_target_pairs={{0,7},{1,0},{2,1},{3,2},{4,3},{5,4},{6,5},{7,6},{8,15},{9,8},{10,9... | collective-permute-start | bytes 1622024 | tf_op jit(solution)/shard_map/ppermute | solution.py:18
  58.6 48.0 %copy-start.10 = (s32[1,4,2]{1,2,0:T(2,128)S(1)}, s32[1,4,2]{1,2,0:T(2,128)}, u32[]{:S(2)}) copy-start(s32[1,4,2]{1,2,0:T(2,128)} %param.5) | copy-start | bytes 100
  67.1 65.8 %copy-start.5 = (bf16[4,264,256]{2,1,0:T(8,128)(2,1)}, bf16[4,264,256]{2,1,0:T(8,128)(2,1)S(1)}, u32[]{:S(2)}) copy-start(bf16[4,264,256]{2,1,0:T(8,128)(2,1)S(1)} %collective-permute-done.5.refs_2_) | copy-start | bytes 1622020
  67.1 18.3 %copy-start.6 = (bf16[4,264,256]{2,1,0:T(8,128)(2,1)}, bf16[4,264,256]{2,1,0:T(8,128)(2,1)S(1)}, u32[]{:S(2)}) copy-start(bf16[4,264,256]{2,1,0:T(8,128)(2,1)S(1)} %collective-permute-done.6.refs_3_) | copy-start | bytes 1622020
  67.1 16.4 %collective-permute-start.7 = (bf16[4,264,256]{2,1,0:T(8,128)(2,1)S(1)}, bf16[4,264,256]{2,1,0:T(8,128)(2,1)S(1)}, u32[]{:S(2)}, u32[]{:S(2)}) collective-permute-start(bf16[4,264,256]{2,1,0:T(8,128)(2,1)S(1)} %collective-permute-done.5.refs_2_), channel_id=1, source_target_pairs={{0,1},{1,2},{2,3},{3,4},{4,5},{5,6},{6,7},{7,0},{8,9},{9,10},{10,1... | collective-permute-start | bytes 1622024 | tf_op jit(solution)/shard_map/ppermute | solution.py:18
  69.9 15.5 %collective-permute-start.8 = (bf16[4,264,256]{2,1,0:T(8,128)(2,1)S(1)}, bf16[4,264,256]{2,1,0:T(8,128)(2,1)S(1)}, u32[]{:S(2)}, u32[]{:S(2)}) collective-permute-start(bf16[4,264,256]{2,1,0:T(8,128)(2,1)S(1)} %collective-permute-done.6.refs_3_), channel_id=1, source_target_pairs={{0,7},{1,0},{2,1},{3,2},{4,3},{5,4},{6,5},{7,6},{8,15},{9,8},{10,9... | collective-permute-start | bytes 1622024 | tf_op jit(solution)/shard_map/ppermute | solution.py:18
  74.2 52.5 %collective-permute-start.13 = (bf16[8,264,256]{2,1,0:T(8,128)(2,1)}, bf16[8,264,256]{2,1,0:T(8,128)(2,1)S(1)}, u32[]{:S(2)}, u32[]{:S(2)}) collective-permute-start(bf16[8,264,256]{2,1,0:T(8,128)(2,1)} %get-tuple-element.19), channel_id=1, source_target_pairs={{0,8},{8,16},{16,24},{24,0},{1,9},{9,17},{17,25},{25,1},{2,10},{10... | collective-permute-start | bytes 3244040 | tf_op jit(solution)/shard_map/ppermute | solution.py:18
  77.8 51.2 %collective-permute-start.14 = (bf16[8,264,256]{2,1,0:T(8,128)(2,1)}, bf16[8,264,256]{2,1,0:T(8,128)(2,1)}, u32[]{:S(2)}, u32[]{:S(2)}) collective-permute-start(bf16[8,264,256]{2,1,0:T(8,128)(2,1)} %get-tuple-element.20), channel_id=1, source_target_pairs={{0,24},{8,0},{16,8},{24,16},{1,25},{9,1},{17,9},{25,17},{2,26},{10... | collective-permute-start | bytes 3244040 | tf_op jit(solution)/shard_map/ppermute | solution.py:18
  83.5 1.9 %copy-start.7 = (bf16[4,264,256]{2,1,0:T(8,128)(2,1)}, bf16[4,264,256]{2,1,0:T(8,128)(2,1)S(1)}, u32[]{:S(2)}) copy-start(bf16[4,264,256]{2,1,0:T(8,128)(2,1)S(1)} %collective-permute-done.7.refs_4_) | copy-start | bytes 1622020
  83.5 15.0 %collective-permute-start.9 = (bf16[4,264,256]{2,1,0:T(8,128)(2,1)S(1)}, bf16[4,264,256]{2,1,0:T(8,128)(2,1)S(1)}, u32[]{:S(2)}, u32[]{:S(2)}) collective-permute-start(bf16[4,264,256]{2,1,0:T(8,128)(2,1)S(1)} %collective-permute-done.7.refs_4_), channel_id=1, source_target_pairs={{0,1},{1,2},{2,3},{3,4},{4,5},{5,6},{6,7},{7,0},{8,9},{9,10},{10,1... | collective-permute-start | bytes 1622024 | tf_op jit(solution)/shard_map/ppermute | solution.py:18
  85.4 15.8 %copy-start.8 = (bf16[4,264,256]{2,1,0:T(8,128)(2,1)}, bf16[4,264,256]{2,1,0:T(8,128)(2,1)S(1)}, u32[]{:S(2)}) copy-start(bf16[4,264,256]{2,1,0:T(8,128)(2,1)S(1)} %collective-permute-done.8.refs_5_) | copy-start | bytes 1622020
  85.4 15.7 %collective-permute-start.10 = (bf16[4,264,256]{2,1,0:T(8,128)(2,1)S(1)}, bf16[4,264,256]{2,1,0:T(8,128)(2,1)S(1)}, u32[]{:S(2)}, u32[]{:S(2)}) collective-permute-start(bf16[4,264,256]{2,1,0:T(8,128)(2,1)S(1)} %collective-permute-done.8.refs_5_), channel_id=1, source_target_pairs={{0,7},{1,0},{2,1},{3,2},{4,3},{5,4},{6,5},{7,6},{8,15},{9,8},{10,9... | collective-permute-start | bytes 1622024 | tf_op jit(solution)/shard_map/ppermute | solution.py:18
  98.5 34.4 %copy-start.2 = (bf16[4,264,256]{2,1,0:T(8,128)(2,1)}, bf16[4,264,256]{2,1,0:T(8,128)(2,1)S(1)}, u32[]{:S(2)}) copy-start(bf16[4,264,256]{2,1,0:T(8,128)(2,1)S(1)} %collective-permute-done.9.refs_6_) | copy-start | bytes 1622020
  99.3 30.6 %collective-permute-start.11 = (bf16[2,264,256]{2,1,0:T(8,128)(2,1)}, bf16[2,264,256]{2,1,0:T(8,128)(2,1)S(1)}, u32[]{:S(2)}, u32[]{:S(2)}) collective-permute-start(bf16[2,264,256]{2,1,0:T(8,128)(2,1)} %slice.128), channel_id=1, source_target_pairs={{0,1},{1,2},{2,3},{3,4},{4,5},{5,6},{6,7},{7,0},{8,9},{9,10},{10,1... | collective-permute-start | bytes 811016 | tf_op jit(solution)/shard_map/ppermute | solution.py:18
  101.2 31.7 %copy-start.3 = (bf16[4,264,256]{2,1,0:T(8,128)(2,1)}, bf16[4,264,256]{2,1,0:T(8,128)(2,1)S(1)}, u32[]{:S(2)}) copy-start(bf16[4,264,256]{2,1,0:T(8,128)(2,1)S(1)} %collective-permute-done.10.refs_7_) | copy-start | bytes 1622020
  102.0 28.0 %collective-permute-start.12 = (bf16[2,264,256]{2,1,0:T(8,128)(2,1)}, bf16[2,264,256]{2,1,0:T(8,128)(2,1)}, u32[]{:S(2)}, u32[]{:S(2)}) collective-permute-start(bf16[2,264,256]{2,1,0:T(8,128)(2,1)} %slice.130), channel_id=1, source_target_pairs={{0,7},{1,0},{2,1},{3,2},{4,3},{5,4},{6,5},{7,6},{8,15},{9,8},{10,9... | collective-permute-start | bytes 811016 | tf_op jit(solution)/shard_map/ppermute | solution.py:18
  126.6 6.3 %copy-start.4 = (bf16[8,264,256]{2,1,0:T(8,128)(2,1)}, bf16[8,264,256]{2,1,0:T(8,128)(2,1)S(1)}, u32[]{:S(2)}) copy-start(bf16[8,264,256]{2,1,0:T(8,128)(2,1)S(1)} %collective-permute-done.13.refs_10_) | copy-start | bytes 3244036
  129.9 3.1 %copy-start.9 = (bf16[2,264,256]{2,1,0:T(8,128)(2,1)}, bf16[2,264,256]{2,1,0:T(8,128)(2,1)S(1)}, u32[]{:S(2)}) copy-start(bf16[2,264,256]{2,1,0:T(8,128)(2,1)S(1)} %collective-permute-done.11.refs_8_) | copy-start | bytes 811012
  138.5 10.8 %all-to-all-start = ((f32[16,2,256]{2,1,0:T(2,128)}), f32[16,2,256]{2,1,0:T(2,128)S(1)}, u32[]{:S(2)}, u32[]{:S(2)}) async-start(f32[16,2,256]{2,1,0:T(2,128)} %get-tuple-element.24), calls=%async_computation | async-start | bytes 65536 | tf_op jit(solution)/shard_map/all_to_all | solution.py:157
Sparse Core Ops, SparseCore 0:
  9.4 46.0 all-gather.5
  57.6 44.0 all-gather.3

commit v6 on v5

v6 whole, which is shorter than its diff:
```python
import jax
import jax.numpy as jnp
from jax import lax
from jax.experimental import pallas as pl
from jax.experimental.pallas import tpu as pltpu
from jax.sharding import Mesh, PartitionSpec as P

COL_BLOCKS = 2
SLOTS = 2
TILE = 256
LATE = 192
PART = TILE - LATE
PAD = 8
PACK = SLOTS * TILE + PAD
FINE = (("zl", 2), ("x", 4), ("core", 2), ("zh", 4), ("y", 8))
ROW = ("zl", "x", "core")
COL = ("zh", "y")
UP, DOWN, UP2, DOWN2, MARKS = 0, TILE + PART, 2 * (TILE + PART), 3 * TILE + 2 * PART, 4 * TILE + 2 * PART
TURNS = (0, -1, 1, -2, 2, -3, 3, 4)
N_Y = len(TURNS)
OWN_TILES = N_Y * SLOTS
RING_TILES = 4 * N_Y
RIGHTS = 32
BUFS = 8


def shift(value, axis, size, by):
    return lax.ppermute(value, axis, [(i, (i + by) % size) for i in range(size)])


def rows_at(start, count):
    return pl.ds(pl.multiple_of(start, PAD), count)


def convert_kernel(in_ref, out_ref):
    out_ref[...] = in_ref[...].astype(jnp.int32)


def product_kernel(pos_ref, out_ref_index, source_ref, *refs):
    own, ring, (late_up, late_down) = refs[0], refs[1 : 1 + N_Y], refs[1 + N_Y : 3 + N_Y]
    right, exp_ref, part_ref, todo, lbuf, rbuf, sem = refs[3 + N_Y :]

    exp_ref[...] = jnp.zeros_like(exp_ref)

    def note(i, n):
        code = pos_ref[i]

        @pl.when(code >= 0)
        def _():
            todo[0, n] = code
            todo[1, n] = i

        return n + (code >= 0).astype(jnp.int32)

    total = lax.fori_loop(0, pos_ref.shape[0], note, jnp.int32(0))

    def pack_rows(tile):
        return rows_at(tile // SLOTS * PACK + tile % SLOTS * TILE, TILE)

    def start(n):
        slot = n % BUFS
        code = todo[0, n]

        def from_block(block, offset, count, target):
            for j, ref in enumerate(ring):

                @pl.when(block == j)
                def _(ref=ref):
                    rows = ref.at[rows_at(offset, count)]
                    pltpu.make_async_copy(rows, target, sem.at[0, slot]).start()

        @pl.when(code < OWN_TILES)
        def _():
            pltpu.make_async_copy(own.at[pack_rows(code)], lbuf.at[slot], sem.at[0, slot]).start()

        @pl.when((code >= OWN_TILES) & (code < OWN_TILES + RING_TILES))
        def _():
            kind = code % 4
            offset = jnp.where(
                kind < 2, jnp.where(kind == 0, UP, DOWN), jnp.where(kind == 2, UP2, DOWN2)
            )
            from_block((code - OWN_TILES) // 4, offset, TILE, lbuf.at[slot])

        for late, offset, first in (
            (late_up, UP + TILE, OWN_TILES + RING_TILES),
            (late_down, DOWN + TILE, OWN_TILES + RING_TILES + N_Y),
        ):

            @pl.when((code >= first) & (code < first + N_Y))
            def _(late=late, offset=offset, first=first):
                block = code - first
                pltpu.make_async_copy(
                    late.at[source_ref[block], pl.ds(0, LATE)],
                    lbuf.at[slot, pl.ds(0, LATE)],
                    sem.at[0, slot],
                ).start()
                from_block(block, offset, PART, lbuf.at[slot, pl.ds(LATE, PART)])

        pltpu.make_async_copy(
            right.at[pack_rows(todo[1, n] % RIGHTS)], rbuf.at[slot], sem.at[1, slot]
        ).start()

    def prime(n, carry):
        start(n)
        return carry

    lax.fori_loop(0, jnp.minimum(total, BUFS), prime, 0)

    def multiply(n, carry):
        slot = n % BUFS
        pltpu.make_async_copy(right.at[pl.ds(0, TILE)], lbuf.at[slot], sem.at[0, slot]).wait()
        pltpu.make_async_copy(right.at[pl.ds(0, TILE)], rbuf.at[slot], sem.at[1, slot]).wait()
        o = todo[1, n] // RIGHTS
        exp_ref[o] += jnp.dot(lbuf[slot], rbuf[slot], preferred_element_type=jnp.float32)

        @pl.when(n + BUFS < total)
        def _():
            start(n + BUFS)

        return carry

    lax.fori_loop(0, total, multiply, 0)

    part_ref[...] = jnp.zeros_like(part_ref)
    for o in range(exp_ref.shape[0]):
        value = exp_ref[o]
        squared = value * value
        exp_ref[o] = squared
        column = out_ref_index[o, 1]
        for j in range(COL_BLOCKS):

            @pl.when((column >= 0) & (column % COL_BLOCKS == j))
            def _():
                part_ref[:, j : j + 1, :] += jnp.sum(squared, axis=0, keepdims=True)[None]


def shards(tiles, in_index, out_index):
    tiles, out_index = tiles[0], out_index[0]
    out_count = out_index.shape[0]
    marks = jnp.pad(
        in_index.reshape(1, -1).astype(tiles.dtype), ((0, PAD - 1), (0, TILE - 2 * SLOTS))
    )
    mine = jnp.concatenate([tiles[0], tiles[1], marks])

    own = lax.all_gather(mine, "y", axis=0, tiled=False)
    other = shift(mine, "zl", 2, 1)
    up = shift(jnp.concatenate([tiles[0], tiles[1, LATE:], marks]), "zh", 4, 1)
    down = shift(jnp.concatenate([tiles[1], tiles[0, LATE:], marks]), "zh", 4, -1)
    up2 = shift(jnp.concatenate([tiles[0], marks]), "zh", 4, 2)
    down2 = shift(jnp.concatenate([tiles[1], marks]), "zh", 4, -2)
    hops = (up, down, up2, down2)
    signs = [hop[-PAD : 1 - PAD] for hop in hops] + [jnp.zeros((PAD - 4, TILE), tiles.dtype)]
    early = jnp.concatenate([hop[:-PAD] for hop in hops] + signs)
    other, early = lax.optimization_barrier((other, early))
    right = lax.all_gather(jnp.concatenate([mine, other]), ("x", "core"), axis=0, tiled=True)

    ring = [early]
    ahead = back = early
    for turn in range(3):
        if turn == 1:
            first, second, ahead, back = lax.optimization_barrier(
                (
                    jnp.concatenate([own[:, :LATE], own[:, -PAD:]], axis=1),
                    jnp.concatenate([own[:, TILE : TILE + LATE], own[:, -PAD:]], axis=1),
                    ahead,
                    back,
                )
            )
            late_up = shift(second, "zh", 4, 1)
            late_down = shift(first, "zh", 4, -1)
        ahead, back = shift(ahead, "y", N_Y, 1), shift(back, "y", N_Y, -1)
        ring += [ahead, back]
    ring.append(shift(back, "y", N_Y, -1))
    lefts = [own.reshape(-1, TILE)] + ring + [late_up, late_down]

    def signs_of(stack):
        return stack[..., : 2 * SLOTS]

    rows = [signs_of(block[MARKS : MARKS + 4]) for block in ring]
    rows = jnp.concatenate(rows).astype(jnp.int32).reshape(N_Y, 4, SLOTS, 2)
    late_rows = pl.pallas_call(
        convert_kernel,
        out_shape=jax.ShapeDtypeStruct((2 * N_Y, TILE), jnp.int32),
        cost_estimate=pl.CostEstimate(flops=2_000_000_000, bytes_accessed=0, transcendentals=0),
    )(jnp.concatenate([late_up[:, LATE], late_down[:, LATE]]))
    left_index = jnp.concatenate(
        [
            signs_of(own[:, -PAD]).astype(jnp.int32).reshape(-1, 2),
            jnp.stack([rows[:, t, t % 2] for t in range(4)], axis=1).reshape(-1, 2),
            late_rows[:N_Y, 2:4],
            late_rows[N_Y:, :2],
        ]
    )
    me = lax.axis_index("y")
    away = (jnp.arange(N_Y, dtype=jnp.int32) - me) % N_Y
    block = jnp.where(away == 4, 7, jnp.where(away < 4, 2 * away, 2 * (N_Y - away) - 1))
    fixed = OWN_TILES + RING_TILES
    places = jnp.concatenate(
        [jnp.arange(fixed, dtype=jnp.int32), fixed + block, fixed + N_Y + block]
    )
    sources = (me + jnp.array(TURNS, jnp.int32)) % N_Y
    right_index = signs_of(right.reshape(-1, PACK, TILE)[:, -PAD]).astype(jnp.int32).reshape(-1, 2)
    matches = (
        (left_index[None, None, :, 0] == out_index[:, None, None, 0])
        & (left_index[None, None, :, 1] == right_index[None, :, None, 0])
        & (right_index[None, :, None, 1] == out_index[:, None, None, 1])
        & (out_index[:, None, None, 0] >= 0)
    )
    pos = jnp.max(jnp.where(matches, places, -1), axis=2).reshape(-1)

    squared, parts = pl.pallas_call(
        product_kernel,
        grid_spec=pltpu.PrefetchScalarGridSpec(
            num_scalar_prefetch=3,
            grid=(),
            in_specs=[pl.BlockSpec(memory_space=pl.ANY)] * (len(lefts) + 1),
            out_specs=[pl.BlockSpec(memory_space=pltpu.VMEM)] * 2,
            scratch_shapes=[
                pltpu.SMEM((2, out_count * RIGHTS), jnp.int32),
                pltpu.VMEM((BUFS, TILE, TILE), jnp.bfloat16),
                pltpu.VMEM((BUFS, TILE, TILE), jnp.bfloat16),
                pltpu.SemaphoreType.DMA((2, BUFS)),
            ],
        ),
        out_shape=[
            pltpu.VMEM((out_count, TILE, TILE), jnp.float32),
            pltpu.VMEM((16, COL_BLOCKS, TILE), jnp.float32),
        ],
    )(pos, out_index, sources, *lefts, right)

    totals = jnp.sum(lax.all_to_all(parts, ROW, split_axis=0, concat_axis=0), axis=0)
    out_used = out_index[:, 0] >= 0
    second = (out_index[:, 1] % COL_BLOCKS == 1)[:, None]
    divisor = jnp.where(second, totals[1][None], totals[0][None])
    divisor = jnp.where(out_used[:, None], divisor, 1.0)
    return (TILE * squared / divisor[:, None, :])[None]


def solution(mesh):
    fine = Mesh(mesh.devices.reshape([size for _, size in FINE]), [name for name, _ in FINE])
    spec = P(ROW, COL)
    return jax.shard_map(
        shards, mesh=fine, in_specs=(spec, spec, spec), out_specs=spec, check_vma=False
    )
```

time: 160 us -> 154 us (0.963)
  waiting for transfers between devices: 56.7 us -> 38.1 us
  starting transfers between devices: 62.8 us -> 74.3 us
    ppermute x15 -> x14, waiting for transfers between devices: 50.4 us -> 27.1 us  [shift(): lax.ppermute(value, axis, [(i, (i + by) % size) for i in range(size)])]
    all_to_all x1, starting transfers between devices: 5.04 us -> 18 us  [shards(): lax.all_to_all(parts, ROW, split_axis=0, concat_axis=0)]
    all_gather x1, waiting for transfers between devices: 0.51 us -> 5.18 us  [shards(): own = lax.all_gather(mine, 'y', axis=0, tiled=False)]
    slice x25 -> x35, local copies, waits for them, and re-layouts: 7.76 us -> 10.2 us  [the longest x16 4.89 us: signs_of(): return stack[..., :2 * SLOTS]]
    pallas_call x1, Pallas kernels: 5.49 us -> 3.08 us  [shards(): pl.pallas_call(product_kernel, grid_spec=pltpu.PrefetchScalarGridSpec(num...]
    ppermute x15 -> x14, starting transfers between devices: 57.8 us -> 56.3 us  [shift(): lax.ppermute(value, axis, [(i, (i + by) % size) for i in range(size)])]
    squeeze x2 -> x3, local copies, waits for them, and re-layouts: 3.72 us -> 2.44 us  [the longest x1 0.98 us: shards(): mine = jnp.concatenate([tiles[0], tiles[1], marks])]
  transfers between devices with their start and end apart: 18 -> 17, of which waited for: 11 -> 10; matrix products, arithmetic and copies ran while one was open for 8% -> 10% of each run, Pallas kernels for 0% -> 1%
where the time goes in v6:
time: 154 us; the launch traced here: 151 us
  starting transfers between devices  74.3 us (48%)
  waiting for transfers between devices  38.1 us (25%)
  local copies, waits for them, and re-layouts  14.2 us (9%)
  between operations  13.8 us (9%)
  other arithmetic  6.46 us (4%)
  Pallas kernels  4.38 us (3%)
    ppermute x14, starting transfers between devices, shift(): lax.ppermute(value, axis, [(i, (i + by) % size) for i in range(size)])  56.3 us
    ppermute x14, waiting for transfers between devices, shift(): lax.ppermute(value, axis, [(i, (i + by) % size) for i in range(size)])  27.1 us
    all_to_all x1, starting transfers between devices, shards(): lax.all_to_all(parts, ROW, split_axis=0, concat_axis=0)  18 us
    all_to_all x1, waiting for transfers between devices, shards(): lax.all_to_all(parts, ROW, split_axis=0, concat_axis=0)  5.79 us
    all_gather x1, waiting for transfers between devices, shards(): own = lax.all_gather(mine, 'y', axis=0, tiled=False)  5.18 us
    slice x16, local copies, waits for them, and re-layouts, signs_of(): return stack[..., :2 * SLOTS]  4.89 us
  transfers between devices with their start and end apart: 17, of which 10 were waited for; matrix products, arithmetic and copies ran while one was open for 10% of the time, Pallas kernels for 1%

profile of v6, /device:TPU:1, one launch (start us, length us, event | category | flops | bytes accessed | tf_op | source)
XLA Modules:
  0.0 151.3 jit_solution(17931168631223895615)
XLA Ops:
  6.5 1.0 slice_bitcast_fusion.1
  7.5 0.7 convert_element_type.25
  8.2 0.1 convert_element_type.26
  8.3 0.7 pad_maximum_fusion.3
  9.1 4.8 %collective-permute-start = (bf16[520,256]{1,0:T(8,128)(2,1)}, bf16[520,256]{1,0:T(8,128)(2,1)S(1)}, u32[]{:S(2)}, u32[]{:S(2)}) collective-permute-start(bf16[520,256]{1,0:T(8,128)(2,1)} %pad_maximum_fusion.3), channel_id=1, source_target_pairs={{0,256},{256,0},{1,257},{257,1},{2,258},{258,2},{3,259},{259,3},{4... | collective-permute-start | bytes 798728 | tf_op jit(solution)/shard_map/ppermute | solution.py:28
  13.9 0.8 slice_bitcast_fusion.2
  14.7 5.8 %collective-permute-start.1 = (bf16[328,256]{1,0:T(8,128)(2,1)S(1)}, bf16[328,256]{1,0:T(8,128)(2,1)S(1)}, u32[]{:S(2)}, u32[]{:S(2)}) collective-permute-start(bf16[328,256]{1,0:T(8,128)(2,1)S(1)} %get-tuple-element.40), channel_id=1, source_target_pairs={{0,8},{8,16},{16,24},{24,0},{1,9},{9,17},{17,25},{25,1},{2,10},{10... | collective-permute-start | bytes 503816 | tf_op jit(solution)/shard_map/ppermute | solution.py:28
  20.6 5.9 %collective-permute-start.2 = (bf16[328,256]{1,0:T(8,128)(2,1)S(1)}, bf16[328,256]{1,0:T(8,128)(2,1)S(1)}, u32[]{:S(2)}, u32[]{:S(2)}) collective-permute-start(bf16[328,256]{1,0:T(8,128)(2,1)S(1)} %get-tuple-element.39), channel_id=1, source_target_pairs={{0,24},{8,0},{16,8},{24,16},{1,25},{9,1},{17,9},{25,17},{2,26},{10... | collective-permute-start | bytes 503816 | tf_op jit(solution)/shard_map/ppermute | solution.py:28
  26.5 5.5 %collective-permute-start.3 = (bf16[264,256]{1,0:T(8,128)(2,1)S(1)}, bf16[264,256]{1,0:T(8,128)(2,1)S(1)}, u32[]{:S(2)}, u32[]{:S(2)}) collective-permute-start(bf16[264,256]{1,0:T(8,128)(2,1)S(1)} %get-tuple-element.38), channel_id=1, source_target_pairs={{0,16},{8,24},{16,0},{24,8},{1,17},{9,25},{17,1},{25,9},{2,18},{10... | collective-permute-start | bytes 405512 | tf_op jit(solution)/shard_map/ppermute | solution.py:28
  31.9 3.7 %collective-permute-start.4 = (bf16[264,256]{1,0:T(8,128)(2,1)S(1)}, bf16[264,256]{1,0:T(8,128)(2,1)S(1)}, u32[]{:S(2)}, u32[]{:S(2)}) collective-permute-start(bf16[264,256]{1,0:T(8,128)(2,1)S(1)} %get-tuple-element.37), channel_id=1, source_target_pairs={{0,16},{8,24},{16,0},{24,8},{1,17},{9,25},{17,1},{25,9},{2,18},{10... | collective-permute-start | bytes 405512 | tf_op jit(solution)/shard_map/ppermute | solution.py:28
  35.7 3.6 %collective-permute-done.3 = bf16[264,256]{1,0:T(8,128)(2,1)S(1)} collective-permute-done((bf16[264,256]{1,0:T(8,128)(2,1)S(1)}, bf16[264,256]{1,0:T(8,128)(2,1)S(1)}, u32[]{:S(2)}, u32[]{:S(2)}) %collective-permute-start.3) | collective-permute-done | bytes 135200 | tf_op jit(solution)/shard_map/ppermute | solution.py:28
  39.3 4.3 %collective-permute-done.4 = bf16[264,256]{1,0:T(8,128)(2,1)S(1)} collective-permute-done((bf16[264,256]{1,0:T(8,128)(2,1)S(1)}, bf16[264,256]{1,0:T(8,128)(2,1)S(1)}, u32[]{:S(2)}, u32[]{:S(2)}) %collective-permute-start.4) | collective-permute-done | bytes 135200 | tf_op jit(solution)/shard_map/ppermute | solution.py:28
  43.7 0.2 concatenate.45.refs_1_
  43.9 0.9 pad_maximum_fusion.2
  44.9 3.2 %collective-permute-start.5 = (bf16[1160,256]{1,0:T(8,128)(2,1)S(1)}, bf16[1160,256]{1,0:T(8,128)(2,1)}, u32[]{:S(2)}, u32[]{:S(2)}) collective-permute-start(bf16[1160,256]{1,0:T(8,128)(2,1)S(1)} %concatenate.45.refs_1_), channel_id=1, source_target_pairs={{0,1},{1,2},{2,3},{3,4},{4,5},{5,6},{6,7},{7,0},{8,9},{9,10},{10,1... | collective-permute-start | bytes 1781768 | tf_op jit(solution)/shard_map/ppermute | solution.py:28
  48.1 3.8 %collective-permute-start.6 = (bf16[1160,256]{1,0:T(8,128)(2,1)S(1)}, bf16[1160,256]{1,0:T(8,128)(2,1)}, u32[]{:S(2)}, u32[]{:S(2)}) collective-permute-start(bf16[1160,256]{1,0:T(8,128)(2,1)S(1)} %concatenate.45.refs_1_), channel_id=1, source_target_pairs={{0,7},{1,0},{2,1},{3,2},{4,3},{5,4},{6,5},{7,6},{8,15},{9,8},{10,9... | collective-permute-start | bytes 1781768 | tf_op jit(solution)/shard_map/ppermute | solution.py:28
  51.9 5.2 %all-gather.6.cloned.1.call-done.refs_0_ = bf16[4160,256]{1,0:T(8,128)(2,1)} async-done(((bf16[520,256]{1,0:T(8,128)(2,1)}), bf16[4160,256]{1,0:T(8,128)(2,1)}) %all-gather.6.cloned.1.call-update) | async-done | bytes 2129936 | tf_op jit(solution)/shard_map/all_gather | solution.py:145
  57.1 0.8 slice.216
  57.9 1.5 fusion.3
  59.4 1.0 pad_maximum_fusion
  60.4 7.0 %collective-permute-done.5.refs_2_ = bf16[1160,256]{1,0:T(8,128)(2,1)} collective-permute-done((bf16[1160,256]{1,0:T(8,128)(2,1)S(1)}, bf16[1160,256]{1,0:T(8,128)(2,1)}, u32[]{:S(2)}, u32[]{:S(2)}) %collective-permute-start.5) | collective-permute-done | bytes 593952 | tf_op jit(solution)/shard_map/ppermute | solution.py:28
  67.4 0.5 collective-permute-done.6.refs_3_
  67.9 3.1 %collective-permute-start.8 = (bf16[1160,256]{1,0:T(8,128)(2,1)}, bf16[1160,256]{1,0:T(8,128)(2,1)}, u32[]{:S(2)}, u32[]{:S(2)}) collective-permute-start(bf16[1160,256]{1,0:T(8,128)(2,1)} %collective-permute-done.6.refs_3_), channel_id=1, source_target_pairs={{0,7},{1,0},{2,1},{3,2},{4,3},{5,4},{6,5},{7,6},{8,15},{9,8},{10,9... | collective-permute-start | bytes 1781768 | tf_op jit(solution)/shard_map/ppermute | solution.py:28
  71.1 0.5 and_select_fusion.1.source_ref
  71.6 2.2 %collective-permute-start.7 = (bf16[1160,256]{1,0:T(8,128)(2,1)}, bf16[1160,256]{1,0:T(8,128)(2,1)}, u32[]{:S(2)}, u32[]{:S(2)}) collective-permute-start(bf16[1160,256]{1,0:T(8,128)(2,1)} %collective-permute-done.5.refs_2_), channel_id=1, source_target_pairs={{0,1},{1,2},{2,3},{3,4},{4,5},{5,6},{6,7},{7,0},{8,9},{9,10},{10,1... | collective-permute-start | bytes 1781768 | tf_op jit(solution)/shard_map/ppermute | solution.py:28
  73.8 5.9 %collective-permute-start.13 = (bf16[8,200,256]{2,1,0:T(8,128)(2,1)}, bf16[8,200,256]{2,1,0:T(8,128)(2,1)S(1)}, u32[]{:S(2)}, u32[]{:S(2)}) collective-permute-start(bf16[8,200,256]{2,1,0:T(8,128)(2,1)} %get-tuple-element.17), channel_id=1, source_target_pairs={{0,24},{8,0},{16,8},{24,16},{1,25},{9,1},{17,9},{25,17},{2,26},{10... | collective-permute-start | bytes 2457608 | tf_op jit(solution)/shard_map/ppermute | solution.py:28
  79.7 2.2 %collective-permute-start.12 = (bf16[8,200,256]{2,1,0:T(8,128)(2,1)S(1)}, bf16[8,200,256]{2,1,0:T(8,128)(2,1)S(1)}, u32[]{:S(2)}, u32[]{:S(2)}) collective-permute-start(bf16[8,200,256]{2,1,0:T(8,128)(2,1)S(1)} %get-tuple-element.16), channel_id=1, source_target_pairs={{0,8},{8,16},{16,24},{24,0},{1,9},{9,17},{17,25},{25,1},{2,10},{10... | collective-permute-start | bytes 2457608 | tf_op jit(solution)/shard_map/ppermute | solution.py:28
  81.8 1.9 %collective-permute-done.8.refs_5_ = bf16[1160,256]{1,0:T(8,128)(2,1)} collective-permute-done((bf16[1160,256]{1,0:T(8,128)(2,1)}, bf16[1160,256]{1,0:T(8,128)(2,1)}, u32[]{:S(2)}, u32[]{:S(2)}) %collective-permute-start.8) | collective-permute-done | bytes 593952 | tf_op jit(solution)/shard_map/ppermute | solution.py:28
  83.8 3.8 %collective-permute-start.10 = (bf16[1160,256]{1,0:T(8,128)(2,1)}, bf16[1160,256]{1,0:T(8,128)(2,1)}, u32[]{:S(2)}, u32[]{:S(2)}) collective-permute-start(bf16[1160,256]{1,0:T(8,128)(2,1)} %collective-permute-done.8.refs_5_), channel_id=1, source_target_pairs={{0,7},{1,0},{2,1},{3,2},{4,3},{5,4},{6,5},{7,6},{8,15},{9,8},{10,9... | collective-permute-start | bytes 1781768 | tf_op jit(solution)/shard_map/ppermute | solution.py:28
  87.6 0.7 copy.57.out_ref_index
  88.4 0.1 copy.44
  88.5 0.7 slice.213
  89.2 0.1 copy.45
  89.3 0.7 slice.214
  90.0 0.1 copy.46
  90.1 0.8 slice.201
  90.9 1.9 %collective-permute-start.9 = (bf16[1160,256]{1,0:T(8,128)(2,1)}, bf16[1160,256]{1,0:T(8,128)(2,1)S(1)}, u32[]{:S(2)}, u32[]{:S(2)}) collective-permute-start(bf16[1160,256]{1,0:T(8,128)(2,1)} %collective-permute-done.7.refs_4_), channel_id=1, source_target_pairs={{0,1},{1,2},{2,3},{3,4},{4,5},{5,6},{6,7},{7,0},{8,9},{9,10},{10,1... | collective-permute-start | bytes 1781768 | tf_op jit(solution)/shard_map/ppermute | solution.py:28
  92.8 5.9 %collective-permute-done.10.refs_7_ = bf16[1160,256]{1,0:T(8,128)(2,1)} collective-permute-done((bf16[1160,256]{1,0:T(8,128)(2,1)}, bf16[1160,256]{1,0:T(8,128)(2,1)}, u32[]{:S(2)}, u32[]{:S(2)}) %collective-permute-start.10) | collective-permute-done | bytes 593952 | tf_op jit(solution)/shard_map/ppermute | solution.py:28
  98.7 4.5 %collective-permute-start.11 = (bf16[1160,256]{1,0:T(8,128)(2,1)}, bf16[1160,256]{1,0:T(8,128)(2,1)}, u32[]{:S(2)}, u32[]{:S(2)}) collective-permute-start(bf16[1160,256]{1,0:T(8,128)(2,1)} %collective-permute-done.10.refs_7_), channel_id=1, source_target_pairs={{0,7},{1,0},{2,1},{3,2},{4,3},{5,4},{6,5},{7,6},{8,15},{9,8},{10,9... | collective-permute-start | bytes 1781768 | tf_op jit(solution)/shard_map/ppermute | solution.py:28
  103.3 0.7 slice.218
  104.0 0.1 copy.47
  104.1 0.6 slice.219
  104.8 0.1 copy.48
  104.9 1.3 collective-permute-done.13.refs_10_
  106.3 0.7 pad_maximum_fusion.8.in_ref
  107.0 1.3 shard_map.46
  108.3 0.8 fusion.4
  109.2 0.1 copy.49
  109.3 0.7 slice.221
  110.0 0.1 copy.50
  110.1 2.5 %collective-permute-done.11.refs_8_ = bf16[1160,256]{1,0:T(8,128)(2,1)} collective-permute-done((bf16[1160,256]{1,0:T(8,128)(2,1)}, bf16[1160,256]{1,0:T(8,128)(2,1)}, u32[]{:S(2)}, u32[]{:S(2)}) %collective-permute-start.11) | collective-permute-done | bytes 593952 | tf_op jit(solution)/shard_map/ppermute | solution.py:28
  112.6 0.7 slice.222
  113.3 0.1 copy.51
  113.4 0.1 concatenate.48
  113.6 0.3 slice_reduce_fusion.5
  113.9 0.1 copy.52
  114.2 0.9 slice.231
  115.2 0.2 slice_reduce_fusion.1
  115.5 0.2 select_reduce_fusion
  115.8 0.6 reshape.216.pos_ref
  116.4 3.1 %shard_map.47 = (f32[4,256,256]{2,1,0:T(8,128)S(1)}, f32[16,2,256]{2,1,0:T(2,128)}) custom-call(s32[128]{0:T(128)} %reshape.216.pos_ref, s32[4,2]{1,0:T(4,128)} %copy.57.out_ref_index, s32[8]{0:T(128)} %and_select_fusion.1.source_ref, bf16[4160,256]{1,0:T(8,128)(2,1)} %all-gather.6.cloned.1.call-done.refs_0_, bf16[1160,256]{1,0:T(8,128)(2,1)} %copy-done, ...), custom_call_target="tpu_custom_call" | custom-call | tf_op jit(solution)/shard_map/pallas_call | solution.py:211
  119.5 18.0 %all-to-all-start = ((f32[16,2,256]{2,1,0:T(2,128)}), f32[16,2,256]{2,1,0:T(2,128)S(1)}, u32[]{:S(2)}, u32[]{:S(2)}) async-start(f32[16,2,256]{2,1,0:T(2,128)} %get-tuple-element.20), calls=%async_computation | async-start | bytes 65536 | tf_op jit(solution)/shard_map/all_to_all | solution.py:231
  137.4 5.8 %all-to-all-done = f32[16,2,256]{2,1,0:T(2,128)S(1)} async-done(((f32[16,2,256]{2,1,0:T(2,128)}), f32[16,2,256]{2,1,0:T(2,128)S(1)}, u32[]{:S(2)}, u32[]{:S(2)}) %all-to-all-start) | async-done | bytes 32800 | tf_op jit(solution)/shard_map/all_to_all | solution.py:231
  143.3 1.1 divide_bitcast_fusion
  (68 shorter events, 1.4 us)
Async XLA Ops:
  6.5 50.6 %all-gather.6.cloned.1.call-start = ((), (), s32[]{:S(2)}) async-start(), calls=%async_computation.2 | async-start | bytes 2396160 | tf_op jit(solution)/shard_map/all_gather | solution.py:145
  9.1 105.2 %all-gather.4.cloned.1.call-start = ((), (), s32[]{:S(2)}) async-start(), calls=%async_computation.1 | async-start | bytes 4792320 | tf_op jit(solution)/shard_map/all_gather | solution.py:155
  9.1 34.8 %collective-permute-start = (bf16[520,256]{1,0:T(8,128)(2,1)}, bf16[520,256]{1,0:T(8,128)(2,1)S(1)}, u32[]{:S(2)}, u32[]{:S(2)}) collective-permute-start(bf16[520,256]{1,0:T(8,128)(2,1)} %pad_maximum_fusion.3), channel_id=1, source_target_pairs={{0,256},{256,0},{1,257},{257,1},{2,258},{258,2},{3,259},{259,3},{4... | collective-permute-start | bytes 798728 | tf_op jit(solution)/shard_map/ppermute | solution.py:28
  14.7 28.9 %collective-permute-start.1 = (bf16[328,256]{1,0:T(8,128)(2,1)S(1)}, bf16[328,256]{1,0:T(8,128)(2,1)S(1)}, u32[]{:S(2)}, u32[]{:S(2)}) collective-permute-start(bf16[328,256]{1,0:T(8,128)(2,1)S(1)} %get-tuple-element.40), channel_id=1, source_target_pairs={{0,8},{8,16},{16,24},{24,0},{1,9},{9,17},{17,25},{25,1},{2,10},{10... | collective-permute-start | bytes 503816 | tf_op jit(solution)/shard_map/ppermute | solution.py:28
  20.6 23.1 %collective-permute-start.2 = (bf16[328,256]{1,0:T(8,128)(2,1)S(1)}, bf16[328,256]{1,0:T(8,128)(2,1)S(1)}, u32[]{:S(2)}, u32[]{:S(2)}) collective-permute-start(bf16[328,256]{1,0:T(8,128)(2,1)S(1)} %get-tuple-element.39), channel_id=1, source_target_pairs={{0,24},{8,0},{16,8},{24,16},{1,25},{9,1},{17,9},{25,17},{2,26},{10... | collective-permute-start | bytes 503816 | tf_op jit(solution)/shard_map/ppermute | solution.py:28
  26.5 12.8 %collective-permute-start.3 = (bf16[264,256]{1,0:T(8,128)(2,1)S(1)}, bf16[264,256]{1,0:T(8,128)(2,1)S(1)}, u32[]{:S(2)}, u32[]{:S(2)}) collective-permute-start(bf16[264,256]{1,0:T(8,128)(2,1)S(1)} %get-tuple-element.38), channel_id=1, source_target_pairs={{0,16},{8,24},{16,0},{24,8},{1,17},{9,25},{17,1},{25,9},{2,18},{10... | collective-permute-start | bytes 405512 | tf_op jit(solution)/shard_map/ppermute | solution.py:28
  31.9 11.7 %collective-permute-start.4 = (bf16[264,256]{1,0:T(8,128)(2,1)S(1)}, bf16[264,256]{1,0:T(8,128)(2,1)S(1)}, u32[]{:S(2)}, u32[]{:S(2)}) collective-permute-start(bf16[264,256]{1,0:T(8,128)(2,1)S(1)} %get-tuple-element.37), channel_id=1, source_target_pairs={{0,16},{8,24},{16,0},{24,8},{1,17},{9,25},{17,1},{25,9},{2,18},{10... | collective-permute-start | bytes 405512 | tf_op jit(solution)/shard_map/ppermute | solution.py:28
  43.9 44.5 %copy-start = (bf16[1160,256]{1,0:T(8,128)(2,1)}, bf16[1160,256]{1,0:T(8,128)(2,1)S(1)}, u32[]{:S(2)}) copy-start(bf16[1160,256]{1,0:T(8,128)(2,1)S(1)} %concatenate.45.refs_1_) | copy-start | bytes 1781764
  44.9 22.6 %collective-permute-start.5 = (bf16[1160,256]{1,0:T(8,128)(2,1)S(1)}, bf16[1160,256]{1,0:T(8,128)(2,1)}, u32[]{:S(2)}, u32[]{:S(2)}) collective-permute-start(bf16[1160,256]{1,0:T(8,128)(2,1)S(1)} %concatenate.45.refs_1_), channel_id=1, source_target_pairs={{0,1},{1,2},{2,3},{3,4},{4,5},{5,6},{6,7},{7,0},{8,9},{9,10},{10,1... | collective-permute-start | bytes 1781768 | tf_op jit(solution)/shard_map/ppermute | solution.py:28
  48.1 19.8 %collective-permute-start.6 = (bf16[1160,256]{1,0:T(8,128)(2,1)S(1)}, bf16[1160,256]{1,0:T(8,128)(2,1)}, u32[]{:S(2)}, u32[]{:S(2)}) collective-permute-start(bf16[1160,256]{1,0:T(8,128)(2,1)S(1)} %concatenate.45.refs_1_), channel_id=1, source_target_pairs={{0,7},{1,0},{2,1},{3,2},{4,3},{5,4},{6,5},{7,6},{8,15},{9,8},{10,9... | collective-permute-start | bytes 1781768 | tf_op jit(solution)/shard_map/ppermute | solution.py:28
  59.4 11.7 %copy-start.5 = (s32[8]{0:T(128)S(1)}, s32[8]{0:T(128)}, u32[]{:S(2)}) copy-start(s32[8]{0:T(128)} %constant.68.clone) | copy-start | bytes 100
  59.4 28.2 %copy-start.4 = (s32[1,4,2]{1,2,0:T(2,128)S(1)}, s32[1,4,2]{1,2,0:T(2,128)}, u32[]{:S(2)}) copy-start(s32[1,4,2]{1,2,0:T(2,128)} %param.6) | copy-start | bytes 100
  67.9 15.8 %collective-permute-start.8 = (bf16[1160,256]{1,0:T(8,128)(2,1)}, bf16[1160,256]{1,0:T(8,128)(2,1)}, u32[]{:S(2)}, u32[]{:S(2)}) collective-permute-start(bf16[1160,256]{1,0:T(8,128)(2,1)} %collective-permute-done.6.refs_3_), channel_id=1, source_target_pairs={{0,7},{1,0},{2,1},{3,2},{4,3},{5,4},{6,5},{7,6},{8,15},{9,8},{10,9... | collective-permute-start | bytes 1781768 | tf_op jit(solution)/shard_map/ppermute | solution.py:28
  71.6 19.2 %collective-permute-start.7 = (bf16[1160,256]{1,0:T(8,128)(2,1)}, bf16[1160,256]{1,0:T(8,128)(2,1)}, u32[]{:S(2)}, u32[]{:S(2)}) collective-permute-start(bf16[1160,256]{1,0:T(8,128)(2,1)} %collective-permute-done.5.refs_2_), channel_id=1, source_target_pairs={{0,1},{1,2},{2,3},{3,4},{4,5},{5,6},{6,7},{7,0},{8,9},{9,10},{10,1... | collective-permute-start | bytes 1781768 | tf_op jit(solution)/shard_map/ppermute | solution.py:28
  73.8 32.5 %collective-permute-start.13 = (bf16[8,200,256]{2,1,0:T(8,128)(2,1)}, bf16[8,200,256]{2,1,0:T(8,128)(2,1)S(1)}, u32[]{:S(2)}, u32[]{:S(2)}) collective-permute-start(bf16[8,200,256]{2,1,0:T(8,128)(2,1)} %get-tuple-element.17), channel_id=1, source_target_pairs={{0,24},{8,0},{16,8},{24,16},{1,25},{9,1},{17,9},{25,17},{2,26},{10... | collective-permute-start | bytes 2457608 | tf_op jit(solution)/shard_map/ppermute | solution.py:28
  79.7 26.6 %collective-permute-start.12 = (bf16[8,200,256]{2,1,0:T(8,128)(2,1)S(1)}, bf16[8,200,256]{2,1,0:T(8,128)(2,1)S(1)}, u32[]{:S(2)}, u32[]{:S(2)}) collective-permute-start(bf16[8,200,256]{2,1,0:T(8,128)(2,1)S(1)} %get-tuple-element.16), channel_id=1, source_target_pairs={{0,8},{8,16},{16,24},{24,0},{1,9},{9,17},{17,25},{25,1},{2,10},{10... | collective-permute-start | bytes 2457608 | tf_op jit(solution)/shard_map/ppermute | solution.py:28
  83.8 14.9 %collective-permute-start.10 = (bf16[1160,256]{1,0:T(8,128)(2,1)}, bf16[1160,256]{1,0:T(8,128)(2,1)}, u32[]{:S(2)}, u32[]{:S(2)}) collective-permute-start(bf16[1160,256]{1,0:T(8,128)(2,1)} %collective-permute-done.8.refs_5_), channel_id=1, source_target_pairs={{0,7},{1,0},{2,1},{3,2},{4,3},{5,4},{6,5},{7,6},{8,15},{9,8},{10,9... | collective-permute-start | bytes 1781768 | tf_op jit(solution)/shard_map/ppermute | solution.py:28
  90.9 18.4 %collective-permute-start.9 = (bf16[1160,256]{1,0:T(8,128)(2,1)}, bf16[1160,256]{1,0:T(8,128)(2,1)S(1)}, u32[]{:S(2)}, u32[]{:S(2)}) collective-permute-start(bf16[1160,256]{1,0:T(8,128)(2,1)} %collective-permute-done.7.refs_4_), channel_id=1, source_target_pairs={{0,1},{1,2},{2,3},{3,4},{4,5},{5,6},{6,7},{7,0},{8,9},{9,10},{10,1... | collective-permute-start | bytes 1781768 | tf_op jit(solution)/shard_map/ppermute | solution.py:28
  98.7 14.0 %collective-permute-start.11 = (bf16[1160,256]{1,0:T(8,128)(2,1)}, bf16[1160,256]{1,0:T(8,128)(2,1)}, u32[]{:S(2)}, u32[]{:S(2)}) collective-permute-start(bf16[1160,256]{1,0:T(8,128)(2,1)} %collective-permute-done.10.refs_7_), channel_id=1, source_target_pairs={{0,7},{1,0},{2,1},{3,2},{4,3},{5,4},{6,5},{7,6},{8,15},{9,8},{10,9... | collective-permute-start | bytes 1781768 | tf_op jit(solution)/shard_map/ppermute | solution.py:28
  106.2 2.1 %copy-start.1 = (bf16[8,200,256]{2,1,0:T(8,128)(2,1)}, bf16[8,200,256]{2,1,0:T(8,128)(2,1)S(1)}, u32[]{:S(2)}) copy-start(bf16[8,200,256]{2,1,0:T(8,128)(2,1)S(1)} %collective-permute-done.13.refs_10_) | copy-start | bytes 2457604
  106.3 2.0 %copy-start.2 = (bf16[8,200,256]{2,1,0:T(8,128)(2,1)}, bf16[8,200,256]{2,1,0:T(8,128)(2,1)S(1)}, u32[]{:S(2)}) copy-start(bf16[8,200,256]{2,1,0:T(8,128)(2,1)S(1)} %collective-permute-done.12.refs_9_) | copy-start | bytes 2457604
  109.2 7.1 %copy-start.3 = (bf16[1160,256]{1,0:T(8,128)(2,1)}, bf16[1160,256]{1,0:T(8,128)(2,1)S(1)}, u32[]{:S(2)}) copy-start(bf16[1160,256]{1,0:T(8,128)(2,1)S(1)} %collective-permute-done.9.refs_6_) | copy-start | bytes 1781764
  119.5 23.8 %all-to-all-start = ((f32[16,2,256]{2,1,0:T(2,128)}), f32[16,2,256]{2,1,0:T(2,128)S(1)}, u32[]{:S(2)}, u32[]{:S(2)}) async-start(f32[16,2,256]{2,1,0:T(2,128)} %get-tuple-element.20), calls=%async_computation | async-start | bytes 65536 | tf_op jit(solution)/shard_map/all_to_all | solution.py:231
Sparse Core Ops, SparseCore 0:
  9.4 47.6 all-gather.5
  59.2 42.7 all-gather.3

commit v7 on v6

--- a/solution.py
+++ b/solution.py
@@ -40,16 +40,11 @@
     own, ring, (late_up, late_down) = refs[0], refs[1 : 1 + N_Y], refs[1 + N_Y : 3 + N_Y]
     right, exp_ref, part_ref, todo, lbuf, rbuf, sem = refs[3 + N_Y :]
 
-    exp_ref[...] = jnp.zeros_like(exp_ref)
-
     def note(i, n):
         code = pos_ref[i]
 
-        @pl.when(code >= 0)
-        def _():
-            todo[0, n] = code
-            todo[1, n] = i
-
+        todo[0, n] = code
+        todo[1, n] = i
         return n + (code >= 0).astype(jnp.int32)
 
     total = lax.fori_loop(0, pos_ref.shape[0], note, jnp.int32(0))
@@ -105,6 +100,7 @@
         return carry
 
     lax.fori_loop(0, jnp.minimum(total, BUFS), prime, 0)
+    exp_ref[...] = jnp.zeros_like(exp_ref)
 
     def multiply(n, carry):
         slot = n % BUFS

time: 154 us -> 154 us (level)
  Pallas kernels: 4.38 us -> 6.56 us
    pallas_call x1, Pallas kernels: 3.08 us -> 5.26 us  [shards(): pl.pallas_call(product_kernel, grid_spec=pltpu.PrefetchScalarGridSpec(num...]
where the time goes in v7:
time: 154 us; the launch traced here: 152 us
  starting transfers between devices  73.4 us (48%)
  waiting for transfers between devices  38.1 us (25%)
  local copies, waits for them, and re-layouts  14.2 us (9%)
  between operations  13.8 us (9%)
  Pallas kernels  6.56 us (4%)
  other arithmetic  6.46 us (4%)
    ppermute x14, starting transfers between devices, shift(): lax.ppermute(value, axis, [(i, (i + by) % size) for i in range(size)])  56.3 us
    ppermute x14, waiting for transfers between devices, shift(): lax.ppermute(value, axis, [(i, (i + by) % size) for i in range(size)])  27.1 us
    all_to_all x1, starting transfers between devices, shards(): lax.all_to_all(parts, ROW, split_axis=0, concat_axis=0)  17 us
    all_to_all x1, waiting for transfers between devices, shards(): lax.all_to_all(parts, ROW, split_axis=0, concat_axis=0)  5.79 us
    pallas_call x1, Pallas kernels, shards(): pl.pallas_call(product_kernel, grid_spec=pltpu.PrefetchScalarGridSpec(num...  5.26 us
    all_gather x1, waiting for transfers between devices, shards(): own = lax.all_gather(mine, 'y', axis=0, tiled=False)  5.18 us
    slice x16, local copies, waits for them, and re-layouts, signs_of(): return stack[..., :2 * SLOTS]  4.89 us
  transfers between devices with their start and end apart: 17, of which 10 were waited for; matrix products, arithmetic and copies ran while one was open for 10% of the time, Pallas kernels for 1%

profile of v7, /device:TPU:1, one launch (start us, length us, event | category | flops | bytes accessed | tf_op | source)
XLA Modules:
  0.0 152.5 jit_solution(9668920633758201631)
XLA Ops:
  6.5 1.0 slice_bitcast_fusion.1
  7.5 0.7 convert_element_type.25
  8.2 0.1 convert_element_type.26
  8.3 0.7 pad_maximum_fusion.3
  9.1 4.8 %collective-permute-start = (bf16[520,256]{1,0:T(8,128)(2,1)}, bf16[520,256]{1,0:T(8,128)(2,1)S(1)}, u32[]{:S(2)}, u32[]{:S(2)}) collective-permute-start(bf16[520,256]{1,0:T(8,128)(2,1)} %pad_maximum_fusion.3), channel_id=1, source_target_pairs={{0,256},{256,0},{1,257},{257,1},{2,258},{258,2},{3,259},{259,3},{4... | collective-permute-start | bytes 798728 | tf_op jit(solution)/shard_map/ppermute | solution.py:28
  13.9 0.8 slice_bitcast_fusion.2
  14.7 5.8 %collective-permute-start.1 = (bf16[328,256]{1,0:T(8,128)(2,1)S(1)}, bf16[328,256]{1,0:T(8,128)(2,1)S(1)}, u32[]{:S(2)}, u32[]{:S(2)}) collective-permute-start(bf16[328,256]{1,0:T(8,128)(2,1)S(1)} %get-tuple-element.40), channel_id=1, source_target_pairs={{0,8},{8,16},{16,24},{24,0},{1,9},{9,17},{17,25},{25,1},{2,10},{10... | collective-permute-start | bytes 503816 | tf_op jit(solution)/shard_map/ppermute | solution.py:28
  20.6 5.9 %collective-permute-start.2 = (bf16[328,256]{1,0:T(8,128)(2,1)S(1)}, bf16[328,256]{1,0:T(8,128)(2,1)S(1)}, u32[]{:S(2)}, u32[]{:S(2)}) collective-permute-start(bf16[328,256]{1,0:T(8,128)(2,1)S(1)} %get-tuple-element.39), channel_id=1, source_target_pairs={{0,24},{8,0},{16,8},{24,16},{1,25},{9,1},{17,9},{25,17},{2,26},{10... | collective-permute-start | bytes 503816 | tf_op jit(solution)/shard_map/ppermute | solution.py:28
  26.5 5.5 %collective-permute-start.3 = (bf16[264,256]{1,0:T(8,128)(2,1)S(1)}, bf16[264,256]{1,0:T(8,128)(2,1)S(1)}, u32[]{:S(2)}, u32[]{:S(2)}) collective-permute-start(bf16[264,256]{1,0:T(8,128)(2,1)S(1)} %get-tuple-element.38), channel_id=1, source_target_pairs={{0,16},{8,24},{16,0},{24,8},{1,17},{9,25},{17,1},{25,9},{2,18},{10... | collective-permute-start | bytes 405512 | tf_op jit(solution)/shard_map/ppermute | solution.py:28
  31.9 3.7 %collective-permute-start.4 = (bf16[264,256]{1,0:T(8,128)(2,1)S(1)}, bf16[264,256]{1,0:T(8,128)(2,1)S(1)}, u32[]{:S(2)}, u32[]{:S(2)}) collective-permute-start(bf16[264,256]{1,0:T(8,128)(2,1)S(1)} %get-tuple-element.37), channel_id=1, source_target_pairs={{0,16},{8,24},{16,0},{24,8},{1,17},{9,25},{17,1},{25,9},{2,18},{10... | collective-permute-start | bytes 405512 | tf_op jit(solution)/shard_map/ppermute | solution.py:28
  35.7 3.6 %collective-permute-done.3 = bf16[264,256]{1,0:T(8,128)(2,1)S(1)} collective-permute-done((bf16[264,256]{1,0:T(8,128)(2,1)S(1)}, bf16[264,256]{1,0:T(8,128)(2,1)S(1)}, u32[]{:S(2)}, u32[]{:S(2)}) %collective-permute-start.3) | collective-permute-done | bytes 135200 | tf_op jit(solution)/shard_map/ppermute | solution.py:28
  39.3 4.3 %collective-permute-done.4 = bf16[264,256]{1,0:T(8,128)(2,1)S(1)} collective-permute-done((bf16[264,256]{1,0:T(8,128)(2,1)S(1)}, bf16[264,256]{1,0:T(8,128)(2,1)S(1)}, u32[]{:S(2)}, u32[]{:S(2)}) %collective-permute-start.4) | collective-permute-done | bytes 135200 | tf_op jit(solution)/shard_map/ppermute | solution.py:28
  43.7 0.2 concatenate.45.refs_1_
  43.9 0.9 pad_maximum_fusion.2
  44.9 3.2 %collective-permute-start.5 = (bf16[1160,256]{1,0:T(8,128)(2,1)S(1)}, bf16[1160,256]{1,0:T(8,128)(2,1)}, u32[]{:S(2)}, u32[]{:S(2)}) collective-permute-start(bf16[1160,256]{1,0:T(8,128)(2,1)S(1)} %concatenate.45.refs_1_), channel_id=1, source_target_pairs={{0,1},{1,2},{2,3},{3,4},{4,5},{5,6},{6,7},{7,0},{8,9},{9,10},{10,1... | collective-permute-start | bytes 1781768 | tf_op jit(solution)/shard_map/ppermute | solution.py:28
  48.1 3.8 %collective-permute-start.6 = (bf16[1160,256]{1,0:T(8,128)(2,1)S(1)}, bf16[1160,256]{1,0:T(8,128)(2,1)}, u32[]{:S(2)}, u32[]{:S(2)}) collective-permute-start(bf16[1160,256]{1,0:T(8,128)(2,1)S(1)} %concatenate.45.refs_1_), channel_id=1, source_target_pairs={{0,7},{1,0},{2,1},{3,2},{4,3},{5,4},{6,5},{7,6},{8,15},{9,8},{10,9... | collective-permute-start | bytes 1781768 | tf_op jit(solution)/shard_map/ppermute | solution.py:28
  51.9 5.2 %all-gather.6.cloned.1.call-done.refs_0_ = bf16[4160,256]{1,0:T(8,128)(2,1)} async-done(((bf16[520,256]{1,0:T(8,128)(2,1)}), bf16[4160,256]{1,0:T(8,128)(2,1)}) %all-gather.6.cloned.1.call-update) | async-done | bytes 2129936 | tf_op jit(solution)/shard_map/all_gather | solution.py:141
  57.1 0.8 slice.216
  57.9 1.5 fusion.3
  59.4 1.0 pad_maximum_fusion
  60.4 7.0 %collective-permute-done.5.refs_2_ = bf16[1160,256]{1,0:T(8,128)(2,1)} collective-permute-done((bf16[1160,256]{1,0:T(8,128)(2,1)S(1)}, bf16[1160,256]{1,0:T(8,128)(2,1)}, u32[]{:S(2)}, u32[]{:S(2)}) %collective-permute-start.5) | collective-permute-done | bytes 593952 | tf_op jit(solution)/shard_map/ppermute | solution.py:28
  67.4 0.5 collective-permute-done.6.refs_3_
  67.9 3.1 %collective-permute-start.8 = (bf16[1160,256]{1,0:T(8,128)(2,1)}, bf16[1160,256]{1,0:T(8,128)(2,1)}, u32[]{:S(2)}, u32[]{:S(2)}) collective-permute-start(bf16[1160,256]{1,0:T(8,128)(2,1)} %collective-permute-done.6.refs_3_), channel_id=1, source_target_pairs={{0,7},{1,0},{2,1},{3,2},{4,3},{5,4},{6,5},{7,6},{8,15},{9,8},{10,9... | collective-permute-start | bytes 1781768 | tf_op jit(solution)/shard_map/ppermute | solution.py:28
  71.1 0.5 and_select_fusion.1.source_ref
  71.6 2.2 %collective-permute-start.7 = (bf16[1160,256]{1,0:T(8,128)(2,1)}, bf16[1160,256]{1,0:T(8,128)(2,1)}, u32[]{:S(2)}, u32[]{:S(2)}) collective-permute-start(bf16[1160,256]{1,0:T(8,128)(2,1)} %collective-permute-done.5.refs_2_), channel_id=1, source_target_pairs={{0,1},{1,2},{2,3},{3,4},{4,5},{5,6},{6,7},{7,0},{8,9},{9,10},{10,1... | collective-permute-start | bytes 1781768 | tf_op jit(solution)/shard_map/ppermute | solution.py:28
  73.8 5.9 %collective-permute-start.13 = (bf16[8,200,256]{2,1,0:T(8,128)(2,1)}, bf16[8,200,256]{2,1,0:T(8,128)(2,1)S(1)}, u32[]{:S(2)}, u32[]{:S(2)}) collective-permute-start(bf16[8,200,256]{2,1,0:T(8,128)(2,1)} %get-tuple-element.17), channel_id=1, source_target_pairs={{0,24},{8,0},{16,8},{24,16},{1,25},{9,1},{17,9},{25,17},{2,26},{10... | collective-permute-start | bytes 2457608 | tf_op jit(solution)/shard_map/ppermute | solution.py:28
  79.7 2.2 %collective-permute-start.12 = (bf16[8,200,256]{2,1,0:T(8,128)(2,1)S(1)}, bf16[8,200,256]{2,1,0:T(8,128)(2,1)S(1)}, u32[]{:S(2)}, u32[]{:S(2)}) collective-permute-start(bf16[8,200,256]{2,1,0:T(8,128)(2,1)S(1)} %get-tuple-element.16), channel_id=1, source_target_pairs={{0,8},{8,16},{16,24},{24,0},{1,9},{9,17},{17,25},{25,1},{2,10},{10... | collective-permute-start | bytes 2457608 | tf_op jit(solution)/shard_map/ppermute | solution.py:28
  81.8 1.9 %collective-permute-done.8.refs_5_ = bf16[1160,256]{1,0:T(8,128)(2,1)} collective-permute-done((bf16[1160,256]{1,0:T(8,128)(2,1)}, bf16[1160,256]{1,0:T(8,128)(2,1)}, u32[]{:S(2)}, u32[]{:S(2)}) %collective-permute-start.8) | collective-permute-done | bytes 593952 | tf_op jit(solution)/shard_map/ppermute | solution.py:28
  83.8 3.8 %collective-permute-start.10 = (bf16[1160,256]{1,0:T(8,128)(2,1)}, bf16[1160,256]{1,0:T(8,128)(2,1)}, u32[]{:S(2)}, u32[]{:S(2)}) collective-permute-start(bf16[1160,256]{1,0:T(8,128)(2,1)} %collective-permute-done.8.refs_5_), channel_id=1, source_target_pairs={{0,7},{1,0},{2,1},{3,2},{4,3},{5,4},{6,5},{7,6},{8,15},{9,8},{10,9... | collective-permute-start | bytes 1781768 | tf_op jit(solution)/shard_map/ppermute | solution.py:28
  87.6 0.7 copy.57.out_ref_index
  88.4 0.1 copy.44
  88.5 0.7 slice.213
  89.2 0.1 copy.45
  89.3 0.7 slice.214
  90.0 0.1 copy.46
  90.1 0.8 slice.201
  90.9 1.9 %collective-permute-start.9 = (bf16[1160,256]{1,0:T(8,128)(2,1)}, bf16[1160,256]{1,0:T(8,128)(2,1)S(1)}, u32[]{:S(2)}, u32[]{:S(2)}) collective-permute-start(bf16[1160,256]{1,0:T(8,128)(2,1)} %collective-permute-done.7.refs_4_), channel_id=1, source_target_pairs={{0,1},{1,2},{2,3},{3,4},{4,5},{5,6},{6,7},{7,0},{8,9},{9,10},{10,1... | collective-permute-start | bytes 1781768 | tf_op jit(solution)/shard_map/ppermute | solution.py:28
  92.8 5.9 %collective-permute-done.10.refs_7_ = bf16[1160,256]{1,0:T(8,128)(2,1)} collective-permute-done((bf16[1160,256]{1,0:T(8,128)(2,1)}, bf16[1160,256]{1,0:T(8,128)(2,1)}, u32[]{:S(2)}, u32[]{:S(2)}) %collective-permute-start.10) | collective-permute-done | bytes 593952 | tf_op jit(solution)/shard_map/ppermute | solution.py:28
  98.7 4.5 %collective-permute-start.11 = (bf16[1160,256]{1,0:T(8,128)(2,1)}, bf16[1160,256]{1,0:T(8,128)(2,1)}, u32[]{:S(2)}, u32[]{:S(2)}) collective-permute-start(bf16[1160,256]{1,0:T(8,128)(2,1)} %collective-permute-done.10.refs_7_), channel_id=1, source_target_pairs={{0,7},{1,0},{2,1},{3,2},{4,3},{5,4},{6,5},{7,6},{8,15},{9,8},{10,9... | collective-permute-start | bytes 1781768 | tf_op jit(solution)/shard_map/ppermute | solution.py:28
  103.3 0.7 slice.218
  104.0 0.1 copy.47
  104.1 0.6 slice.219
  104.8 0.1 copy.48
  104.9 1.3 collective-permute-done.13.refs_10_
  106.3 0.7 pad_maximum_fusion.8.in_ref
  107.0 1.3 shard_map.46
  108.3 0.8 fusion.4
  109.2 0.1 copy.49
  109.3 0.7 slice.221
  110.0 0.1 copy.50
  110.1 2.5 %collective-permute-done.11.refs_8_ = bf16[1160,256]{1,0:T(8,128)(2,1)} collective-permute-done((bf16[1160,256]{1,0:T(8,128)(2,1)}, bf16[1160,256]{1,0:T(8,128)(2,1)}, u32[]{:S(2)}, u32[]{:S(2)}) %collective-permute-start.11) | collective-permute-done | bytes 593952 | tf_op jit(solution)/shard_map/ppermute | solution.py:28
  112.6 0.7 slice.222
  113.3 0.1 copy.51
  113.4 0.1 concatenate.48
  113.6 0.3 slice_reduce_fusion.5
  113.9 0.1 copy.52
  114.2 0.9 slice.231
  115.2 0.2 slice_reduce_fusion.1
  115.5 0.2 select_reduce_fusion
  115.8 0.6 reshape.216.pos_ref
  116.4 5.3 %shard_map.47 = (f32[4,256,256]{2,1,0:T(8,128)S(1)}, f32[16,2,256]{2,1,0:T(2,128)}) custom-call(s32[128]{0:T(128)} %reshape.216.pos_ref, s32[4,2]{1,0:T(4,128)} %copy.57.out_ref_index, s32[8]{0:T(128)} %and_select_fusion.1.source_ref, bf16[4160,256]{1,0:T(8,128)(2,1)} %all-gather.6.cloned.1.call-done.refs_0_, bf16[1160,256]{1,0:T(8,128)(2,1)} %copy-done, ...), custom_call_target="tpu_custom_call" | custom-call | tf_op jit(solution)/shard_map/pallas_call | solution.py:207
  121.6 17.0 %all-to-all-start = ((f32[16,2,256]{2,1,0:T(2,128)}), f32[16,2,256]{2,1,0:T(2,128)S(1)}, u32[]{:S(2)}, u32[]{:S(2)}) async-start(f32[16,2,256]{2,1,0:T(2,128)} %get-tuple-element.20), calls=%async_computation | async-start | bytes 65536 | tf_op jit(solution)/shard_map/all_to_all | solution.py:227
  138.7 5.8 %all-to-all-done = f32[16,2,256]{2,1,0:T(2,128)S(1)} async-done(((f32[16,2,256]{2,1,0:T(2,128)}), f32[16,2,256]{2,1,0:T(2,128)S(1)}, u32[]{:S(2)}, u32[]{:S(2)}) %all-to-all-start) | async-done | bytes 32800 | tf_op jit(solution)/shard_map/all_to_all | solution.py:227
  144.6 1.1 divide_bitcast_fusion
  (68 shorter events, 1.4 us)
Async XLA Ops:
  6.5 50.6 %all-gather.6.cloned.1.call-start = ((), (), s32[]{:S(2)}) async-start(), calls=%async_computation.2 | async-start | bytes 2396160 | tf_op jit(solution)/shard_map/all_gather | solution.py:141
  9.1 105.2 %all-gather.4.cloned.1.call-start = ((), (), s32[]{:S(2)}) async-start(), calls=%async_computation.1 | async-start | bytes 4792320 | tf_op jit(solution)/shard_map/all_gather | solution.py:151
  9.1 34.8 %collective-permute-start = (bf16[520,256]{1,0:T(8,128)(2,1)}, bf16[520,256]{1,0:T(8,128)(2,1)S(1)}, u32[]{:S(2)}, u32[]{:S(2)}) collective-permute-start(bf16[520,256]{1,0:T(8,128)(2,1)} %pad_maximum_fusion.3), channel_id=1, source_target_pairs={{0,256},{256,0},{1,257},{257,1},{2,258},{258,2},{3,259},{259,3},{4... | collective-permute-start | bytes 798728 | tf_op jit(solution)/shard_map/ppermute | solution.py:28
  14.7 28.9 %collective-permute-start.1 = (bf16[328,256]{1,0:T(8,128)(2,1)S(1)}, bf16[328,256]{1,0:T(8,128)(2,1)S(1)}, u32[]{:S(2)}, u32[]{:S(2)}) collective-permute-start(bf16[328,256]{1,0:T(8,128)(2,1)S(1)} %get-tuple-element.40), channel_id=1, source_target_pairs={{0,8},{8,16},{16,24},{24,0},{1,9},{9,17},{17,25},{25,1},{2,10},{10... | collective-permute-start | bytes 503816 | tf_op jit(solution)/shard_map/ppermute | solution.py:28
  20.6 23.1 %collective-permute-start.2 = (bf16[328,256]{1,0:T(8,128)(2,1)S(1)}, bf16[328,256]{1,0:T(8,128)(2,1)S(1)}, u32[]{:S(2)}, u32[]{:S(2)}) collective-permute-start(bf16[328,256]{1,0:T(8,128)(2,1)S(1)} %get-tuple-element.39), channel_id=1, source_target_pairs={{0,24},{8,0},{16,8},{24,16},{1,25},{9,1},{17,9},{25,17},{2,26},{10... | collective-permute-start | bytes 503816 | tf_op jit(solution)/shard_map/ppermute | solution.py:28
  26.5 12.8 %collective-permute-start.3 = (bf16[264,256]{1,0:T(8,128)(2,1)S(1)}, bf16[264,256]{1,0:T(8,128)(2,1)S(1)}, u32[]{:S(2)}, u32[]{:S(2)}) collective-permute-start(bf16[264,256]{1,0:T(8,128)(2,1)S(1)} %get-tuple-element.38), channel_id=1, source_target_pairs={{0,16},{8,24},{16,0},{24,8},{1,17},{9,25},{17,1},{25,9},{2,18},{10... | collective-permute-start | bytes 405512 | tf_op jit(solution)/shard_map/ppermute | solution.py:28
  31.9 11.7 %collective-permute-start.4 = (bf16[264,256]{1,0:T(8,128)(2,1)S(1)}, bf16[264,256]{1,0:T(8,128)(2,1)S(1)}, u32[]{:S(2)}, u32[]{:S(2)}) collective-permute-start(bf16[264,256]{1,0:T(8,128)(2,1)S(1)} %get-tuple-element.37), channel_id=1, source_target_pairs={{0,16},{8,24},{16,0},{24,8},{1,17},{9,25},{17,1},{25,9},{2,18},{10... | collective-permute-start | bytes 405512 | tf_op jit(solution)/shard_map/ppermute | solution.py:28
  43.9 44.5 %copy-start = (bf16[1160,256]{1,0:T(8,128)(2,1)}, bf16[1160,256]{1,0:T(8,128)(2,1)S(1)}, u32[]{:S(2)}) copy-start(bf16[1160,256]{1,0:T(8,128)(2,1)S(1)} %concatenate.45.refs_1_) | copy-start | bytes 1781764
  44.9 22.6 %collective-permute-start.5 = (bf16[1160,256]{1,0:T(8,128)(2,1)S(1)}, bf16[1160,256]{1,0:T(8,128)(2,1)}, u32[]{:S(2)}, u32[]{:S(2)}) collective-permute-start(bf16[1160,256]{1,0:T(8,128)(2,1)S(1)} %concatenate.45.refs_1_), channel_id=1, source_target_pairs={{0,1},{1,2},{2,3},{3,4},{4,5},{5,6},{6,7},{7,0},{8,9},{9,10},{10,1... | collective-permute-start | bytes 1781768 | tf_op jit(solution)/shard_map/ppermute | solution.py:28
  48.1 19.8 %collective-permute-start.6 = (bf16[1160,256]{1,0:T(8,128)(2,1)S(1)}, bf16[1160,256]{1,0:T(8,128)(2,1)}, u32[]{:S(2)}, u32[]{:S(2)}) collective-permute-start(bf16[1160,256]{1,0:T(8,128)(2,1)S(1)} %concatenate.45.refs_1_), channel_id=1, source_target_pairs={{0,7},{1,0},{2,1},{3,2},{4,3},{5,4},{6,5},{7,6},{8,15},{9,8},{10,9... | collective-permute-start | bytes 1781768 | tf_op jit(solution)/shard_map/ppermute | solution.py:28
  59.4 11.7 %copy-start.5 = (s32[8]{0:T(128)S(1)}, s32[8]{0:T(128)}, u32[]{:S(2)}) copy-start(s32[8]{0:T(128)} %constant.68.clone) | copy-start | bytes 100
  59.4 28.2 %copy-start.4 = (s32[1,4,2]{1,2,0:T(2,128)S(1)}, s32[1,4,2]{1,2,0:T(2,128)}, u32[]{:S(2)}) copy-start(s32[1,4,2]{1,2,0:T(2,128)} %param.6) | copy-start | bytes 100
  67.9 15.8 %collective-permute-start.8 = (bf16[1160,256]{1,0:T(8,128)(2,1)}, bf16[1160,256]{1,0:T(8,128)(2,1)}, u32[]{:S(2)}, u32[]{:S(2)}) collective-permute-start(bf16[1160,256]{1,0:T(8,128)(2,1)} %collective-permute-done.6.refs_3_), channel_id=1, source_target_pairs={{0,7},{1,0},{2,1},{3,2},{4,3},{5,4},{6,5},{7,6},{8,15},{9,8},{10,9... | collective-permute-start | bytes 1781768 | tf_op jit(solution)/shard_map/ppermute | solution.py:28
  71.6 19.2 %collective-permute-start.7 = (bf16[1160,256]{1,0:T(8,128)(2,1)}, bf16[1160,256]{1,0:T(8,128)(2,1)}, u32[]{:S(2)}, u32[]{:S(2)}) collective-permute-start(bf16[1160,256]{1,0:T(8,128)(2,1)} %collective-permute-done.5.refs_2_), channel_id=1, source_target_pairs={{0,1},{1,2},{2,3},{3,4},{4,5},{5,6},{6,7},{7,0},{8,9},{9,10},{10,1... | collective-permute-start | bytes 1781768 | tf_op jit(solution)/shard_map/ppermute | solution.py:28
  73.8 32.5 %collective-permute-start.13 = (bf16[8,200,256]{2,1,0:T(8,128)(2,1)}, bf16[8,200,256]{2,1,0:T(8,128)(2,1)S(1)}, u32[]{:S(2)}, u32[]{:S(2)}) collective-permute-start(bf16[8,200,256]{2,1,0:T(8,128)(2,1)} %get-tuple-element.17), channel_id=1, source_target_pairs={{0,24},{8,0},{16,8},{24,16},{1,25},{9,1},{17,9},{25,17},{2,26},{10... | collective-permute-start | bytes 2457608 | tf_op jit(solution)/shard_map/ppermute | solution.py:28
  79.7 26.6 %collective-permute-start.12 = (bf16[8,200,256]{2,1,0:T(8,128)(2,1)S(1)}, bf16[8,200,256]{2,1,0:T(8,128)(2,1)S(1)}, u32[]{:S(2)}, u32[]{:S(2)}) collective-permute-start(bf16[8,200,256]{2,1,0:T(8,128)(2,1)S(1)} %get-tuple-element.16), channel_id=1, source_target_pairs={{0,8},{8,16},{16,24},{24,0},{1,9},{9,17},{17,25},{25,1},{2,10},{10... | collective-permute-start | bytes 2457608 | tf_op jit(solution)/shard_map/ppermute | solution.py:28
  83.8 14.9 %collective-permute-start.10 = (bf16[1160,256]{1,0:T(8,128)(2,1)}, bf16[1160,256]{1,0:T(8,128)(2,1)}, u32[]{:S(2)}, u32[]{:S(2)}) collective-permute-start(bf16[1160,256]{1,0:T(8,128)(2,1)} %collective-permute-done.8.refs_5_), channel_id=1, source_target_pairs={{0,7},{1,0},{2,1},{3,2},{4,3},{5,4},{6,5},{7,6},{8,15},{9,8},{10,9... | collective-permute-start | bytes 1781768 | tf_op jit(solution)/shard_map/ppermute | solution.py:28
  90.9 18.4 %collective-permute-start.9 = (bf16[1160,256]{1,0:T(8,128)(2,1)}, bf16[1160,256]{1,0:T(8,128)(2,1)S(1)}, u32[]{:S(2)}, u32[]{:S(2)}) collective-permute-start(bf16[1160,256]{1,0:T(8,128)(2,1)} %collective-permute-done.7.refs_4_), channel_id=1, source_target_pairs={{0,1},{1,2},{2,3},{3,4},{4,5},{5,6},{6,7},{7,0},{8,9},{9,10},{10,1... | collective-permute-start | bytes 1781768 | tf_op jit(solution)/shard_map/ppermute | solution.py:28
  98.7 14.0 %collective-permute-start.11 = (bf16[1160,256]{1,0:T(8,128)(2,1)}, bf16[1160,256]{1,0:T(8,128)(2,1)}, u32[]{:S(2)}, u32[]{:S(2)}) collective-permute-start(bf16[1160,256]{1,0:T(8,128)(2,1)} %collective-permute-done.10.refs_7_), channel_id=1, source_target_pairs={{0,7},{1,0},{2,1},{3,2},{4,3},{5,4},{6,5},{7,6},{8,15},{9,8},{10,9... | collective-permute-start | bytes 1781768 | tf_op jit(solution)/shard_map/ppermute | solution.py:28
  106.2 2.1 %copy-start.1 = (bf16[8,200,256]{2,1,0:T(8,128)(2,1)}, bf16[8,200,256]{2,1,0:T(8,128)(2,1)S(1)}, u32[]{:S(2)}) copy-start(bf16[8,200,256]{2,1,0:T(8,128)(2,1)S(1)} %collective-permute-done.13.refs_10_) | copy-start | bytes 2457604
  106.3 2.0 %copy-start.2 = (bf16[8,200,256]{2,1,0:T(8,128)(2,1)}, bf16[8,200,256]{2,1,0:T(8,128)(2,1)S(1)}, u32[]{:S(2)}) copy-start(bf16[8,200,256]{2,1,0:T(8,128)(2,1)S(1)} %collective-permute-done.12.refs_9_) | copy-start | bytes 2457604
  109.2 7.1 %copy-start.3 = (bf16[1160,256]{1,0:T(8,128)(2,1)}, bf16[1160,256]{1,0:T(8,128)(2,1)S(1)}, u32[]{:S(2)}) copy-start(bf16[1160,256]{1,0:T(8,128)(2,1)S(1)} %collective-permute-done.9.refs_6_) | copy-start | bytes 1781764
  121.6 22.8 %all-to-all-start = ((f32[16,2,256]{2,1,0:T(2,128)}), f32[16,2,256]{2,1,0:T(2,128)S(1)}, u32[]{:S(2)}, u32[]{:S(2)}) async-start(f32[16,2,256]{2,1,0:T(2,128)} %get-tuple-element.20), calls=%async_computation | async-start | bytes 65536 | tf_op jit(solution)/shard_map/all_to_all | solution.py:227
Sparse Core Ops, SparseCore 0:
  9.4 47.6 all-gather.5
  59.2 42.7 all-gather.3
